TPU v7x, 32 devices: a whole 2x2x4 slice. The times are simulated.
32 devices in a mesh: groups: 2 (over y), space: 8 (over z, x), tm: 2 (over core).
Axes of the slice: x: 2, y: 2, z: 4, core: 2. Of those that a mesh axis runs over, the one named last changes fastest.
Arguments:
- base_latent: bfloat16 [64, 2, 12, 128], P(('groups', 'space'), 'tm'), parts along dimension 0, may hold values from -6 to 6
- cotangent: bfloat16 [64, 8, 48, 128], P(('groups', 'space'), 'tm'), parts along dimension 0, may hold values from -6 to 6
- w_spatial: bfloat16 [3, 3, 128, 128], replicated, may hold values from -0.1875 to 0.1875
- w_temporal: bfloat16 [5, 128, 128], replicated, may hold values from -0.25 to 0.25
Outputs:
- result: bfloat16 [64, 8, 48, 128], P(('groups', 'space'), 'tm'), parts along dimension 0
- grad_base: float32 [64, 2, 12, 128], P(('groups', 'space'), 'tm'), parts along dimension 0
- grad_spatial: float32 [6, 3, 128, 128], P('groups'), parts along dimension 0
- grad_temporal: float32 [10, 128, 128], P('groups'), parts along dimension 0
There are 2 independent parts, one for each index of `groups`. A program takes and returns all parts, laid end to end along the dimension named above; an argument that names none is the same for every part. Nothing has to cross between parts.
All inputs are finite; a program needn't handle non-finite values.
Results may differ from a plain program's by a relative error of at most 0.0064.
Values may be sent and summed in bfloat16 or wider, within the bound.
No kernel may reach another device: no remote copies, remote signals or barrier semaphores. Data moves between devices by JAX's collectives and lax.ppermute only.
A program may use at most 64 MiB of HBM per device.

v0:
```python
import jax
import jax.numpy as jnp
from jax import lax
from jax.sharding import PartitionSpec as P

FRAME_DILATION = 2


def shifted(value, axis, by):
    count = lax.axis_size(axis)
    pairs = [(i, i + by) for i in range(count) if 0 <= i + by < count]
    return lax.ppermute(value, axis, pairs)


def extended(cells, sides, width):
    for axis, dim in sides:
        count = lax.axis_size(axis)
        ends = count - 1
        head = lax.slice_in_dim(cells, 0, width, axis=dim)
        tail = lax.slice_in_dim(cells, cells.shape[dim] - width, cells.shape[dim], axis=dim)
        cells = jnp.concatenate(
            [
                lax.ppermute(tail, axis, [(i, (i + 1) % count) for i in range(ends)]),
                cells,
                lax.ppermute(head, axis, [((i + 1) % count, i) for i in range(ends)]),
            ],
            axis=dim,
        )
    return cells


def widen_cols(field):
    left_cols = jnp.concatenate([field[:, :, :1], field[:, :, :-1]], axis=2)
    right_cols = jnp.concatenate([field[:, :, 1:], field[:, :, -1:]], axis=2)
    phases = jnp.stack(
        [
            0.375 * left_cols + 0.625 * field,
            0.125 * left_cols + 0.875 * field,
            0.875 * field + 0.125 * right_cols,
            0.625 * field + 0.375 * right_cols,
        ],
        axis=3,
    )
    return phases.reshape(field.shape[0], field.shape[1], field.shape[2] * 4, field.shape[3])


def widen_rows(below_rows, middle, above_rows):
    phases = jnp.stack(
        [
            0.375 * below_rows + 0.625 * middle,
            0.125 * below_rows + 0.875 * middle,
            0.875 * middle + 0.125 * above_rows,
            0.625 * middle + 0.375 * above_rows,
        ],
        axis=2,
    )
    return phases.reshape(middle.shape[0], middle.shape[1] * 4, middle.shape[2], middle.shape[3])


def silu_slope(value):
    sigmoid_val = jax.nn.sigmoid(value)
    return sigmoid_val * (1.0 + value * (1.0 - sigmoid_val))


def conv_three(padded, weight, row_count, col_count, start):
    frame_count = padded.shape[0]
    channels = weight.shape[3]
    summed = jnp.zeros((frame_count * row_count * col_count, channels), jnp.float32)
    for tap_row in range(3):
        for tap_col in range(3):
            r0 = start - tap_row if start else tap_row
            c0 = start - tap_col if start else tap_col
            frame_window = padded[:, r0 : r0 + row_count, c0 : c0 + col_count].reshape(
                -1, padded.shape[3]
            )
            kernel = weight[tap_row, tap_col] if not start else weight[tap_row, tap_col].T
            summed = summed + jnp.dot(frame_window, kernel, preferred_element_type=jnp.float32)
    return summed.reshape(frame_count, row_count, col_count, channels)


def space_grads(padded, delta, row_count, col_count):
    flat = delta.reshape(-1, delta.shape[3])
    taps = []
    for tap_row in range(3):
        for tap_col in range(3):
            frame_window = padded[
                :, tap_row : tap_row + row_count, tap_col : tap_col + col_count
            ].reshape(-1, padded.shape[3])
            taps.append(
                lax.dot_general(
                    frame_window, flat, (((0,), (0,)), ((), ())), preferred_element_type=jnp.float32
                )
            )
    return jnp.stack(taps).reshape(3, 3, padded.shape[3], delta.shape[3])


def conv_time(frames_extended, weight, frame_count, reversed_order):
    channels = weight.shape[2]
    tensor_shape = frames_extended.shape
    summed = jnp.zeros((frame_count * tensor_shape[1] * tensor_shape[2], channels), jnp.float32)
    for kernel_tap in range(5):
        frame_offset = (
            (4 - kernel_tap) * FRAME_DILATION if reversed_order else kernel_tap * FRAME_DILATION
        )
        frame_window = frames_extended[frame_offset : frame_offset + frame_count].reshape(
            -1, tensor_shape[3]
        )
        kernel = weight[kernel_tap].T if reversed_order else weight[kernel_tap]
        summed = summed + jnp.dot(frame_window, kernel, preferred_element_type=jnp.float32)
    return summed.reshape(frame_count, tensor_shape[1], tensor_shape[2], channels)


def time_grads(frames_extended, delta, frame_count):
    flat = delta.reshape(-1, delta.shape[3])
    taps = []
    for kernel_tap in range(5):
        frame_window = frames_extended[
            kernel_tap * FRAME_DILATION : kernel_tap * FRAME_DILATION + frame_count
        ].reshape(-1, frames_extended.shape[3])
        taps.append(
            lax.dot_general(
                frame_window, flat, (((0,), (0,)), ((), ())), preferred_element_type=jnp.float32
            )
        )
    return jnp.stack(taps)


def shrink_base(grad_image, row_rank, row_devices, latent_shape):
    frame_count, low_rows, low_cols, channels = latent_shape
    _, col_pull = jax.vjp(
        widen_cols, jnp.zeros((frame_count, grad_image.shape[1], low_cols, channels), jnp.float32)
    )
    narrow = col_pull(grad_image)[0].reshape(frame_count, low_rows, 4, low_cols, channels)
    to_lower = 0.375 * narrow[:, :, 0] + 0.125 * narrow[:, :, 1]
    to_middle = (
        0.625 * narrow[:, :, 0]
        + 0.875 * narrow[:, :, 1]
        + 0.875 * narrow[:, :, 2]
        + 0.625 * narrow[:, :, 3]
    )
    to_upper = 0.125 * narrow[:, :, 2] + 0.375 * narrow[:, :, 3]
    from_above = shifted(to_lower, "tm", -1)
    from_below = shifted(to_upper, "tm", 1)
    next_lower = jnp.concatenate([to_lower[:, 1:], from_above], axis=1)
    prev_upper = jnp.concatenate([from_below, to_upper[:, :-1]], axis=1)
    edge_low = jnp.where(row_rank == 0, to_lower, jnp.zeros_like(to_lower))
    edge_high = jnp.where(row_rank == row_devices - 1, to_upper, jnp.zeros_like(to_upper))
    empty_rows = jnp.zeros((frame_count, low_rows - 1, low_cols, channels), jnp.float32)
    summed = to_middle + next_lower + prev_upper
    return (
        summed
        + jnp.concatenate([edge_low, empty_rows], axis=1)
        + jnp.concatenate([empty_rows, edge_high], axis=1)
    )


def local(base_latent, cotangent, w_spatial, w_temporal):
    row_rank = lax.axis_index("tm")
    row_devices = lax.axis_size("tm")
    padded_base = extended(base_latent, (("tm", 1),), 1)
    low_first = jnp.where(row_rank == 0, base_latent, padded_base[:, :1])
    high_last = jnp.where(row_rank == row_devices - 1, base_latent, padded_base[:, -1:])
    latent32 = base_latent.astype(jnp.float32)
    below_rows = jnp.concatenate([low_first, base_latent[:, :-1]], axis=1).astype(jnp.float32)
    above_rows = jnp.concatenate([base_latent[:, 1:], high_last], axis=1).astype(jnp.float32)
    upsampled = widen_cols(widen_rows(below_rows, latent32, above_rows)).astype(jnp.bfloat16)
    frame_count, row_count, col_count = (upsampled.shape[0], upsampled.shape[1], upsampled.shape[2])
    image_ext = extended(upsampled, (("tm", 1),), 1)
    padded = jnp.pad(image_ext, ((0, 0), (0, 0), (1, 1), (0, 0)))
    pre_one = conv_three(padded, w_spatial, row_count, col_count, 0)
    first_activation = jax.nn.silu(pre_one).astype(jnp.bfloat16)
    frames_extended = extended(first_activation, (("space", 0),), 2 * FRAME_DILATION)
    pre_two = conv_time(frames_extended, w_temporal, frame_count, False)
    result = (upsampled.astype(jnp.float32) + jax.nn.silu(pre_two)).astype(jnp.bfloat16)
    upstream = cotangent.astype(jnp.float32)
    second_gradient = (upstream * silu_slope(pre_two)).astype(jnp.bfloat16)
    temporal_local = time_grads(frames_extended, second_gradient, frame_count)
    grad_temporal = lax.psum(temporal_local, ("space", "tm"))
    gradient_extended = extended(second_gradient, (("space", 0),), 2 * FRAME_DILATION)
    back_one = conv_time(gradient_extended, w_temporal, frame_count, True)
    delta_one = (back_one * silu_slope(pre_one)).astype(jnp.bfloat16)
    spatial_local = space_grads(padded, delta_one, row_count, col_count)
    delta_rows = extended(delta_one, (("tm", 1),), 1)
    delta_pad = jnp.pad(delta_rows, ((0, 0), (0, 0), (1, 1), (0, 0)))
    grad_image = upstream + conv_three(delta_pad, w_spatial, row_count, col_count, 2)
    grad_base = shrink_base(grad_image, row_rank, row_devices, base_latent.shape)
    grad_spatial = lax.psum(spatial_local, ("space", "tm"))
    return (result, grad_base, grad_spatial, grad_temporal)


def solution(mesh):
    in_specs = (
        P(("groups", "space"), "tm", None, None),
        P(("groups", "space"), "tm", None, None),
        P(),
        P(),
    )
    out_specs = (
        P(("groups", "space"), "tm", None, None),
        P(("groups", "space"), "tm", None, None),
        P("groups", None, None, None),
        P("groups", None, None),
    )
    return jax.shard_map(local, mesh=mesh, in_specs=in_specs, out_specs=out_specs, check_vma=False)
```

profile of v0, /device:TPU:0, one launch (start us, length us, event | category | flops | bytes accessed | tf_op | source)
XLA Modules:
  0.0 162.9 jit_solution(3683068652345166377)
XLA Ops:
  7.2 0.8 copy.55
  8.0 2.4 %collective-permute-start = (bf16[4,1,12,128]{3,1,2,0:T(2,128)(2,1)S(1)}, bf16[4,1,12,128]{3,1,2,0:T(2,128)(2,1)S(1)}, u32[]{:S(2)}, u32[]{:S(2)}) collective-permute-start(bf16[4,1,12,128]{3,1,2,0:T(2,128)(2,1)S(1)} %copy.55), channel_id=1, source_target_pairs={{0,1},{2,3},{4,5},{6,7},{8,9},{10,11},{12,13},{14,15},{16,17},{18,... | collective-permute-start | bytes 36872 | tf_op jit(solution)/shard_map/ppermute | solution.py:23
  10.4 1.3 collective-permute-start.1
  11.7 1.8 %collective-permute-done.1 = bf16[4,1,12,128]{3,1,2,0:T(2,128)(2,1)S(1)} collective-permute-done((bf16[4,1,12,128]{3,1,2,0:T(2,128)(2,1)S(1)}, bf16[4,1,12,128]{3,1,2,0:T(2,128)(2,1)S(1)}, u32[]{:S(2)}, u32[]{:S(2)}) %collective-permute-start.1) | collective-permute-done | bytes 12320 | tf_op jit(solution)/shard_map/ppermute | solution.py:25
  14.4 2.1 %collective-permute-start.2 = (bf16[4,1,48,128]{3,2,1,0:T(8,128)(2,1)S(1)}, bf16[4,1,48,128]{3,2,1,0:T(8,128)(2,1)S(1)}, u32[]{:S(2)}, u32[]{:S(2)}) collective-permute-start(bf16[4,1,48,128]{3,2,1,0:T(8,128)(2,1)S(1)} %get-tuple-element.34), channel_id=1, source_target_pairs={{0,1},{2,3},{4,5},{6,7},{8,9},{10,11},{12,13},{14,15},{16,17},{18,... | collective-permute-start | bytes 147464 | tf_op jit(solution)/shard_map/ppermute | solution.py:23
  16.5 1.3 collective-permute-start.3
  17.8 1.8 %collective-permute-done.3 = bf16[4,1,48,128]{3,2,1,0:T(8,128)(2,1)S(1)} collective-permute-done((bf16[4,1,48,128]{3,2,1,0:T(8,128)(2,1)S(1)}, bf16[4,1,48,128]{3,2,1,0:T(8,128)(2,1)S(1)}, u32[]{:S(2)}, u32[]{:S(2)}) %collective-permute-start.3) | collective-permute-done | bytes 49184 | tf_op jit(solution)/shard_map/ppermute | solution.py:25
  19.9 0.8 copy-done
  21.5 0.2 convolution_add_fusion.15
  22.3 0.2 fusion
  22.7 4.2 %collective-permute-start.4 = (bf16[4,4,48,128]{3,2,1,0:T(8,128)(2,1)S(1)}, bf16[4,4,48,128]{3,2,1,0:T(8,128)(2,1)S(1)}, u32[]{:S(2)}, u32[]{:S(2)}) collective-permute-start(bf16[4,4,48,128]{3,2,1,0:T(8,128)(2,1)S(1)} %multiply_convert_fusion.3), channel_id=1, source_target_pairs={{0,2},{2,4},{4,6},{6,8},{8,10},{10,12},{12,14},{1,3},{3,5},{5,7},{... | collective-permute-start | bytes 589832 | tf_op jit(solution)/shard_map/ppermute | solution.py:23
  26.9 1.3 collective-permute-start.5
  28.2 0.2 fusion.35
  28.4 3.0 %collective-permute-done.4 = bf16[4,4,48,128]{3,2,1,0:T(8,128)(2,1)S(1)} collective-permute-done((bf16[4,4,48,128]{3,2,1,0:T(8,128)(2,1)S(1)}, bf16[4,4,48,128]{3,2,1,0:T(8,128)(2,1)S(1)}, u32[]{:S(2)}, u32[]{:S(2)}) %collective-permute-start.4) | collective-permute-done | bytes 196640 | tf_op jit(solution)/shard_map/ppermute | solution.py:23
  31.4 4.0 %collective-permute-done.5 = bf16[4,4,48,128]{3,2,1,0:T(8,128)(2,1)S(1)} collective-permute-done((bf16[4,4,48,128]{3,2,1,0:T(8,128)(2,1)S(1)}, bf16[4,4,48,128]{3,2,1,0:T(8,128)(2,1)S(1)}, u32[]{:S(2)}, u32[]{:S(2)}) %collective-permute-start.5) | collective-permute-done | bytes 196640 | tf_op jit(solution)/shard_map/ppermute | solution.py:25
  35.9 0.2 fusion.1
  36.1 0.2 fusion.2
  36.3 0.7 copy-done.1
  37.0 0.9 fusion.21
  37.9 1.3 collective-permute-start.6
  39.2 5.1 %collective-permute-start.7 = (bf16[4,4,48,128]{3,2,1,0:T(8,128)(2,1)S(1)}, bf16[4,4,48,128]{3,2,1,0:T(8,128)(2,1)S(1)}, u32[]{:S(2)}, u32[]{:S(2)}) collective-permute-start(bf16[4,4,48,128]{3,2,1,0:T(8,128)(2,1)S(1)} %get-tuple-element.10), channel_id=1, source_target_pairs={{0,2},{2,4},{4,6},{6,8},{8,10},{10,12},{12,14},{1,3},{3,5},{5,7},{... | collective-permute-start | bytes 589832 | tf_op jit(solution)/shard_map/ppermute | solution.py:23
  44.4 0.2 fusion.12
  44.6 0.3 fusion.7
  44.9 0.3 fusion.11
  45.1 0.2 fusion.46
  45.3 0.3 fusion.6
  45.6 0.3 fusion.10
  45.9 0.6 collective-permute-done.6
  46.5 5.2 %collective-permute-done.7 = bf16[4,4,48,128]{3,2,1,0:T(8,128)(2,1)S(1)} collective-permute-done((bf16[4,4,48,128]{3,2,1,0:T(8,128)(2,1)S(1)}, bf16[4,4,48,128]{3,2,1,0:T(8,128)(2,1)S(1)}, u32[]{:S(2)}, u32[]{:S(2)}) %collective-permute-start.7) | collective-permute-done | bytes 196640 | tf_op jit(solution)/shard_map/ppermute | solution.py:23
  51.7 0.2 fusion.49
  51.9 0.2 fusion.40
  52.1 0.2 fusion.3
  52.4 0.3 multiply_convert_fusion
  52.8 0.2 fusion.19
  53.1 0.2 fusion.9
  53.3 0.3 fusion.18
  53.6 0.2 fusion.17
  53.9 0.2 fusion.16
  54.1 0.3 fusion.15
  54.4 0.2 fusion.14
  54.6 1.9 %collective-permute-start.8 = (bf16[4,1,48,128]{3,2,1,0:T(8,128)(2,1)S(1)}, bf16[4,1,48,128]{3,2,1,0:T(8,128)(2,1)S(1)}, u32[]{:S(2)}, u32[]{:S(2)}) collective-permute-start(bf16[4,1,48,128]{3,2,1,0:T(8,128)(2,1)S(1)} %get-tuple-element.26), channel_id=1, source_target_pairs={{0,1},{2,3},{4,5},{6,7},{8,9},{10,11},{12,13},{14,15},{16,17},{18,... | collective-permute-start | bytes 147464 | tf_op jit(solution)/shard_map/ppermute | solution.py:23
  56.6 1.3 collective-permute-start.9
  57.9 0.3 fusion.8
  58.1 0.3 fusion.13
  58.4 0.8 copy-done.2
  59.2 0.5 collective-permute-done.9
  60.0 0.2 fusion.73
  60.2 0.2 convolution_add_fusion.6
  60.4 0.2 convolution_add_fusion.5
  60.7 0.2 convolution_add_fusion.4
  60.9 0.2 convolution_add_fusion.3
  61.1 0.2 fusion.55
  61.3 0.2 convolution_add_fusion.2
  61.5 0.2 convolution_add_fusion.1
  61.7 0.2 fusion.5
  62.0 0.3 fusion.122
  62.5 0.6 copy-done.7
  63.3 1.3 collective-permute-start.10
  64.6 3.0 %collective-permute-start.11 = (f32[4,1,12,128]{3,1,2,0:T(1,128)S(1)}, f32[4,1,12,128]{3,1,2,0:T(1,128)S(1)}, u32[]{:S(2)}, u32[]{:S(2)}) collective-permute-start(f32[4,1,12,128]{3,1,2,0:T(1,128)S(1)} %get-tuple-element.40), channel_id=1, source_target_pairs={{0,1},{2,3},{4,5},{6,7},{8,9},{10,11},{12,13},{14,15},{16,17},{18,... | collective-permute-start | bytes 73736 | tf_op jit(solution)/shard_map/ppermute | solution.py:12
  67.7 0.8 collective-permute-done.11
  68.5 0.7 fusion.107
  69.2 84.1 %all-reduce.8.cloned.1.call-done = (f32[3,3,128,128]{3,2,1,0:T(8,128)}, f32[5,128,128]{2,1,0:T(8,128)}) async-done(((f32[3,3,128,128]{3,2,1,0:T(8,128)}, f32[5,128,128]{2,1,0:T(8,128)}), (f32[3,3,128,128]{3,2,1,0:T(8,128)}, f32[5,128,128]{2,1,0:T(8,128)})) %all-reduce.8.cloned.1.call-update) | async-done | bytes 917520 | tf_op jit(solution)/shard_map/psum | solution.py:187
  153.4 2.0 %copy.127 = f32[3,3,128,128]{3,2,1,0:T(8,128)} copy(f32[3,3,128,128]{3,2,1,0:T(8,128)} %get-tuple-element.58) | data formatting | bytes 1179648
  155.3 0.7 copy.128
  (54 shorter events, 4.1 us)
Async XLA Ops:
  7.2 146.2 %all-reduce.8.cloned.1.call-start = ((), (), s32[]{:S(2)}) async-start(), calls=%async_computation | async-start | bytes 1835008 | tf_op jit(solution)/shard_map/psum | solution.py:187
  7.2 6.3 %copy-start.6 = (bf16[4,1,12,128]{3,0,2,1:T(4,128)(2,1)S(1)}, bf16[4,1,12,128]{3,0,2,1:T(4,128)(2,1)}, u32[]{:S(2)}) copy-start(bf16[4,1,12,128]{3,0,2,1:T(4,128)(2,1)} %param.4) | copy-start | bytes 36868
  8.0 3.7 %collective-permute-start = (bf16[4,1,12,128]{3,1,2,0:T(2,128)(2,1)S(1)}, bf16[4,1,12,128]{3,1,2,0:T(2,128)(2,1)S(1)}, u32[]{:S(2)}, u32[]{:S(2)}) collective-permute-start(bf16[4,1,12,128]{3,1,2,0:T(2,128)(2,1)S(1)} %copy.55), channel_id=1, source_target_pairs={{0,1},{2,3},{4,5},{6,7},{8,9},{10,11},{12,13},{14,15},{16,17},{18,... | collective-permute-start | bytes 36872 | tf_op jit(solution)/shard_map/ppermute | solution.py:23
  10.4 3.1 %collective-permute-start.1 = (bf16[4,1,12,128]{3,1,2,0:T(2,128)(2,1)S(1)}, bf16[4,1,12,128]{3,1,2,0:T(2,128)(2,1)S(1)}, u32[]{:S(2)}, u32[]{:S(2)}) collective-permute-start(bf16[4,1,12,128]{3,1,2,0:T(2,128)(2,1)S(1)} %copy.55), channel_id=1, source_target_pairs={{1,0},{3,2},{5,4},{7,6},{9,8},{11,10},{13,12},{15,14},{17,16},{19,... | collective-permute-start | bytes 36872 | tf_op jit(solution)/shard_map/ppermute | solution.py:25
  14.4 3.4 %collective-permute-start.2 = (bf16[4,1,48,128]{3,2,1,0:T(8,128)(2,1)S(1)}, bf16[4,1,48,128]{3,2,1,0:T(8,128)(2,1)S(1)}, u32[]{:S(2)}, u32[]{:S(2)}) collective-permute-start(bf16[4,1,48,128]{3,2,1,0:T(8,128)(2,1)S(1)} %get-tuple-element.34), channel_id=1, source_target_pairs={{0,1},{2,3},{4,5},{6,7},{8,9},{10,11},{12,13},{14,15},{16,17},{18,... | collective-permute-start | bytes 147464 | tf_op jit(solution)/shard_map/ppermute | solution.py:23
  16.5 3.1 %collective-permute-start.3 = (bf16[4,1,48,128]{3,2,1,0:T(8,128)(2,1)S(1)}, bf16[4,1,48,128]{3,2,1,0:T(8,128)(2,1)S(1)}, u32[]{:S(2)}, u32[]{:S(2)}) collective-permute-start(bf16[4,1,48,128]{3,2,1,0:T(8,128)(2,1)S(1)} %get-tuple-element.35), channel_id=1, source_target_pairs={{1,0},{3,2},{5,4},{7,6},{9,8},{11,10},{13,12},{15,14},{17,16},{19,... | collective-permute-start | bytes 147464 | tf_op jit(solution)/shard_map/ppermute | solution.py:25
  19.7 1.0 copy-start
  22.5 5.7 %copy-start.3 = (bf16[5,128,128]{2,1,0:T(8,128)(2,1)S(1)}, bf16[5,128,128]{2,1,0:T(8,128)(2,1)}, u32[]{:S(2)}) copy-start(bf16[5,128,128]{2,1,0:T(8,128)(2,1)} %param.7) | copy-start | bytes 491524
  22.7 8.8 %collective-permute-start.4 = (bf16[4,4,48,128]{3,2,1,0:T(8,128)(2,1)S(1)}, bf16[4,4,48,128]{3,2,1,0:T(8,128)(2,1)S(1)}, u32[]{:S(2)}, u32[]{:S(2)}) collective-permute-start(bf16[4,4,48,128]{3,2,1,0:T(8,128)(2,1)S(1)} %multiply_convert_fusion.3), channel_id=1, source_target_pairs={{0,2},{2,4},{4,6},{6,8},{8,10},{10,12},{12,14},{1,3},{3,5},{5,7},{... | collective-permute-start | bytes 589832 | tf_op jit(solution)/shard_map/ppermute | solution.py:23
  26.9 8.6 %collective-permute-start.5 = (bf16[4,4,48,128]{3,2,1,0:T(8,128)(2,1)S(1)}, bf16[4,4,48,128]{3,2,1,0:T(8,128)(2,1)S(1)}, u32[]{:S(2)}, u32[]{:S(2)}) collective-permute-start(bf16[4,4,48,128]{3,2,1,0:T(8,128)(2,1)S(1)} %multiply_convert_fusion.3), channel_id=1, source_target_pairs={{2,0},{4,2},{6,4},{8,6},{10,8},{12,10},{14,12},{3,1},{5,3},{7,5},{... | collective-permute-start | bytes 589832 | tf_op jit(solution)/shard_map/ppermute | solution.py:25
  36.1 0.9 copy-start.1
  37.9 8.5 %collective-permute-start.6 = (bf16[4,4,48,128]{3,2,1,0:T(8,128)(2,1)S(1)}, bf16[4,4,48,128]{3,2,1,0:T(8,128)(2,1)S(1)}, u32[]{:S(2)}, u32[]{:S(2)}) collective-permute-start(bf16[4,4,48,128]{3,2,1,0:T(8,128)(2,1)S(1)} %get-tuple-element.10), channel_id=1, source_target_pairs={{2,0},{4,2},{6,4},{8,6},{10,8},{12,10},{14,12},{3,1},{5,3},{7,5},{... | collective-permute-start | bytes 589832 | tf_op jit(solution)/shard_map/ppermute | solution.py:25
  39.2 12.4 %collective-permute-start.7 = (bf16[4,4,48,128]{3,2,1,0:T(8,128)(2,1)S(1)}, bf16[4,4,48,128]{3,2,1,0:T(8,128)(2,1)S(1)}, u32[]{:S(2)}, u32[]{:S(2)}) collective-permute-start(bf16[4,4,48,128]{3,2,1,0:T(8,128)(2,1)S(1)} %get-tuple-element.10), channel_id=1, source_target_pairs={{0,2},{2,4},{4,6},{6,8},{8,10},{10,12},{12,14},{1,3},{3,5},{5,7},{... | collective-permute-start | bytes 589832 | tf_op jit(solution)/shard_map/ppermute | solution.py:23
  45.9 5.8 %copy-start.4 = (f32[5,128,128]{2,1,0:T(8,128)}, f32[5,128,128]{2,1,0:T(8,128)S(1)}, u32[]{:S(2)}) copy-start(f32[5,128,128]{2,1,0:T(8,128)S(1)} %fusion.10) | copy-start | bytes 983044
  54.6 4.6 %collective-permute-start.8 = (bf16[4,1,48,128]{3,2,1,0:T(8,128)(2,1)S(1)}, bf16[4,1,48,128]{3,2,1,0:T(8,128)(2,1)S(1)}, u32[]{:S(2)}, u32[]{:S(2)}) collective-permute-start(bf16[4,1,48,128]{3,2,1,0:T(8,128)(2,1)S(1)} %get-tuple-element.26), channel_id=1, source_target_pairs={{0,1},{2,3},{4,5},{6,7},{8,9},{10,11},{12,13},{14,15},{16,17},{18,... | collective-permute-start | bytes 147464 | tf_op jit(solution)/shard_map/ppermute | solution.py:23
  56.6 3.1 %collective-permute-start.9 = (bf16[4,1,48,128]{3,2,1,0:T(8,128)(2,1)S(1)}, bf16[4,1,48,128]{3,2,1,0:T(8,128)(2,1)S(1)}, u32[]{:S(2)}, u32[]{:S(2)}) collective-permute-start(bf16[4,1,48,128]{3,2,1,0:T(8,128)(2,1)S(1)} %get-tuple-element.27), channel_id=1, source_target_pairs={{1,0},{3,2},{5,4},{7,6},{9,8},{11,10},{13,12},{15,14},{17,16},{19,... | collective-permute-start | bytes 147464 | tf_op jit(solution)/shard_map/ppermute | solution.py:25
  58.4 0.8 copy-start.2
  62.4 0.7 copy-start.7
  63.3 4.3 %collective-permute-start.10 = (f32[4,1,12,128]{3,1,2,0:T(1,128)S(1)}, f32[4,1,12,128]{3,1,2,0:T(1,128)S(1)}, u32[]{:S(2)}, u32[]{:S(2)}) collective-permute-start(f32[4,1,12,128]{3,1,2,0:T(1,128)S(1)} %get-tuple-element.41), channel_id=1, source_target_pairs={{1,0},{3,2},{5,4},{7,6},{9,8},{11,10},{13,12},{15,14},{17,16},{19,... | collective-permute-start | bytes 73736 | tf_op jit(solution)/shard_map/ppermute | solution.py:12
  64.6 3.9 %collective-permute-start.11 = (f32[4,1,12,128]{3,1,2,0:T(1,128)S(1)}, f32[4,1,12,128]{3,1,2,0:T(1,128)S(1)}, u32[]{:S(2)}, u32[]{:S(2)}) collective-permute-start(f32[4,1,12,128]{3,1,2,0:T(1,128)S(1)} %get-tuple-element.40), channel_id=1, source_target_pairs={{0,1},{2,3},{4,5},{6,7},{8,9},{10,11},{12,13},{14,15},{16,17},{18,... | collective-permute-start | bytes 73736 | tf_op jit(solution)/shard_map/ppermute | solution.py:12
  153.4 2.0 %copy-start.5 = (f32[5,128,128]{2,1,0:T(8,128)S(1)}, f32[5,128,128]{2,1,0:T(8,128)}, u32[]{:S(2)}) copy-start(f32[5,128,128]{2,1,0:T(8,128)} %get-tuple-element.59) | copy-start | bytes 983044
Sparse Core Ops, SparseCore 0:
  59.3 93.9 all-reduce.7
where the time goes:
time: 163 us
  waiting for transfers between devices  102 us (63%)
  starting transfers between devices  26.5 us (16%)
  between operations  14.7 us (9%)
  matrix products  9.25 us (6%)
  local copies, waits for them, and re-layouts  7.29 us (4%)
  other arithmetic  3.34 us (2%)
    psum x1, waiting for transfers between devices, local(): grad_spatial = lax.psum(spatial_local, ('space', 'tm'))  84.1 us
    ppermute x5, starting transfers between devices, extended(): lax.ppermute(tail, axis, [(i, (i + 1) % count) for i in range(ends)])  15.7 us
    ppermute x5, waiting for transfers between devices, extended(): lax.ppermute(head, axis, [((i + 1) % count, i) for i in range(ends)])  8.69 us
    ppermute x5, waiting for transfers between devices, extended(): lax.ppermute(tail, axis, [(i, (i + 1) % count) for i in range(ends)])  8.19 us
    ppermute x5, starting transfers between devices, extended(): lax.ppermute(head, axis, [((i + 1) % count, i) for i in range(ends)])  6.45 us
    unnamed x19, local copies, waits for them, and re-layouts  6.45 us
    ppermute x2, starting transfers between devices, shifted(): return lax.ppermute(value, axis, pairs)  4.32 us
    dot_general x18, matrix products, conv_three(): jnp.dot(frame_window, kernel, preferred_element_type=jnp.float32)  3.61 us
  transfers between devices with their start and end apart: 13, of which 9 were waited for; matrix products, arithmetic and copies ran while one was open for 4% of the time, Pallas kernels for 0%

commit v1 on v0

v1 whole, which is shorter than its diff:
```python
import jax
import jax.numpy as jnp
import numpy as np
from jax import lax
from jax.experimental import pallas as pl
from jax.experimental.pallas import tpu as pltpu
from jax.sharding import PartitionSpec as P

BF = jnp.bfloat16
F32 = jnp.float32
C = 128
FRAMES = 4
ROWS = 4
COLS = 48
LROWS = 2
LCOLS = 12
PIX = ROWS * COLS
LOW = LROWS * LCOLS
TAPS = 9
LT = TAPS * LOW
GROUP = 2 * PIX
BOTH = ("space", "tm")


def up_matrix(n):
    m = np.zeros((4 * n, n))
    for k in range(n):
        lo, hi = max(k - 1, 0), min(k + 1, n - 1)
        for j, (a, at) in enumerate(((0.375, lo), (0.125, lo), (0.125, hi), (0.375, hi))):
            m[4 * k + j, at] += a
            m[4 * k + j, k] += 1.0 - a
    return m


def moved(m, tap):
    out = np.zeros_like(m)
    for i in range(m.shape[0]):
        if 0 <= i + tap - 1 < m.shape[0]:
            out[i] = m[i + tap - 1]
    return out


def constants():
    rows, cols = up_matrix(LROWS), up_matrix(LCOLS)
    up = np.kron(rows, cols).reshape(2, PIX, LOW)
    conv = np.concatenate(
        [np.kron(moved(rows, a), moved(cols, b)) for a in range(3) for b in range(3)], axis=1
    ).reshape(2, PIX, LT)
    as_bf = lambda m: jnp.asarray(m, BF)
    return as_bf(up), as_bf(conv), as_bf(up.transpose(0, 2, 1)), as_bf(conv.transpose(0, 2, 1))


def dot(a, b, dims=((1,), (0,))):
    return lax.dot_general(a, b, (dims, ((), ())), preferred_element_type=F32)


def lanes(parts):
    return jnp.concatenate(parts, axis=1)


def forward_kernel(
    base, near, far_near, cot, conv, up, ws, wt, res, gt, d2, slope1, slope2, z, act
):
    core = lax.axis_index("tm")
    at = lax.axis_index("space")
    count = lax.axis_size("space")

    def low_res(block, slot):
        for tap in range(TAPS):
            prod = dot(block, ws[tap]).reshape(FRAMES, LOW, C)
            z[pl.ds(slot * FRAMES, FRAMES), tap * LOW : (tap + 1) * LOW, :] = prod

    low_res(base[...], 2)
    mine_back = core == 0
    for ref, back in ((near, mine_back), (far_near, jnp.logical_not(mine_back))):
        for hop in (1, 2):
            inside = jnp.where(back, at - hop >= 0, at + hop < count)
            block = ref[(hop - 1) * FRAMES * LOW : hop * FRAMES * LOW, :]
            block = jnp.where(inside, block, jnp.zeros_like(block))
            low_res(block, jnp.where(back, 2 - hop, 2 + hop))

    matrix = conv[core]
    for p in range(5 * FRAMES // 2):
        pair = lanes([z[2 * p], z[2 * p + 1]]).astype(BF)
        pre = dot(matrix, pair)
        sig = jax.nn.sigmoid(pre)
        one = (pre * sig).astype(BF)
        for k in range(2):
            act[p * GROUP + k * PIX : p * GROUP + (k + 1) * PIX, :] = one[:, k * C : (k + 1) * C]
        if p in (4, 5):
            slope = sig * (1.0 + pre * (1.0 - sig))
            for k in range(2):
                lo = (p - 4) * GROUP + k * PIX
                slope1[lo : lo + PIX, :] = slope[:, k * C : (k + 1) * C]

    zero = jnp.zeros((C, C), BF)
    time = jnp.concatenate(
        [
            lanes([wt[k] if k < 5 else zero, wt[k - 1] if k > 0 else zero])
            for k in range(6)
        ],
        axis=0,
    )

    def window(first):
        return lanes([act[(first + k) * GROUP : (first + k + 1) * GROUP, :] for k in range(6)])

    def time_conv(first):
        pre = dot(window(first), time)
        sig = jax.nn.sigmoid(pre)
        return pre, sig, sig * (1.0 + pre * (1.0 - sig))

    pre, sig, slope = time_conv(2)
    extra = pre * sig
    upm = up[core]
    for p in range(2):
        for k in range(2):
            f = 2 * p + k
            big = dot(upm, base[f * LOW : (f + 1) * LOW, :]).astype(BF).astype(F32)
            res[f * PIX : (f + 1) * PIX, :] = (
                big + extra[k * PIX : (k + 1) * PIX, p * C : (p + 1) * C]
            ).astype(BF)
        lo = p * GROUP
        d2[lo : lo + GROUP, :] = (
            cot[lo : lo + GROUP, :].astype(F32) * slope[:, p * C : (p + 1) * C]
        ).astype(BF)
    for side, first in ((0, 0), (1, 4)):
        slope = time_conv(first)[2]
        for p in range(2):
            slope2[side, p * GROUP : (p + 1) * GROUP, :] = slope[:, p * C : (p + 1) * C]

    outer = dot(window(2), lanes([d2[:GROUP, :], d2[GROUP:, :]]), ((0,), (0,)))
    for t in range(5):
        gt[t] = outer[t * C : (t + 1) * C, :C] + outer[(t + 1) * C : (t + 2) * C, C:]


def backward_kernel(
    even, odd, d2, slope1, slope2, cot, base, gt, conv_t, up_t, ws, wt, send, keep, low, dsc
):
    core = lax.axis_index("tm")
    at = lax.axis_index("space")
    count = lax.axis_size("space")
    is_even = at % 2 == 0
    zeros = jnp.zeros((FRAMES * PIX, C), F32)

    def outside(first, second, inside, side):
        got = jnp.where(is_even, first[...], second[...]).astype(F32)
        return jnp.where(inside, (got * slope2[side]), zeros).astype(BF)

    before = outside(odd, even, at > 0, 0)
    after = outside(even, odd, at < count - 1, 1)
    window = lanes(
        [
            before[:GROUP],
            before[GROUP:],
            d2[:GROUP, :],
            d2[GROUP:, :],
            after[:GROUP],
            after[GROUP:],
        ]
    )
    zero = jnp.zeros((C, C), BF)
    time = jnp.concatenate(
        [
            lanes([wt[4 - k] if k < 5 else zero for k in range(6)]),
            lanes([wt[5 - k] if k > 0 else zero for k in range(6)]),
        ],
        axis=0,
    )
    back = dot(window, time, ((1,), (1,)))
    matrix = conv_t[core]
    for p in range(2):
        lo = p * GROUP
        d1 = (back[:, p * C : (p + 1) * C] * slope1[lo : lo + GROUP, :]).astype(BF)
        small = dot(matrix, lanes([d1[:PIX], d1[PIX:]]))
        dsc[2 * p] = small[:, :C]
        dsc[2 * p + 1] = small[:, C:]
    taps = [
        dsc[:, k * LOW : (k + 1) * LOW, :].reshape(FRAMES * LOW, C).astype(BF) for k in range(TAPS)
    ]
    every = lanes(taps)
    total = dot(every, lanes([ws[k] for k in range(TAPS)]), ((1,), (1,)))
    direct = dot(up_t[core], lanes([cot[f * PIX : (f + 1) * PIX, :] for f in range(FRAMES)]))
    for f in range(FRAMES):
        low[f * LOW : (f + 1) * LOW, :] = (
            total[f * LOW : (f + 1) * LOW, :] + direct[:, f * C : (f + 1) * C]
        )
    space = dot(base[...], every, ((0,), (0,)))
    grads = [space[:, k * C : (k + 1) * C] for k in range(TAPS)] + [gt[t] for t in range(5)]
    for j in range(7):
        first, second = grads[j], grads[j + 7]
        send[j] = jnp.where(core == 0, second, first).astype(send.dtype)
        keep[j] = jnp.where(core == 0, first, second)


def full(pairs, total):
    sources, targets = {a for a, _ in pairs}, {b for _, b in pairs}
    return pairs + list(
        zip(
            [i for i in range(total) if i not in sources],
            [i for i in range(total) if i not in targets],
        )
    )


def hop_pairs(count, hop):
    pairs = []
    for s in range(count):
        pairs.append((2 * s, 2 * (s + hop)) if s + hop < count else (2 * s, 2 * s + 1))
        pairs.append((2 * s + 1, 2 * (s - hop) + 1) if s - hop >= 0 else (2 * s + 1, 2 * s))
    return pairs


def swap_pairs(count, first):
    pairs = []
    for i in range(first, count - 1, 2):
        pairs += [(i, i + 1), (i + 1, i)]
    return full(pairs, count)


def swap_cores(value):
    return lax.ppermute(value, "tm", [(0, 1), (1, 0)])


def reduce_chips(value, count, core, at):
    bits = count.bit_length() - 1
    if count != 1 << bits:
        return lax.psum(value, "space").astype(BF)
    orders = [list(range(bits)), [(b + 2) % bits for b in range(bits)]] if bits > 2 else [list(range(bits))] * 2

    def pairs_of(step):
        pairs = []
        for s in range(count):
            for c in range(2):
                pairs.append((2 * s + c, 2 * (s ^ (1 << orders[c][step])) + c))
        return pairs

    def bit_of(step):
        return jnp.where(core == 0, (at >> orders[0][step]) & 1, (at >> orders[1][step]) & 1)

    levels = min(1, bits)
    for step in range(levels):
        halves = value.reshape(2, value.shape[0] // 2, C)
        bit = bit_of(step)
        out = lax.dynamic_index_in_dim(halves, 1 - bit, 0, False).astype(BF)
        mine = lax.dynamic_index_in_dim(halves, bit, 0, False)
        value = mine + lax.ppermute(out, BOTH, pairs_of(step)).astype(F32)
    for step in range(levels, bits):
        out = value.astype(BF)
        value = out.astype(F32) + lax.ppermute(out, BOTH, pairs_of(step)).astype(F32)
    value = value.astype(BF)
    for step in reversed(range(levels)):
        got = lax.ppermute(value, BOTH, pairs_of(step))
        value = jnp.where(
            bit_of(step) == 0,
            jnp.concatenate([value, got], axis=0),
            jnp.concatenate([got, value], axis=0),
        )
    return value


def local(base_latent, cotangent, w_spatial, w_temporal):
    core = lax.axis_index("tm")
    at = lax.axis_index("space")
    count = lax.axis_size("space")
    up, conv, up_t, conv_t = constants()
    ws = w_spatial.reshape(TAPS, C, C)
    cot = cotangent.reshape(FRAMES * PIX, C)
    own = base_latent.reshape(FRAMES, LCOLS, C)
    other = swap_cores(own)
    base = jnp.where(
        core == 0, jnp.concatenate([own, other], axis=1), jnp.concatenate([other, own], axis=1)
    ).reshape(FRAMES * LOW, C)
    near = jnp.concatenate(
        [lax.ppermute(base, BOTH, hop_pairs(count, hop)) for hop in (1, 2)], axis=0
    )
    far = swap_cores(near)
    even = lax.ppermute(cot, "space", swap_pairs(count, 0))
    odd = lax.ppermute(cot, "space", swap_pairs(count, 1))

    shape = jax.ShapeDtypeStruct
    n_own = FRAMES * PIX
    params = pltpu.CompilerParams(vmem_limit_bytes=32 << 20)
    res, gt, d2, slope1, slope2 = pl.pallas_call(
        forward_kernel,
        out_shape=(
            shape((n_own, C), BF),
            shape((5, C, C), F32),
            shape((n_own, C), BF),
            shape((n_own, C), F32),
            shape((2, n_own, C), F32),
        ),
        scratch_shapes=[
            pltpu.VMEM((5 * FRAMES, LT, C), F32),
            pltpu.VMEM((5 * n_own, C), BF),
        ],
        compiler_params=params,
        cost_estimate=pl.CostEstimate(flops=1 << 30, bytes_accessed=4 << 20, transcendentals=1 << 20),
        name="forward",
    )(base, near, far, cot, conv, up, ws, w_temporal)
    send, keep, low = pl.pallas_call(
        backward_kernel,
        out_shape=(shape((7, C, C), F32), shape((7, C, C), F32), shape((FRAMES * LOW, C), F32)),
        scratch_shapes=[pltpu.VMEM((FRAMES, LT, C), F32)],
        compiler_params=params,
        cost_estimate=pl.CostEstimate(flops=1 << 29, bytes_accessed=4 << 20, transcendentals=0),
        name="backward",
    )(even, odd, d2, slope1, slope2, cot, base, gt, conv_t, up_t, ws, w_temporal)

    low = low.reshape(FRAMES, LROWS, LCOLS, C)
    grad_base = lax.dynamic_slice_in_dim(low, core, 1, 1) + swap_cores(
        lax.dynamic_slice_in_dim(low, 1 - core, 1, 1)
    )
    half = (keep + swap_cores(send)).reshape(7 * C, C)
    half = reduce_chips(half, count, core, at).reshape(7, C, C)
    rest = swap_cores(half)
    grads = jnp.where(
        core == 0, jnp.concatenate([half, rest], axis=0), jnp.concatenate([rest, half], axis=0)
    ).astype(F32)
    return (
        res.reshape(cotangent.shape),
        grad_base,
        grads[:TAPS].reshape(3, 3, C, C),
        grads[TAPS:],
    )


def solution(mesh):
    rows = P(("groups", "space"), "tm", None, None)
    return jax.shard_map(
        local,
        mesh=mesh,
        in_specs=(rows, rows, P(), P()),
        out_specs=(rows, rows, P("groups", None, None, None), P("groups", None, None)),
        check_vma=False,
    )
```

time: 163 us -> 49.6 us (0.30)
  the two profiles are of different devices: /device:TPU:0 before, /device:TPU:31 now
where the time goes in v1:
time: 49.6 us; the launch traced here: 49.3 us
  waiting for transfers between devices  19.5 us (39%)
  starting transfers between devices  18.6 us (38%)
  local copies, waits for them, and re-layouts  6.01 us (12%)
  Pallas kernels  3.28 us (7%)
  other arithmetic  1.11 us (2%)
  between operations  0.77 us (2%)
    ppermute x5, starting transfers between devices, swap_cores(): return lax.ppermute(value, 'tm', [(0, 1), (1, 0)])  13.2 us
    ppermute x2, waiting for transfers between devices, reduce_chips(): lax.ppermute(out, BOTH, pairs_of(step)).astype(F32)  7.38 us
    ppermute x1, waiting for transfers between devices, reduce_chips(): value = mine + lax.ppermute(out, BOTH, pairs_of(step)).astype(F32)  5.51 us
    unnamed x18, local copies, waits for them, and re-layouts  4.35 us
    ppermute x5, waiting for transfers between devices, swap_cores(): return lax.ppermute(value, 'tm', [(0, 1), (1, 0)])  3.87 us
    ppermute x2, starting transfers between devices, local(): lax.ppermute(base, BOTH, hop_pairs(count, hop))  2.22 us
    pallas_call x1, Pallas kernels, local(): pl.pallas_call(forward_kernel, out_shape=(shape((n_own, C), BF), shape((5...  2.21 us
    ppermute x1, waiting for transfers between devices, reduce_chips(): got = lax.ppermute(value, BOTH, pairs_of(step))  1.81 us
  transfers between devices with their start and end apart: 13, of which 9 were waited for; matrix products, arithmetic and copies ran while one was open for 1% of the time, Pallas kernels for 4%

profile of v1, /device:TPU:31, one launch (start us, length us, event | category | flops | bytes accessed | tf_op | source)
XLA Modules:
  0.0 49.3 jit_solution(16102072745174228425)
XLA Ops:
  0.6 0.0 copy-start.3
  0.6 0.7 %collective-permute-start = (bf16[4,12,128]{2,0,1:T(4,128)(2,1)}, bf16[4,12,128]{2,0,1:T(4,128)(2,1)S(1)}, u32[]{:S(2)}, u32[]{:S(2)}) collective-permute-start(bf16[4,12,128]{2,0,1:T(4,128)(2,1)} %bitcast.29), channel_id=1, source_target_pairs={{0,1},{1,0},{2,3},{3,2},{4,5},{5,4},{6,7},{7,6},{8,9},{9,8},{10,11... | collective-permute-start | bytes 36872 | tf_op jit(solution)/shard_map/ppermute | solution.py:222
  1.4 1.0 %collective-permute-done = bf16[4,12,128]{2,0,1:T(4,128)(2,1)S(1)} collective-permute-done((bf16[4,12,128]{2,0,1:T(4,128)(2,1)}, bf16[4,12,128]{2,0,1:T(4,128)(2,1)S(1)}, u32[]{:S(2)}, u32[]{:S(2)}) %collective-permute-start) | collective-permute-done | bytes 12320 | tf_op jit(solution)/shard_map/ppermute | solution.py:222
  2.4 0.8 %maximum_select_fusion.2 = bf16[4,24,128]{2,0,1:T(4,128)(2,1)S(1)} fusion(bf16[4,12,128]{2,0,1:T(4,128)(2,1)S(1)} %collective-permute-done, bf16[4,12,128]{2,0,1:T(4,128)(2,1)} %bitcast.30, pred[]{:T(512)S(6)} %eq.4), kind=kLoop, calls=%fused_computation.10 | loop fusion | flops 36864 | bytes 49153 | tf_op jit(solution)/shard_map/jit(_where)/select_n | solution.py:271
  3.3 0.3 collective-permute-start.1
  3.6 1.1 %collective-permute-start.4 = (bf16[768,128]{1,0:T(8,128)(2,1)}, bf16[768,128]{1,0:T(8,128)(2,1)S(1)}, u32[]{:S(2)}, u32[]{:S(2)}) collective-permute-start(bf16[768,128]{1,0:T(8,128)(2,1)} %bitcast.16), channel_id=1, source_target_pairs={{0,2},{2,0},{4,6},{6,4},{8,10},{10,8},{12,14},{14,12},{1,3},{3,1},... | collective-permute-start | bytes 589832 | tf_op jit(solution)/shard_map/ppermute | solution.py:278
  4.7 1.6 %collective-permute-start.5 = (bf16[768,128]{1,0:T(8,128)(2,1)}, bf16[768,128]{1,0:T(8,128)(2,1)S(1)}, u32[]{:S(2)}, u32[]{:S(2)}) collective-permute-start(bf16[768,128]{1,0:T(8,128)(2,1)} %bitcast.17), channel_id=1, source_target_pairs={{2,4},{4,2},{6,8},{8,6},{10,12},{12,10},{0,0},{14,14},{3,5},{5,3},... | collective-permute-start | bytes 589832 | tf_op jit(solution)/shard_map/ppermute | solution.py:279
  6.2 1.9 %collective-permute-start.2 = (bf16[96,128]{1,0:T(8,128)(2,1)S(1)}, bf16[96,128]{1,0:T(8,128)(2,1)S(1)}, u32[]{:S(2)}, u32[]{:S(2)}) collective-permute-start(bf16[96,128]{1,0:T(8,128)(2,1)S(1)} %bitcast.21), channel_id=1, source_target_pairs={{0,4},{1,0},{2,6},{3,2},{4,8},{5,1},{6,10},{7,3},{8,12},{9,5},{10,... | collective-permute-start | bytes 73736 | tf_op jit(solution)/shard_map/ppermute | solution.py:275
  8.2 0.0 collective-permute-done.1
  8.2 0.9 %collective-permute-done.2 = bf16[96,128]{1,0:T(8,128)(2,1)S(1)} collective-permute-done((bf16[96,128]{1,0:T(8,128)(2,1)S(1)}, bf16[96,128]{1,0:T(8,128)(2,1)S(1)}, u32[]{:S(2)}, u32[]{:S(2)}) %collective-permute-start.2) | collective-permute-done | bytes 24608 | tf_op jit(solution)/shard_map/ppermute | solution.py:275
  9.1 5.4 %collective-permute-start.3 = (bf16[192,128]{1,0:T(8,128)(2,1)S(1)}, bf16[192,128]{1,0:T(8,128)(2,1)S(1)}, u32[]{:S(2)}, u32[]{:S(2)}) collective-permute-start(bf16[192,128]{1,0:T(8,128)(2,1)S(1)} %constant_dynamic-update-slice_fusion.near), channel_id=1, source_target_pairs={{0,1},{1,0},{2,3},{3,2},{4,5},{5,4},{6,7},{7,6},{8,9},{9,8},{10,11... | collective-permute-start | bytes 147464 | tf_op jit(solution)/shard_map/ppermute | solution.py:222
  14.5 0.9 %collective-permute-done.3.far_near = bf16[192,128]{1,0:T(8,128)(2,1)S(1)} collective-permute-done((bf16[192,128]{1,0:T(8,128)(2,1)S(1)}, bf16[192,128]{1,0:T(8,128)(2,1)S(1)}, u32[]{:S(2)}, u32[]{:S(2)}) %collective-permute-start.3) | collective-permute-done | bytes 49184 | tf_op jit(solution)/shard_map/ppermute | solution.py:222
  15.4 0.0 copy-done.3
  15.4 0.0 copy-start
  15.4 1.0 %copy-done = bf16[3,3,128,128]{3,2,1,0:T(8,128)(2,1)S(1)} copy-done((bf16[3,3,128,128]{3,2,1,0:T(8,128)(2,1)S(1)}, bf16[3,3,128,128]{3,2,1,0:T(8,128)(2,1)}, u32[]{:S(2)}) %copy-start) | copy-done | bytes 294936
  16.3 0.0 copy-start.4
  16.3 0.9 %copy-done.4 = bf16[5,128,128]{2,1,0:T(8,128)(2,1)S(1)} copy-done((bf16[5,128,128]{2,1,0:T(8,128)(2,1)S(1)}, bf16[5,128,128]{2,1,0:T(8,128)(2,1)}, u32[]{:S(2)}) %copy-start.4) | copy-done | bytes 163864
  17.3 0.0 copy-start.6
  17.3 0.9 %copy-done.6 = bf16[2,192,216]{2,1,0:T(8,128)(2,1)S(1)} copy-done((bf16[2,192,216]{2,1,0:T(8,128)(2,1)S(1)}, bf16[2,192,216]{2,1,0:T(8,128)(2,1)}, u32[]{:S(2)}) %copy-start.6) | copy-done | bytes 165912
  18.2 0.0 copy-start.7
  18.2 0.9 %copy-done.7 = bf16[2,192,24]{2,1,0:T(8,128)(2,1)S(1)} copy-done((bf16[2,192,24]{2,1,0:T(8,128)(2,1)S(1)}, bf16[2,192,24]{2,1,0:T(8,128)(2,1)}, u32[]{:S(2)}) %copy-start.7) | copy-done | bytes 18456
  19.1 0.0 copy-start.1
  19.1 0.0 copy-start.2
  19.1 0.0 copy-start.5
  19.1 2.2 %forward.1 = (bf16[768,128]{1,0:T(8,128)(2,1)}, f32[5,128,128]{2,1,0:T(8,128)S(1)}, bf16[768,128]{1,0:T(8,128)(2,1)S(1)}, f32[768,128]{1,0:T(8,128)S(1)}, f32[2,768,128]{2,1,0:T(8,128)S(1)}) custom-call(bf16[96,128]{1,0:T(8,128)(2,1)S(1)} %bitcast.22, bf16[192,128]{1,0:T(8,128)(2,1)S(1)} %constant_dynamic-update-slice_fusion.near, ...), custom_call_target="tpu_custom_call" | custom-call | flops 1073741824 | bytes 4194304 | tf_op jit(solution)/shard_map/forward/pallas_call | solution.py:284
  21.3 0.0 collective-permute-done.4.even
  21.3 0.0 collective-permute-done.5.odd
  21.3 0.0 copy-done.1
  21.3 0.0 copy-done.2
  21.3 0.0 copy-done.5
  21.3 1.1 %backward.1 = (f32[7,128,128]{2,1,0:T(8,128)S(1)}, f32[7,128,128]{2,1,0:T(8,128)S(1)}, f32[96,128]{1,0:T(8,128)S(1)}) custom-call(bf16[768,128]{1,0:T(8,128)(2,1)S(1)} %collective-permute-done.4.even, bf16[768,128]{1,0:T(8,128)(2,1)S(1)} %collective-permute-done.5.odd, bf16[768,128]{1,0:T(8,128)(2,1)S(1)} %get-tuple-element.13.d2, ...), custom_call_target="tpu_custom_call" | custom-call | flops 536870912 | bytes 4194304 | tf_op jit(solution)/shard_map/backward/pallas_call | solution.py:301
  22.4 0.4 collective-permute-start.7
  22.8 1.5 %collective-permute-done.7 = f32[7,128,128]{2,1,0:T(8,128)S(1)} collective-permute-done((f32[7,128,128]{2,1,0:T(8,128)S(1)}, f32[7,128,128]{2,1,0:T(8,128)S(1)}, u32[]{:S(2)}, u32[]{:S(2)}) %collective-permute-start.7) | collective-permute-done | bytes 458784 | tf_op jit(solution)/shard_map/ppermute | solution.py:222
  24.4 0.3 collective-permute-start.8
  24.7 5.5 %collective-permute-done.8 = bf16[448,128]{1,0:T(8,128)(2,1)S(1)} collective-permute-done((bf16[448,128]{1,0:T(8,128)(2,1)S(1)}, bf16[448,128]{1,0:T(8,128)(2,1)S(1)}, u32[]{:S(2)}, u32[]{:S(2)}) %collective-permute-start.8) | collective-permute-done | bytes 114720 | tf_op jit(solution)/shard_map/ppermute | solution.py:247
  30.2 0.1 collective-permute-start.9
  30.3 3.7 %collective-permute-done.9 = bf16[448,128]{1,0:T(8,128)(2,1)S(1)} collective-permute-done((bf16[448,128]{1,0:T(8,128)(2,1)S(1)}, bf16[448,128]{1,0:T(8,128)(2,1)S(1)}, u32[]{:S(2)}, u32[]{:S(2)}) %collective-permute-start.9) | collective-permute-done | bytes 114720 | tf_op jit(solution)/shard_map/ppermute | solution.py:250
  34.1 0.1 collective-permute-start.10
  34.2 3.6 %collective-permute-done.10 = bf16[448,128]{1,0:T(8,128)(2,1)S(1)} collective-permute-done((bf16[448,128]{1,0:T(8,128)(2,1)S(1)}, bf16[448,128]{1,0:T(8,128)(2,1)S(1)}, u32[]{:S(2)}, u32[]{:S(2)}) %collective-permute-start.10) | collective-permute-done | bytes 114720 | tf_op jit(solution)/shard_map/ppermute | solution.py:250
  37.8 0.1 collective-permute-start.11
  38.0 3.7 %collective-permute-start.6 = (f32[4,1,12,128]{3,2,1,0:T(8,128)S(1)}, f32[4,1,12,128]{3,2,1,0:T(8,128)S(1)}, u32[]{:S(2)}, u32[]{:S(2)}) collective-permute-start(f32[4,1,12,128]{3,2,1,0:T(8,128)S(1)} %constant_dynamic-slice_fusion), channel_id=1, source_target_pairs={{0,1},{1,0},{2,3},{3,2},{4,5},{5,4},{6,7},{7,6},{8,9},{9,8},{10,11... | collective-permute-start | bytes 73736 | tf_op jit(solution)/shard_map/ppermute | solution.py:222
  41.7 1.8 %collective-permute-done.11 = bf16[448,128]{1,0:T(8,128)(2,1)S(1)} collective-permute-done((bf16[448,128]{1,0:T(8,128)(2,1)S(1)}, bf16[448,128]{1,0:T(8,128)(2,1)S(1)}, u32[]{:S(2)}, u32[]{:S(2)}) %collective-permute-start.11) | collective-permute-done | bytes 114720 | tf_op jit(solution)/shard_map/ppermute | solution.py:253
  43.5 0.1 maximum_select_fusion.1
  43.6 2.9 %collective-permute-start.12 = (bf16[7,128,128]{2,1,0:T(8,128)(2,1)S(1)}, bf16[7,128,128]{2,1,0:T(8,128)(2,1)S(1)}, u32[]{:S(2)}, u32[]{:S(2)}) collective-permute-start(bf16[7,128,128]{2,1,0:T(8,128)(2,1)S(1)} %bitcast.26), channel_id=1, source_target_pairs={{0,1},{1,0},{2,3},{3,2},{4,5},{5,4},{6,7},{7,6},{8,9},{9,8},{10,11... | collective-permute-start | bytes 688136 | tf_op jit(solution)/shard_map/ppermute | solution.py:222
  46.5 0.0 collective-permute-done.6
  46.5 0.6 %copy.16 = f32[4,1,12,128]{3,1,2,0:T(1,128)} copy(f32[4,1,12,128]{3,2,1,0:T(8,128)S(1)} %dynamic-slice_add_fusion) | data formatting | bytes 49152
  47.2 0.5 collective-permute-done.12
  47.6 0.1 fusion
  47.7 0.9 %slice.8 = f32[9,128,128]{2,1,0:T(8,128)} slice(f32[14,128,128]{2,1,0:T(8,128)S(1)} %fusion), slice={[0:9], [0:128], [0:128]} | slice | bytes 1179648 | tf_op jit(solution)/shard_map/slice | solution.py:323
  48.6 0.7 %slice.9 = f32[5,128,128]{2,1,0:T(8,128)} slice(f32[14,128,128]{2,1,0:T(8,128)S(1)} %fusion), slice={[9:14], [0:128], [0:128]} | slice | bytes 655360 | tf_op jit(solution)/shard_map/slice | solution.py:324
  (11 shorter events, 0.2 us)
Async XLA Ops:
  0.6 14.7 %copy-start.3 = (bf16[4,4,48,128]{3,2,1,0:T(8,128)(2,1)S(1)}, bf16[4,4,48,128]{3,2,1,0:T(8,128)(2,1)}, u32[]{:S(2)}) copy-start(bf16[4,4,48,128]{3,2,1,0:T(8,128)(2,1)} %param.9) | copy-start | bytes 589828
  0.6 1.8 %collective-permute-start = (bf16[4,12,128]{2,0,1:T(4,128)(2,1)}, bf16[4,12,128]{2,0,1:T(4,128)(2,1)S(1)}, u32[]{:S(2)}, u32[]{:S(2)}) collective-permute-start(bf16[4,12,128]{2,0,1:T(4,128)(2,1)} %bitcast.29), channel_id=1, source_target_pairs={{0,1},{1,0},{2,3},{3,2},{4,5},{5,4},{6,7},{7,6},{8,9},{9,8},{10,11... | collective-permute-start | bytes 36872 | tf_op jit(solution)/shard_map/ppermute | solution.py:222
  3.3 4.9 %collective-permute-start.1 = (bf16[96,128]{1,0:T(8,128)(2,1)S(1)}, bf16[96,128]{1,0:T(8,128)(2,1)S(1)}, u32[]{:S(2)}, u32[]{:S(2)}) collective-permute-start(bf16[96,128]{1,0:T(8,128)(2,1)S(1)} %bitcast.20), channel_id=1, source_target_pairs={{0,2},{1,0},{2,4},{3,1},{4,6},{5,3},{6,8},{7,5},{8,10},{9,7},{10,1... | collective-permute-start | bytes 73736 | tf_op jit(solution)/shard_map/ppermute | solution.py:275
  3.6 17.7 %collective-permute-start.4 = (bf16[768,128]{1,0:T(8,128)(2,1)}, bf16[768,128]{1,0:T(8,128)(2,1)S(1)}, u32[]{:S(2)}, u32[]{:S(2)}) collective-permute-start(bf16[768,128]{1,0:T(8,128)(2,1)} %bitcast.16), channel_id=1, source_target_pairs={{0,2},{2,0},{4,6},{6,4},{8,10},{10,8},{12,14},{14,12},{1,3},{3,1},... | collective-permute-start | bytes 589832 | tf_op jit(solution)/shard_map/ppermute | solution.py:278
  4.7 16.6 %collective-permute-start.5 = (bf16[768,128]{1,0:T(8,128)(2,1)}, bf16[768,128]{1,0:T(8,128)(2,1)S(1)}, u32[]{:S(2)}, u32[]{:S(2)}) collective-permute-start(bf16[768,128]{1,0:T(8,128)(2,1)} %bitcast.17), channel_id=1, source_target_pairs={{2,4},{4,2},{6,8},{8,6},{10,12},{12,10},{0,0},{14,14},{3,5},{5,3},... | collective-permute-start | bytes 589832 | tf_op jit(solution)/shard_map/ppermute | solution.py:279
  6.2 2.9 %collective-permute-start.2 = (bf16[96,128]{1,0:T(8,128)(2,1)S(1)}, bf16[96,128]{1,0:T(8,128)(2,1)S(1)}, u32[]{:S(2)}, u32[]{:S(2)}) collective-permute-start(bf16[96,128]{1,0:T(8,128)(2,1)S(1)} %bitcast.21), channel_id=1, source_target_pairs={{0,4},{1,0},{2,6},{3,2},{4,8},{5,1},{6,10},{7,3},{8,12},{9,5},{10,... | collective-permute-start | bytes 73736 | tf_op jit(solution)/shard_map/ppermute | solution.py:275
  9.1 6.3 %collective-permute-start.3 = (bf16[192,128]{1,0:T(8,128)(2,1)S(1)}, bf16[192,128]{1,0:T(8,128)(2,1)S(1)}, u32[]{:S(2)}, u32[]{:S(2)}) collective-permute-start(bf16[192,128]{1,0:T(8,128)(2,1)S(1)} %constant_dynamic-update-slice_fusion.near), channel_id=1, source_target_pairs={{0,1},{1,0},{2,3},{3,2},{4,5},{5,4},{6,7},{7,6},{8,9},{9,8},{10,11... | collective-permute-start | bytes 147464 | tf_op jit(solution)/shard_map/ppermute | solution.py:222
  15.4 1.0 %copy-start = (bf16[3,3,128,128]{3,2,1,0:T(8,128)(2,1)S(1)}, bf16[3,3,128,128]{3,2,1,0:T(8,128)(2,1)}, u32[]{:S(2)}) copy-start(bf16[3,3,128,128]{3,2,1,0:T(8,128)(2,1)} %param.10) | copy-start | bytes 884740
  16.3 0.9 %copy-start.4 = (bf16[5,128,128]{2,1,0:T(8,128)(2,1)S(1)}, bf16[5,128,128]{2,1,0:T(8,128)(2,1)}, u32[]{:S(2)}) copy-start(bf16[5,128,128]{2,1,0:T(8,128)(2,1)} %wt.3) | copy-start | bytes 491524
  17.3 0.9 %copy-start.6 = (bf16[2,192,216]{2,1,0:T(8,128)(2,1)S(1)}, bf16[2,192,216]{2,1,0:T(8,128)(2,1)}, u32[]{:S(2)}) copy-start(bf16[2,192,216]{2,1,0:T(8,128)(2,1)} %constant.32.clone.conv) | copy-start | bytes 497668
  18.2 0.9 %copy-start.7 = (bf16[2,192,24]{2,1,0:T(8,128)(2,1)S(1)}, bf16[2,192,24]{2,1,0:T(8,128)(2,1)}, u32[]{:S(2)}) copy-start(bf16[2,192,24]{2,1,0:T(8,128)(2,1)} %constant.31.clone.up) | copy-start | bytes 55300
  19.1 2.2 %copy-start.1 = (bf16[3,3,128,128]{3,2,1,0:T(8,128)(2,1)S(1)}, bf16[3,3,128,128]{3,2,1,0:T(8,128)(2,1)}, u32[]{:S(2)}) copy-start(bf16[3,3,128,128]{3,2,1,0:T(8,128)(2,1)} %param.10) | copy-start | bytes 884740
  19.1 2.2 %copy-start.2 = (bf16[2,216,192]{2,1,0:T(8,128)(2,1)S(1)}, bf16[2,216,192]{2,1,0:T(8,128)(2,1)}, u32[]{:S(2)}) copy-start(bf16[2,216,192]{2,1,0:T(8,128)(2,1)} %constant.34.clone.conv_t) | copy-start | bytes 497668
  19.1 2.2 %copy-start.5 = (bf16[2,24,192]{2,1,0:T(8,128)(2,1)S(1)}, bf16[2,24,192]{2,1,0:T(8,128)(2,1)}, u32[]{:S(2)}) copy-start(bf16[2,24,192]{2,1,0:T(8,128)(2,1)} %constant.33.clone.up_t) | copy-start | bytes 55300
  22.4 1.9 %collective-permute-start.7 = (f32[7,128,128]{2,1,0:T(8,128)S(1)}, f32[7,128,128]{2,1,0:T(8,128)S(1)}, u32[]{:S(2)}, u32[]{:S(2)}) collective-permute-start(f32[7,128,128]{2,1,0:T(8,128)S(1)} %get-tuple-element.19), channel_id=1, source_target_pairs={{0,1},{1,0},{2,3},{3,2},{4,5},{5,4},{6,7},{7,6},{8,9},{9,8},{10,11... | collective-permute-start | bytes 1376264 | tf_op jit(solution)/shard_map/ppermute | solution.py:222
  24.4 5.8 %collective-permute-start.8 = (bf16[448,128]{1,0:T(8,128)(2,1)S(1)}, bf16[448,128]{1,0:T(8,128)(2,1)S(1)}, u32[]{:S(2)}, u32[]{:S(2)}) collective-permute-start(bf16[448,128]{1,0:T(8,128)(2,1)S(1)} %fusion.2), channel_id=1, source_target_pairs={{0,2},{1,9},{2,0},{3,11},{4,6},{5,13},{6,4},{7,15},{8,10},{9,1},{1... | collective-permute-start | bytes 344072 | tf_op jit(solution)/shard_map/ppermute | solution.py:247
  30.2 3.8 %collective-permute-start.9 = (bf16[448,128]{1,0:T(8,128)(2,1)S(1)}, bf16[448,128]{1,0:T(8,128)(2,1)S(1)}, u32[]{:S(2)}, u32[]{:S(2)}) collective-permute-start(bf16[448,128]{1,0:T(8,128)(2,1)S(1)} %fusion.1), channel_id=1, source_target_pairs={{0,4},{1,3},{2,6},{3,1},{4,0},{5,7},{6,2},{7,5},{8,12},{9,11},{10,... | collective-permute-start | bytes 344072 | tf_op jit(solution)/shard_map/ppermute | solution.py:250
  34.1 3.7 %collective-permute-start.10 = (bf16[448,128]{1,0:T(8,128)(2,1)S(1)}, bf16[448,128]{1,0:T(8,128)(2,1)S(1)}, u32[]{:S(2)}, u32[]{:S(2)}) collective-permute-start(bf16[448,128]{1,0:T(8,128)(2,1)S(1)} %add_convert_fusion.1), channel_id=1, source_target_pairs={{0,8},{1,5},{2,10},{3,7},{4,12},{5,1},{6,14},{7,3},{8,0},{9,13},{1... | collective-permute-start | bytes 344072 | tf_op jit(solution)/shard_map/ppermute | solution.py:250
  37.8 5.7 %collective-permute-start.11 = (bf16[448,128]{1,0:T(8,128)(2,1)S(1)}, bf16[448,128]{1,0:T(8,128)(2,1)S(1)}, u32[]{:S(2)}, u32[]{:S(2)}) collective-permute-start(bf16[448,128]{1,0:T(8,128)(2,1)S(1)} %add_convert_fusion), channel_id=1, source_target_pairs={{0,2},{1,9},{2,0},{3,11},{4,6},{5,13},{6,4},{7,15},{8,10},{9,1},{1... | collective-permute-start | bytes 344072 | tf_op jit(solution)/shard_map/ppermute | solution.py:253
  38.0 8.5 %collective-permute-start.6 = (f32[4,1,12,128]{3,2,1,0:T(8,128)S(1)}, f32[4,1,12,128]{3,2,1,0:T(8,128)S(1)}, u32[]{:S(2)}, u32[]{:S(2)}) collective-permute-start(f32[4,1,12,128]{3,2,1,0:T(8,128)S(1)} %constant_dynamic-slice_fusion), channel_id=1, source_target_pairs={{0,1},{1,0},{2,3},{3,2},{4,5},{5,4},{6,7},{7,6},{8,9},{9,8},{10,11... | collective-permute-start | bytes 73736 | tf_op jit(solution)/shard_map/ppermute | solution.py:222
  43.6 4.0 %collective-permute-start.12 = (bf16[7,128,128]{2,1,0:T(8,128)(2,1)S(1)}, bf16[7,128,128]{2,1,0:T(8,128)(2,1)S(1)}, u32[]{:S(2)}, u32[]{:S(2)}) collective-permute-start(bf16[7,128,128]{2,1,0:T(8,128)(2,1)S(1)} %bitcast.26), channel_id=1, source_target_pairs={{0,1},{1,0},{2,3},{3,2},{4,5},{5,4},{6,7},{7,6},{8,9},{9,8},{10,11... | collective-permute-start | bytes 688136 | tf_op jit(solution)/shard_map/ppermute | solution.py:222

commit v2 on v1

v2 whole, which is shorter than its diff:
```python
import jax
import jax.numpy as jnp
import numpy as np
from jax import lax
from jax.experimental import pallas as pl
from jax.experimental.pallas import tpu as pltpu
from jax.sharding import PartitionSpec as P

BF = jnp.bfloat16
F32 = jnp.float32
C = 128
FRAMES = 4
ROWS = 4
COLS = 48
LROWS = 2
LCOLS = 12
PIX = ROWS * COLS
LOW = LROWS * LCOLS
TAPS = 9
LT = TAPS * LOW
GROUP = 2 * PIX
BOTH = ("space", "tm")


def up_matrix(n):
    m = np.zeros((4 * n, n))
    for k in range(n):
        lo, hi = max(k - 1, 0), min(k + 1, n - 1)
        for j, (a, at) in enumerate(((0.375, lo), (0.125, lo), (0.125, hi), (0.375, hi))):
            m[4 * k + j, at] += a
            m[4 * k + j, k] += 1.0 - a
    return m


def moved(m, tap):
    out = np.zeros_like(m)
    for i in range(m.shape[0]):
        if 0 <= i + tap - 1 < m.shape[0]:
            out[i] = m[i + tap - 1]
    return out


def constants():
    rows, cols = up_matrix(LROWS), up_matrix(LCOLS)
    up = np.kron(rows, cols).reshape(2, PIX, LOW)
    conv = np.concatenate(
        [np.kron(moved(rows, a), moved(cols, b)) for a in range(3) for b in range(3)], axis=1
    ).reshape(2, PIX, LT)
    as_bf = lambda m: jnp.asarray(m, BF)
    return as_bf(up), as_bf(conv), as_bf(up.transpose(0, 2, 1)), as_bf(conv.transpose(0, 2, 1))


def dot(a, b, dims=((1,), (0,))):
    return lax.dot_general(a, b, (dims, ((), ())), preferred_element_type=F32)


def lanes(parts):
    return jnp.concatenate(parts, axis=1)


def prepare_kernel(
    base, cot_h, conv_h, conv_t_h, up_h, up_t_h, ws_h, wt_h,
    ws, cot, conv, conv_t, time, time_t, big, direct, act, slope1,
    up, up_t, wt, z, sems,
):
    core = lax.axis_index("tm")
    copies = [
        pltpu.make_async_copy(src, dst, sems.at[i])
        for i, (src, dst) in enumerate(
            (
                (ws_h, ws),
                (conv_h.at[core], conv),
                (up_h.at[core], up),
                (cot_h, cot),
                (up_t_h.at[core], up_t),
                (wt_h, wt),
                (conv_t_h.at[core], conv_t),
            )
        )
    ]
    for copy in copies:
        copy.start()
    for copy in copies[:3]:
        copy.wait()
    low_res(base[...], ws, z)
    for p in range(FRAMES // 2):
        pre = dot(conv[...], lanes([z[2 * p], z[2 * p + 1]]).astype(BF))
        sig = jax.nn.sigmoid(pre)
        one = (pre * sig).astype(BF)
        slope = sig * (1.0 + pre * (1.0 - sig))
        for k in range(2):
            lo = p * GROUP + k * PIX
            act[lo : lo + PIX, :] = one[:, k * C : (k + 1) * C]
            slope1[lo : lo + PIX, :] = slope[:, k * C : (k + 1) * C]
    for f in range(FRAMES):
        big[f * PIX : (f + 1) * PIX, :] = dot(up[...], base[f * LOW : (f + 1) * LOW, :]).astype(BF)
    for copy in copies[3:]:
        copy.wait()
    both = dot(up_t[...], lanes([cot[f * PIX : (f + 1) * PIX, :] for f in range(FRAMES)]))
    for f in range(FRAMES):
        direct[f * LOW : (f + 1) * LOW, :] = both[:, f * C : (f + 1) * C]
    zero = jnp.zeros((C, C), BF)
    for k in range(6):
        here = slice(k * C, (k + 1) * C)
        time[here, :C] = wt[k] if k < 5 else zero
        time[here, C:] = wt[k - 1] if k > 0 else zero
        time_t[:C, here] = wt[4 - k] if k < 5 else zero
        time_t[C:, here] = wt[5 - k] if k > 0 else zero


def low_res(block, ws, z):
    frames = block.shape[0] // LOW
    for first in range(0, TAPS, 2):
        taps = range(first, min(first + 2, TAPS))
        prod = dot(block, lanes([ws[tap] for tap in taps]))
        for k, tap in enumerate(taps):
            z[:, tap * LOW : (tap + 1) * LOW, :] = prod[:, k * C : (k + 1) * C].reshape(
                frames, LOW, C
            )


def main_kernel(
    near, far, even, odd, ws, conv, conv_t, act_own, slope1, time, time_t, cot, base,
    send, keep, every, act_near, d2_own, extra, z, act,
):
    core = lax.axis_index("tm")
    at = lax.axis_index("space")
    count = lax.axis_size("space")
    size = FRAMES * LOW
    before = jnp.where(core == 0, near[...], far[...])
    after = jnp.where(core == 0, far[...], near[...])
    none = jnp.zeros((size, C), BF)
    low_res(
        jnp.concatenate(
            [
                jnp.where(at >= 2, before[size:], none),
                jnp.where(at >= 1, before[:size], none),
                jnp.where(at + 1 < count, after[:size], none),
                jnp.where(at + 2 < count, after[size:], none),
            ],
            axis=0,
        ),
        ws,
        z,
    )
    for p in range(2 * FRAMES):
        group = p if p < FRAMES else p + FRAMES // 2
        pre = dot(conv[...], lanes([z[2 * p], z[2 * p + 1]]).astype(BF))
        one = (pre * jax.nn.sigmoid(pre)).astype(BF)
        for k in range(2):
            part = one[:, k * C : (k + 1) * C]
            lo = group * GROUP + k * PIX
            act[lo : lo + PIX, :] = part
            if 2 <= group < 8:
                act_near[lo - 2 * GROUP : lo - 2 * GROUP + PIX, :] = part
    act_near[2 * GROUP : 4 * GROUP, :] = act_own[...]

    def group_of(p):
        if p in (4, 5):
            return act_own[(p - 4) * GROUP : (p - 3) * GROUP, :]
        return act[p * GROUP : (p + 1) * GROUP, :]

    def time_conv(first):
        pre = dot(lanes([group_of(first + k) for k in range(6)]), time[...])
        sig = jax.nn.sigmoid(pre)
        return pre, sig, sig * (1.0 + pre * (1.0 - sig))

    is_even = at % 2 == 0
    blank = jnp.zeros((GROUP, C), BF)
    d2 = []
    for first, inside in ((0, at > 0), (2, None), (4, at < count - 1)):
        pre, sig, slope = time_conv(first)
        for p in range(2):
            here = slice(p * GROUP, (p + 1) * GROUP)
            part = slice(p * C, (p + 1) * C)
            if inside is None:
                got = cot[here, :]
                extra[here, :] = pre[:, part] * sig[:, part]
            else:
                first_choice, other = (odd, even) if first == 0 else (even, odd)
                got = jnp.where(is_even, first_choice[here, :], other[here, :])
                got = jnp.where(inside, got, blank)
            value = (got.astype(F32) * slope[:, part]).astype(BF)
            if inside is None:
                d2_own[here, :] = value
            d2.append(value)

    back = dot(lanes(d2), time_t[...], ((1,), (1,)))
    for p in range(2):
        lo = p * GROUP
        d1 = (back[:, p * C : (p + 1) * C] * slope1[lo : lo + GROUP, :]).astype(BF)
        small = dot(conv_t[...], lanes([d1[:PIX], d1[PIX:]]))
        z[2 * p] = small[:, :C]
        z[2 * p + 1] = small[:, C:]
    every[...] = lanes(
        [
            z[:FRAMES, k * LOW : (k + 1) * LOW, :].reshape(FRAMES * LOW, C).astype(BF)
            for k in range(TAPS)
        ]
    )
    space = dot(base[...], every[...], ((0,), (0,)))
    halve(
        jnp.concatenate([space[:, k * C : (k + 1) * C] for k in range(TAPS)], axis=0),
        core,
        send,
        keep,
    )


def late_kernel(
    act, d2, extra, big, every, ws, direct, res, gt_send, gt_keep, low_send, low_keep
):
    core = lax.axis_index("tm")
    window = lanes([act[k * GROUP : (k + 1) * GROUP, :] for k in range(6)])
    outer = dot(window, lanes([d2[:GROUP, :], d2[GROUP:, :]]), ((0,), (0,)))
    grads = jnp.concatenate(
        [
            outer[t * C : (t + 1) * C, :C] + outer[(t + 1) * C : (t + 2) * C, C:]
            for t in range(5)
        ],
        axis=0,
    )
    halve(grads, core, gt_send, gt_keep)
    total = dot(every[...], lanes([ws[k] for k in range(TAPS)]), ((1,), (1,))) + direct[...]
    for f in range(FRAMES):
        upper = total[f * LOW : f * LOW + LCOLS, :]
        lower = total[f * LOW + LCOLS : (f + 1) * LOW, :]
        low_send[f] = jnp.where(core == 0, lower, upper)
        low_keep[f] = jnp.where(core == 0, upper, lower)
    res[...] = (big[...].astype(F32) + extra[...]).astype(BF)


def halve(grads, core, send, keep):
    rows = grads.shape[0] // 2
    send[...] = jnp.where(core == 0, grads[rows:], grads[:rows]).astype(send.dtype)
    keep[...] = jnp.where(core == 0, grads[:rows], grads[rows:])


def output_kernel(space_half, space_rest, time_half, time_rest, space, time):
    core = lax.axis_index("tm")
    for half, rest, out in ((space_half, space_rest, space), (time_half, time_rest, time)):
        rows = half.shape[0]
        out[:rows] = jnp.where(core == 0, half[...], rest[...]).astype(F32)
        out[rows:] = jnp.where(core == 0, rest[...], half[...]).astype(F32)


def full(pairs, total):
    sources, targets = {a for a, _ in pairs}, {b for _, b in pairs}
    return pairs + list(
        zip(
            [i for i in range(total) if i not in sources],
            [i for i in range(total) if i not in targets],
        )
    )


def hop_pairs(count, hop):
    pairs = []
    for s in range(count):
        pairs.append((2 * s, 2 * (s + hop)) if s + hop < count else (2 * s, 2 * s + 1))
        pairs.append((2 * s + 1, 2 * (s - hop) + 1) if s - hop >= 0 else (2 * s + 1, 2 * s))
    return pairs


def swap_pairs(count, first):
    pairs = []
    for i in range(first, count - 1, 2):
        pairs += [(i, i + 1), (i + 1, i)]
    return full(pairs, count)


def swap_cores(value):
    return lax.ppermute(value, "tm", [(0, 1), (1, 0)])


def reduce_chips(value, count, core, at, levels):
    bits = count.bit_length() - 1
    if count != 1 << bits:
        return lax.psum(value, "space").astype(BF)
    orders = [list(range(bits)), [(b + 2) % bits for b in range(bits)]] if bits > 2 else [list(range(bits))] * 2

    def pairs_of(step):
        pairs = []
        for s in range(count):
            for c in range(2):
                pairs.append((2 * s + c, 2 * (s ^ (1 << orders[c][step])) + c))
        return pairs

    def bit_of(step):
        return jnp.where(core == 0, (at >> orders[0][step]) & 1, (at >> orders[1][step]) & 1)

    levels = min(levels, bits)
    for step in range(levels):
        halves = value.reshape(2, value.shape[0] // 2, C)
        bit = bit_of(step)
        out = lax.dynamic_index_in_dim(halves, 1 - bit, 0, False).astype(BF)
        mine = lax.dynamic_index_in_dim(halves, bit, 0, False)
        value = mine + lax.ppermute(out, BOTH, pairs_of(step)).astype(F32)
    for step in range(levels, bits):
        out = value.astype(BF)
        value = out.astype(F32) + lax.ppermute(out, BOTH, pairs_of(step)).astype(F32)
    value = value.astype(BF)
    for step in reversed(range(levels)):
        got = lax.ppermute(value, BOTH, pairs_of(step))
        value = jnp.where(
            bit_of(step) == 0,
            jnp.concatenate([value, got], axis=0),
            jnp.concatenate([got, value], axis=0),
        )
    return value


def local(base_latent, cotangent, w_spatial, w_temporal):
    core = lax.axis_index("tm")
    at = lax.axis_index("space")
    count = lax.axis_size("space")
    up, conv, up_t, conv_t = constants()
    ws = w_spatial.reshape(TAPS, C, C)
    cot = cotangent.reshape(FRAMES * PIX, C)
    own = base_latent.reshape(FRAMES, LCOLS, C)
    other = swap_cores(own)
    base = jnp.where(
        core == 0, jnp.concatenate([own, other], axis=1), jnp.concatenate([other, own], axis=1)
    ).reshape(FRAMES * LOW, C)
    even, odd = (lax.ppermute(cot, "space", swap_pairs(count, first)) for first in (0, 1))
    near = jnp.concatenate(
        [lax.ppermute(base, BOTH, hop_pairs(count, hop)) for hop in (1, 2)], axis=0
    )

    shape = jax.ShapeDtypeStruct
    n_own = FRAMES * PIX
    params = pltpu.CompilerParams(vmem_limit_bytes=32 << 20)
    vmem = pl.BlockSpec(memory_space=pltpu.VMEM)
    hbm = pl.BlockSpec(memory_space=pltpu.HBM)
    cost = lambda flops: pl.CostEstimate(flops=flops, bytes_accessed=2 << 20, transcendentals=0)
    ws_v, cot_v, conv_v, conv_t_v, time, time_t, big, direct, act, slope1 = pl.pallas_call(
        prepare_kernel,
        in_specs=[vmem] + [hbm] * 7,
        out_shape=(
            shape((TAPS, C, C), BF),
            shape((n_own, C), BF),
            shape((PIX, LT), BF),
            shape((LT, PIX), BF),
            shape((6 * C, 2 * C), BF),
            shape((2 * C, 6 * C), BF),
            shape((n_own, C), BF),
            shape((FRAMES * LOW, C), F32),
            shape((n_own, C), BF),
            shape((n_own, C), F32),
        ),
        scratch_shapes=[
            pltpu.VMEM((PIX, LOW), BF),
            pltpu.VMEM((LOW, PIX), BF),
            pltpu.VMEM((5, C, C), BF),
            pltpu.VMEM((FRAMES, LT, C), F32),
            pltpu.SemaphoreType.DMA((7,)),
        ],
        compiler_params=params,
        cost_estimate=cost(1 << 29),
        name="prepare",
    )(base, *(pltpu.with_memory_space_constraint(x, pltpu.HBM) for x in (cot, conv, conv_t, up, up_t, ws, w_temporal)))
    near, even, cot_v = lax.optimization_barrier((near, even, cot_v))
    far = swap_cores(near)
    half_space = TAPS * C // 2
    half_time = 5 * C // 2
    send, keep, every, act_near, d2, extra = pl.pallas_call(
        main_kernel,
        out_shape=(
            shape((half_space, C), BF),
            shape((half_space, C), F32),
            shape((FRAMES * LOW, TAPS * C), BF),
            shape((6 * GROUP, C), BF),
            shape((n_own, C), BF),
            shape((n_own, C), F32),
        ),
        scratch_shapes=[
            pltpu.VMEM((4 * FRAMES, LT, C), F32),
            pltpu.VMEM((5 * n_own, C), BF),
        ],
        compiler_params=params,
        cost_estimate=cost(1 << 30),
        name="main",
    )(near, far, even, odd, ws_v, conv_v, conv_t_v, act, slope1, time, time_t, cot_v, base)
    res, gt_send, gt_keep, low_send, low_keep = pl.pallas_call(
        late_kernel,
        out_shape=(
            shape((n_own, C), BF),
            shape((half_time, C), BF),
            shape((half_time, C), F32),
            shape((FRAMES, LCOLS, C), F32),
            shape((FRAMES, LCOLS, C), F32),
        ),
        compiler_params=params,
        cost_estimate=cost(1 << 29),
        name="late",
    )(act_near, d2, extra, big, every, ws_v, direct)

    grad_base = low_keep + swap_cores(low_send)
    halves = []
    for out, mine, levels in ((gt_send, gt_keep, 0), (send, keep, 1)):
        halves.append(reduce_chips(mine + swap_cores(out).astype(F32), count, core, at, levels))
    time_half, space_half = halves
    grad_spatial, grad_temporal = pl.pallas_call(
        output_kernel,
        out_shape=(shape((TAPS * C, C), F32), shape((5 * C, C), F32)),
        compiler_params=params,
        name="output",
    )(space_half, swap_cores(space_half), time_half, swap_cores(time_half))
    return (
        res.reshape(cotangent.shape),
        grad_base.reshape(base_latent.shape),
        grad_spatial.reshape(3, 3, C, C),
        grad_temporal.reshape(5, C, C),
    )


def solution(mesh):
    rows = P(("groups", "space"), "tm", None, None)
    return jax.shard_map(
        local,
        mesh=mesh,
        in_specs=(rows, rows, P(), P()),
        out_specs=(rows, rows, P("groups", None, None, None), P("groups", None, None)),
        check_vma=False,
    )
```

time: 49.6 us -> 41.2 us (0.83)
  the two profiles are of different devices: /device:TPU:31 before, /device:TPU:0 now
where the time goes in v2:
time: 41.2 us; the launch traced here: 40.9 us
  starting transfers between devices  24.9 us (60%)
  waiting for transfers between devices  7.67 us (19%)
  Pallas kernels  5.83 us (14%)
  other arithmetic  1.05 us (3%)
  between operations  0.75 us (2%)
  local copies, waits for them, and re-layouts  0.66 us (2%)
    ppermute x5, starting transfers between devices, reduce_chips(): lax.ppermute(out, BOTH, pairs_of(step)).astype(F32)  9.18 us
    ppermute x2, starting transfers between devices, local(): lax.ppermute(base, BOTH, hop_pairs(count, hop))  5.02 us
    ppermute x2, starting transfers between devices, local(): lax.ppermute(cot, 'space', swap_pairs(count, first))  4.14 us
    ppermute x1, starting transfers between devices, reduce_chips(): value = mine + lax.ppermute(out, BOTH, pairs_of(step)).astype(F32)  2.55 us
    ppermute x5, waiting for transfers between devices, reduce_chips(): lax.ppermute(out, BOTH, pairs_of(step)).astype(F32)  2.37 us
    ppermute x7, starting transfers between devices, swap_cores(): return lax.ppermute(value, 'tm', [(0, 1), (1, 0)])  2.21 us
    pallas_call x1, Pallas kernels, local(): pl.pallas_call(main_kernel, out_shape=(shape((half_space, C), BF), shape(...  1.95 us
    ppermute x1, starting transfers between devices, reduce_chips(): got = lax.ppermute(value, BOTH, pairs_of(step))  1.85 us
  transfers between devices with their start and end apart: 18, of which 9 were waited for; matrix products, arithmetic and copies ran while one was open for 4% of the time, Pallas kernels for 7%

profile of v2, /device:TPU:0, one launch (start us, length us, event | category | flops | bytes accessed | tf_op | source)
XLA Modules:
  0.0 40.9 jit_solution(11364158936615705377)
XLA Ops:
  0.6 0.5 %collective-permute-start = (bf16[4,12,128]{2,0,1:T(4,128)(2,1)}, bf16[4,12,128]{2,0,1:T(4,128)(2,1)S(1)}, u32[]{:S(2)}, u32[]{:S(2)}) collective-permute-start(bf16[4,12,128]{2,0,1:T(4,128)(2,1)} %bitcast.22), channel_id=1, source_target_pairs={{0,1},{1,0},{2,3},{3,2},{4,5},{5,4},{6,7},{7,6},{8,9},{9,8},{10,11... | collective-permute-start | bytes 36872 | tf_op jit(solution)/shard_map/ppermute | solution.py:273
  1.1 2.6 %collective-permute-start.3 = (bf16[768,128]{1,0:T(8,128)(2,1)}, bf16[768,128]{1,0:T(8,128)(2,1)S(1)}, u32[]{:S(2)}, u32[]{:S(2)}) collective-permute-start(bf16[768,128]{1,0:T(8,128)(2,1)} %bitcast.27), channel_id=1, source_target_pairs={{0,2},{2,0},{4,6},{6,4},{8,10},{10,8},{12,14},{14,12},{1,3},{3,1},... | collective-permute-start | bytes 589832 | tf_op jit(solution)/shard_map/ppermute | solution.py:325
  3.7 1.6 %collective-permute-start.5 = (bf16[768,128]{1,0:T(8,128)(2,1)}, bf16[768,128]{1,0:T(8,128)(2,1)S(1)}, u32[]{:S(2)}, u32[]{:S(2)}) collective-permute-start(bf16[768,128]{1,0:T(8,128)(2,1)} %bitcast.28), channel_id=1, source_target_pairs={{2,4},{4,2},{6,8},{8,6},{10,12},{12,10},{0,0},{14,14},{3,5},{5,3},... | collective-permute-start | bytes 589832 | tf_op jit(solution)/shard_map/ppermute | solution.py:325
  5.3 0.0 collective-permute-done
  5.3 0.8 %maximum_select_fusion.1 = bf16[4,24,128]{2,0,1:T(4,128)(2,1)S(1)} fusion(bf16[4,12,128]{2,0,1:T(4,128)(2,1)S(1)} %collective-permute-done, bf16[4,12,128]{2,0,1:T(4,128)(2,1)} %bitcast.23, pred[]{:T(512)S(6)} %eq.8), kind=kLoop, calls=%fused_computation.14 | loop fusion | flops 36864 | bytes 49153 | tf_op jit(solution)/shard_map/jit(_where)/select_n | solution.py:322
  6.1 3.4 %collective-permute-start.1 = (bf16[96,128]{1,0:T(8,128)(2,1)S(1)}, bf16[96,128]{1,0:T(8,128)(2,1)S(1)}, u32[]{:S(2)}, u32[]{:S(2)}) collective-permute-start(bf16[96,128]{1,0:T(8,128)(2,1)S(1)} %bitcast.16), channel_id=1, source_target_pairs={{0,2},{1,0},{2,4},{3,1},{4,6},{5,3},{6,8},{7,5},{8,10},{9,7},{10,1... | collective-permute-start | bytes 73736 | tf_op jit(solution)/shard_map/ppermute | solution.py:327
  9.6 1.6 %collective-permute-start.2 = (bf16[96,128]{1,0:T(8,128)(2,1)S(1)}, bf16[96,128]{1,0:T(8,128)(2,1)S(1)}, u32[]{:S(2)}, u32[]{:S(2)}) collective-permute-start(bf16[96,128]{1,0:T(8,128)(2,1)S(1)} %bitcast.17), channel_id=1, source_target_pairs={{0,4},{1,0},{2,6},{3,2},{4,8},{5,1},{6,10},{7,3},{8,12},{9,5},{10,... | collective-permute-start | bytes 73736 | tf_op jit(solution)/shard_map/ppermute | solution.py:327
  11.1 1.7 %prepare.1 = (bf16[9,128,128]{2,1,0:T(8,128)(2,1)S(1)}, bf16[768,128]{1,0:T(8,128)(2,1)S(1)}, bf16[192,216]{1,0:T(8,128)(2,1)S(1)}, bf16[216,192]{1,0:T(8,128)(2...) custom-call(bf16[96,128]{1,0:T(8,128)(2,1)S(1)} %bitcast.18, ...), custom_call_target="tpu_custom_call" | custom-call | flops 536870912 | bytes 2097152 | tf_op jit(solution)/shard_map/prepare/pallas_call | solution.py:336
  12.9 0.6 %collective-permute-done.1 = bf16[96,128]{1,0:T(8,128)(2,1)S(1)} collective-permute-done((bf16[96,128]{1,0:T(8,128)(2,1)S(1)}, bf16[96,128]{1,0:T(8,128)(2,1)S(1)}, u32[]{:S(2)}, u32[]{:S(2)}) %collective-permute-start.1) | collective-permute-done | bytes 24608 | tf_op jit(solution)/shard_map/ppermute | solution.py:327
  13.4 0.0 collective-permute-done.2
  13.4 0.0 collective-permute-done.3.even
  13.4 0.1 collective-permute-start.4
  13.5 0.0 collective-permute-done.5.odd
  13.5 1.2 %collective-permute-done.4.far = bf16[192,128]{1,0:T(8,128)(2,1)S(1)} collective-permute-done((bf16[192,128]{1,0:T(8,128)(2,1)S(1)}, bf16[192,128]{1,0:T(8,128)(2,1)S(1)}, u32[]{:S(2)}, u32[]{:S(2)}) %collective-permute-start.4) | collective-permute-done | bytes 49184 | tf_op jit(solution)/shard_map/ppermute | solution.py:273
  14.7 1.9 %main.1 = (bf16[576,128]{1,0:T(8,128)(2,1)S(1)}, f32[576,128]{1,0:T(8,128)S(1)}, bf16[96,1152]{1,0:T(8,128)(2,1)S(1)}, bf16[2304,128]{1,0:T(8,128)(2,1)S(1)}, bf...) custom-call(bf16[192,128]{1,0:T(8,128)(2,1)S(1)} %pad_maximum_fusion.near, ...), custom_call_target="tpu_custom_call" | custom-call | flops 1073741824 | bytes 2097152 | tf_op jit(solution)/shard_map/main/pallas_call | solution.py:366
  16.7 0.2 collective-permute-start.7
  16.9 1.2 %late.1 = (bf16[768,128]{1,0:T(8,128)(2,1)}, bf16[320,128]{1,0:T(8,128)(2,1)S(1)}, f32[320,128]{1,0:T(8,128)S(1)}, f32[4,12,128]{2,1,0:T(8,128)S(1)}, f32[4,12,128]{2,1,0:T(8,128)S(1)}) custom-call(bf16[2304,128]{1,0:T(8,128)(2,1)S(1)} %get-tuple-element.41.act, bf16[768,128]{1,0:T(8,128)(2,1)S(1)} %get-tuple-element.42.d2, ...), custom_call_target="tpu_custom_call" | custom-call | flops 536870912 | bytes 2097152 | tf_op jit(solution)/shard_map/late/pallas_call | solution.py:384
  18.1 0.3 collective-permute-start.13
  18.4 0.2 collective-permute-start.6
  18.6 0.0 collective-permute-done.7
  18.7 2.5 %collective-permute-start.8 = (bf16[288,128]{1,0:T(8,128)(2,1)S(1)}, bf16[288,128]{1,0:T(8,128)(2,1)S(1)}, u32[]{:S(2)}, u32[]{:S(2)}) collective-permute-start(bf16[288,128]{1,0:T(8,128)(2,1)S(1)} %fusion.1), channel_id=1, source_target_pairs={{0,2},{1,9},{2,0},{3,11},{4,6},{5,13},{6,4},{7,15},{8,10},{9,1},{1... | collective-permute-start | bytes 221192 | tf_op jit(solution)/shard_map/ppermute | solution.py:298
  21.2 0.0 collective-permute-done.13
  21.2 0.7 %collective-permute-start.14 = (bf16[320,128]{1,0:T(8,128)(2,1)S(1)}, bf16[320,128]{1,0:T(8,128)(2,1)S(1)}, u32[]{:S(2)}, u32[]{:S(2)}) collective-permute-start(bf16[320,128]{1,0:T(8,128)(2,1)S(1)} %add_convert_fusion.3), channel_id=1, source_target_pairs={{0,2},{1,9},{2,0},{3,11},{4,6},{5,13},{6,4},{7,15},{8,10},{9,1},{1... | collective-permute-start | bytes 245768 | tf_op jit(solution)/shard_map/ppermute | solution.py:301
  21.9 1.6 %collective-permute-done.8 = bf16[288,128]{1,0:T(8,128)(2,1)S(1)} collective-permute-done((bf16[288,128]{1,0:T(8,128)(2,1)S(1)}, bf16[288,128]{1,0:T(8,128)(2,1)S(1)}, u32[]{:S(2)}, u32[]{:S(2)}) %collective-permute-start.8) | collective-permute-done | bytes 73760 | tf_op jit(solution)/shard_map/ppermute | solution.py:298
  23.6 1.9 %collective-permute-start.9 = (bf16[288,128]{1,0:T(8,128)(2,1)S(1)}, bf16[288,128]{1,0:T(8,128)(2,1)S(1)}, u32[]{:S(2)}, u32[]{:S(2)}) collective-permute-start(bf16[288,128]{1,0:T(8,128)(2,1)S(1)} %fusion), channel_id=1, source_target_pairs={{0,4},{1,3},{2,6},{3,1},{4,0},{5,7},{6,2},{7,5},{8,12},{9,11},{10,... | collective-permute-start | bytes 221192 | tf_op jit(solution)/shard_map/ppermute | solution.py:301
  25.5 0.3 collective-permute-done.14
  25.8 1.6 %collective-permute-start.15 = (bf16[320,128]{1,0:T(8,128)(2,1)S(1)}, bf16[320,128]{1,0:T(8,128)(2,1)S(1)}, u32[]{:S(2)}, u32[]{:S(2)}) collective-permute-start(bf16[320,128]{1,0:T(8,128)(2,1)S(1)} %add_convert_fusion.2), channel_id=1, source_target_pairs={{0,4},{1,3},{2,6},{3,1},{4,0},{5,7},{6,2},{7,5},{8,12},{9,11},{10,... | collective-permute-start | bytes 245768 | tf_op jit(solution)/shard_map/ppermute | solution.py:301
  27.4 0.6 %collective-permute-done.9 = bf16[288,128]{1,0:T(8,128)(2,1)S(1)} collective-permute-done((bf16[288,128]{1,0:T(8,128)(2,1)S(1)}, bf16[288,128]{1,0:T(8,128)(2,1)S(1)}, u32[]{:S(2)}, u32[]{:S(2)}) %collective-permute-start.9) | collective-permute-done | bytes 73760 | tf_op jit(solution)/shard_map/ppermute | solution.py:301
  28.0 2.9 %collective-permute-start.10 = (bf16[288,128]{1,0:T(8,128)(2,1)S(1)}, bf16[288,128]{1,0:T(8,128)(2,1)S(1)}, u32[]{:S(2)}, u32[]{:S(2)}) collective-permute-start(bf16[288,128]{1,0:T(8,128)(2,1)S(1)} %add_convert_fusion.5), channel_id=1, source_target_pairs={{0,8},{1,5},{2,10},{3,7},{4,12},{5,1},{6,14},{7,3},{8,0},{9,13},{1... | collective-permute-start | bytes 221192 | tf_op jit(solution)/shard_map/ppermute | solution.py:301
  30.9 0.0 collective-permute-done.15
  31.0 2.0 %collective-permute-start.16 = (bf16[320,128]{1,0:T(8,128)(2,1)S(1)}, bf16[320,128]{1,0:T(8,128)(2,1)S(1)}, u32[]{:S(2)}, u32[]{:S(2)}) collective-permute-start(bf16[320,128]{1,0:T(8,128)(2,1)S(1)} %add_convert_fusion.1), channel_id=1, source_target_pairs={{0,8},{1,5},{2,10},{3,7},{4,12},{5,1},{6,14},{7,3},{8,0},{9,13},{1... | collective-permute-start | bytes 245768 | tf_op jit(solution)/shard_map/ppermute | solution.py:301
  33.0 0.6 %collective-permute-done.10 = bf16[288,128]{1,0:T(8,128)(2,1)S(1)} collective-permute-done((bf16[288,128]{1,0:T(8,128)(2,1)S(1)}, bf16[288,128]{1,0:T(8,128)(2,1)S(1)}, u32[]{:S(2)}, u32[]{:S(2)}) %collective-permute-start.10) | collective-permute-done | bytes 73760 | tf_op jit(solution)/shard_map/ppermute | solution.py:301
  33.6 1.8 %collective-permute-start.11 = (bf16[288,128]{1,0:T(8,128)(2,1)S(1)}, bf16[288,128]{1,0:T(8,128)(2,1)S(1)}, u32[]{:S(2)}, u32[]{:S(2)}) collective-permute-start(bf16[288,128]{1,0:T(8,128)(2,1)S(1)} %add_convert_fusion.4), channel_id=1, source_target_pairs={{0,2},{1,9},{2,0},{3,11},{4,6},{5,13},{6,4},{7,15},{8,10},{9,1},{1... | collective-permute-start | bytes 221192 | tf_op jit(solution)/shard_map/ppermute | solution.py:304
  35.5 0.9 %collective-permute-done.16 = bf16[320,128]{1,0:T(8,128)(2,1)S(1)} collective-permute-done((bf16[320,128]{1,0:T(8,128)(2,1)S(1)}, bf16[320,128]{1,0:T(8,128)(2,1)S(1)}, u32[]{:S(2)}, u32[]{:S(2)}) %collective-permute-start.16) | collective-permute-done | bytes 81952 | tf_op jit(solution)/shard_map/ppermute | solution.py:301
  36.4 0.1 collective-permute-start.17
  36.5 1.6 %collective-permute-done.11 = bf16[288,128]{1,0:T(8,128)(2,1)S(1)} collective-permute-done((bf16[288,128]{1,0:T(8,128)(2,1)S(1)}, bf16[288,128]{1,0:T(8,128)(2,1)S(1)}, u32[]{:S(2)}, u32[]{:S(2)}) %collective-permute-start.11) | collective-permute-done | bytes 73760 | tf_op jit(solution)/shard_map/ppermute | solution.py:304
  38.1 0.8 %collective-permute-start.12 = (bf16[576,128]{1,0:T(8,128)(2,1)S(1)}, bf16[576,128]{1,0:T(8,128)(2,1)S(1)}, u32[]{:S(2)}, u32[]{:S(2)}) collective-permute-start(bf16[576,128]{1,0:T(8,128)(2,1)S(1)} %maximum_select_fusion.space_half), channel_id=1, source_target_pairs={{0,1},{1,0},{2,3},{3,2},{4,5},{5,4},{6,7},{7,6},{8,9},{9,8},{10,11... | collective-permute-start | bytes 442376 | tf_op jit(solution)/shard_map/ppermute | solution.py:273
  38.9 0.0 collective-permute-done.6
  38.9 0.6 %copy.13 = f32[4,1,12,128]{3,1,2,0:T(1,128)} copy(f32[4,1,12,128]{3,2,0,1:T(8,128)S(1)} %add_bitcast_fusion) | data formatting | bytes 49152
  39.5 0.0 collective-permute-done.17.time_rest
  39.5 0.4 collective-permute-done.12.space_rest
  39.9 1.0 %output.1 = (f32[1152,128]{1,0:T(8,128)}, f32[640,128]{1,0:T(8,128)}) custom-call(bf16[576,128]{1,0:T(8,128)(2,1)S(1)} %maximum_select_fusion.space_half, bf16[576,128]{1,0:T(8,128)(2,1)S(1)} %collective-permute-done.12.space_rest, bf16[320,128]{1,0:T(8,128)(2,1)S(1)} %add_convert_fusion.time_half, bf16[320,128]{1,0:T(8,128)(2,1)S(1)} %collective-permute-done.17.time_rest), custom_call_target="tpu_custom_call" | custom-call | tf_op jit(solution)/shard_map/output/pallas_call | solution.py:403
  (13 shorter events, 0.3 us)
Async XLA Ops:
  0.6 4.7 %collective-permute-start = (bf16[4,12,128]{2,0,1:T(4,128)(2,1)}, bf16[4,12,128]{2,0,1:T(4,128)(2,1)S(1)}, u32[]{:S(2)}, u32[]{:S(2)}) collective-permute-start(bf16[4,12,128]{2,0,1:T(4,128)(2,1)} %bitcast.22), channel_id=1, source_target_pairs={{0,1},{1,0},{2,3},{3,2},{4,5},{5,4},{6,7},{7,6},{8,9},{9,8},{10,11... | collective-permute-start | bytes 36872 | tf_op jit(solution)/shard_map/ppermute | solution.py:273
  1.1 12.3 %collective-permute-start.3 = (bf16[768,128]{1,0:T(8,128)(2,1)}, bf16[768,128]{1,0:T(8,128)(2,1)S(1)}, u32[]{:S(2)}, u32[]{:S(2)}) collective-permute-start(bf16[768,128]{1,0:T(8,128)(2,1)} %bitcast.27), channel_id=1, source_target_pairs={{0,2},{2,0},{4,6},{6,4},{8,10},{10,8},{12,14},{14,12},{1,3},{3,1},... | collective-permute-start | bytes 589832 | tf_op jit(solution)/shard_map/ppermute | solution.py:325
  3.7 9.8 %collective-permute-start.5 = (bf16[768,128]{1,0:T(8,128)(2,1)}, bf16[768,128]{1,0:T(8,128)(2,1)S(1)}, u32[]{:S(2)}, u32[]{:S(2)}) collective-permute-start(bf16[768,128]{1,0:T(8,128)(2,1)} %bitcast.28), channel_id=1, source_target_pairs={{2,4},{4,2},{6,8},{8,6},{10,12},{12,10},{0,0},{14,14},{3,5},{5,3},... | collective-permute-start | bytes 589832 | tf_op jit(solution)/shard_map/ppermute | solution.py:325
  6.1 7.3 %collective-permute-start.1 = (bf16[96,128]{1,0:T(8,128)(2,1)S(1)}, bf16[96,128]{1,0:T(8,128)(2,1)S(1)}, u32[]{:S(2)}, u32[]{:S(2)}) collective-permute-start(bf16[96,128]{1,0:T(8,128)(2,1)S(1)} %bitcast.16), channel_id=1, source_target_pairs={{0,2},{1,0},{2,4},{3,1},{4,6},{5,3},{6,8},{7,5},{8,10},{9,7},{10,1... | collective-permute-start | bytes 73736 | tf_op jit(solution)/shard_map/ppermute | solution.py:327
  9.6 3.9 %collective-permute-start.2 = (bf16[96,128]{1,0:T(8,128)(2,1)S(1)}, bf16[96,128]{1,0:T(8,128)(2,1)S(1)}, u32[]{:S(2)}, u32[]{:S(2)}) collective-permute-start(bf16[96,128]{1,0:T(8,128)(2,1)S(1)} %bitcast.17), channel_id=1, source_target_pairs={{0,4},{1,0},{2,6},{3,2},{4,8},{5,1},{6,10},{7,3},{8,12},{9,5},{10,... | collective-permute-start | bytes 73736 | tf_op jit(solution)/shard_map/ppermute | solution.py:327
  13.4 1.3 %collective-permute-start.4 = (bf16[192,128]{1,0:T(8,128)(2,1)S(1)}, bf16[192,128]{1,0:T(8,128)(2,1)S(1)}, u32[]{:S(2)}, u32[]{:S(2)}) collective-permute-start(bf16[192,128]{1,0:T(8,128)(2,1)S(1)} %pad_maximum_fusion.near), channel_id=1, source_target_pairs={{0,1},{1,0},{2,3},{3,2},{4,5},{5,4},{6,7},{7,6},{8,9},{9,8},{10,11... | collective-permute-start | bytes 147464 | tf_op jit(solution)/shard_map/ppermute | solution.py:273
  16.7 1.9 %collective-permute-start.7 = (bf16[576,128]{1,0:T(8,128)(2,1)S(1)}, bf16[576,128]{1,0:T(8,128)(2,1)S(1)}, u32[]{:S(2)}, u32[]{:S(2)}) collective-permute-start(bf16[576,128]{1,0:T(8,128)(2,1)S(1)} %get-tuple-element.51), channel_id=1, source_target_pairs={{0,1},{1,0},{2,3},{3,2},{4,5},{5,4},{6,7},{7,6},{8,9},{9,8},{10,11... | collective-permute-start | bytes 442376 | tf_op jit(solution)/shard_map/ppermute | solution.py:273
  18.1 3.1 %collective-permute-start.13 = (bf16[320,128]{1,0:T(8,128)(2,1)S(1)}, bf16[320,128]{1,0:T(8,128)(2,1)S(1)}, u32[]{:S(2)}, u32[]{:S(2)}) collective-permute-start(bf16[320,128]{1,0:T(8,128)(2,1)S(1)} %get-tuple-element.53), channel_id=1, source_target_pairs={{0,1},{1,0},{2,3},{3,2},{4,5},{5,4},{6,7},{7,6},{8,9},{9,8},{10,11... | collective-permute-start | bytes 245768 | tf_op jit(solution)/shard_map/ppermute | solution.py:273
  18.4 20.5 %collective-permute-start.6 = (f32[4,12,128]{2,1,0:T(8,128)S(1)}, f32[4,12,128]{2,1,0:T(8,128)S(1)}, u32[]{:S(2)}, u32[]{:S(2)}) collective-permute-start(f32[4,12,128]{2,1,0:T(8,128)S(1)} %get-tuple-element.49), channel_id=1, source_target_pairs={{0,1},{1,0},{2,3},{3,2},{4,5},{5,4},{6,7},{7,6},{8,9},{9,8},{10,11... | collective-permute-start | bytes 73736 | tf_op jit(solution)/shard_map/ppermute | solution.py:273
  18.7 4.9 %collective-permute-start.8 = (bf16[288,128]{1,0:T(8,128)(2,1)S(1)}, bf16[288,128]{1,0:T(8,128)(2,1)S(1)}, u32[]{:S(2)}, u32[]{:S(2)}) collective-permute-start(bf16[288,128]{1,0:T(8,128)(2,1)S(1)} %fusion.1), channel_id=1, source_target_pairs={{0,2},{1,9},{2,0},{3,11},{4,6},{5,13},{6,4},{7,15},{8,10},{9,1},{1... | collective-permute-start | bytes 221192 | tf_op jit(solution)/shard_map/ppermute | solution.py:298
  21.2 4.5 %collective-permute-start.14 = (bf16[320,128]{1,0:T(8,128)(2,1)S(1)}, bf16[320,128]{1,0:T(8,128)(2,1)S(1)}, u32[]{:S(2)}, u32[]{:S(2)}) collective-permute-start(bf16[320,128]{1,0:T(8,128)(2,1)S(1)} %add_convert_fusion.3), channel_id=1, source_target_pairs={{0,2},{1,9},{2,0},{3,11},{4,6},{5,13},{6,4},{7,15},{8,10},{9,1},{1... | collective-permute-start | bytes 245768 | tf_op jit(solution)/shard_map/ppermute | solution.py:301
  23.6 4.4 %collective-permute-start.9 = (bf16[288,128]{1,0:T(8,128)(2,1)S(1)}, bf16[288,128]{1,0:T(8,128)(2,1)S(1)}, u32[]{:S(2)}, u32[]{:S(2)}) collective-permute-start(bf16[288,128]{1,0:T(8,128)(2,1)S(1)} %fusion), channel_id=1, source_target_pairs={{0,4},{1,3},{2,6},{3,1},{4,0},{5,7},{6,2},{7,5},{8,12},{9,11},{10,... | collective-permute-start | bytes 221192 | tf_op jit(solution)/shard_map/ppermute | solution.py:301
  25.8 5.2 %collective-permute-start.15 = (bf16[320,128]{1,0:T(8,128)(2,1)S(1)}, bf16[320,128]{1,0:T(8,128)(2,1)S(1)}, u32[]{:S(2)}, u32[]{:S(2)}) collective-permute-start(bf16[320,128]{1,0:T(8,128)(2,1)S(1)} %add_convert_fusion.2), channel_id=1, source_target_pairs={{0,4},{1,3},{2,6},{3,1},{4,0},{5,7},{6,2},{7,5},{8,12},{9,11},{10,... | collective-permute-start | bytes 245768 | tf_op jit(solution)/shard_map/ppermute | solution.py:301
  28.0 5.6 %collective-permute-start.10 = (bf16[288,128]{1,0:T(8,128)(2,1)S(1)}, bf16[288,128]{1,0:T(8,128)(2,1)S(1)}, u32[]{:S(2)}, u32[]{:S(2)}) collective-permute-start(bf16[288,128]{1,0:T(8,128)(2,1)S(1)} %add_convert_fusion.5), channel_id=1, source_target_pairs={{0,8},{1,5},{2,10},{3,7},{4,12},{5,1},{6,14},{7,3},{8,0},{9,13},{1... | collective-permute-start | bytes 221192 | tf_op jit(solution)/shard_map/ppermute | solution.py:301
  31.0 5.4 %collective-permute-start.16 = (bf16[320,128]{1,0:T(8,128)(2,1)S(1)}, bf16[320,128]{1,0:T(8,128)(2,1)S(1)}, u32[]{:S(2)}, u32[]{:S(2)}) collective-permute-start(bf16[320,128]{1,0:T(8,128)(2,1)S(1)} %add_convert_fusion.1), channel_id=1, source_target_pairs={{0,8},{1,5},{2,10},{3,7},{4,12},{5,1},{6,14},{7,3},{8,0},{9,13},{1... | collective-permute-start | bytes 245768 | tf_op jit(solution)/shard_map/ppermute | solution.py:301
  33.6 4.4 %collective-permute-start.11 = (bf16[288,128]{1,0:T(8,128)(2,1)S(1)}, bf16[288,128]{1,0:T(8,128)(2,1)S(1)}, u32[]{:S(2)}, u32[]{:S(2)}) collective-permute-start(bf16[288,128]{1,0:T(8,128)(2,1)S(1)} %add_convert_fusion.4), channel_id=1, source_target_pairs={{0,2},{1,9},{2,0},{3,11},{4,6},{5,13},{6,4},{7,15},{8,10},{9,1},{1... | collective-permute-start | bytes 221192 | tf_op jit(solution)/shard_map/ppermute | solution.py:304
  36.4 3.1 %collective-permute-start.17 = (bf16[320,128]{1,0:T(8,128)(2,1)S(1)}, bf16[320,128]{1,0:T(8,128)(2,1)S(1)}, u32[]{:S(2)}, u32[]{:S(2)}) collective-permute-start(bf16[320,128]{1,0:T(8,128)(2,1)S(1)} %add_convert_fusion.time_half), channel_id=1, source_target_pairs={{0,1},{1,0},{2,3},{3,2},{4,5},{5,4},{6,7},{7,6},{8,9},{9,8},{10,11... | collective-permute-start | bytes 245768 | tf_op jit(solution)/shard_map/ppermute | solution.py:273
  38.1 1.8 %collective-permute-start.12 = (bf16[576,128]{1,0:T(8,128)(2,1)S(1)}, bf16[576,128]{1,0:T(8,128)(2,1)S(1)}, u32[]{:S(2)}, u32[]{:S(2)}) collective-permute-start(bf16[576,128]{1,0:T(8,128)(2,1)S(1)} %maximum_select_fusion.space_half), channel_id=1, source_target_pairs={{0,1},{1,0},{2,3},{3,2},{4,5},{5,4},{6,7},{7,6},{8,9},{9,8},{10,11... | collective-permute-start | bytes 442376 | tf_op jit(solution)/shard_map/ppermute | solution.py:273

commit v3 on v2

--- a/solution.py
+++ b/solution.py
@@ -20,6 +20,9 @@
 LT = TAPS * LOW
 GROUP = 2 * PIX
 BOTH = ("space", "tm")
+EXT = ROWS + 2
+WIDE = 3 * EXT * COLS
+DEEP = 12 * C
 
 
 def up_matrix(n):
@@ -42,12 +45,21 @@
 
 def constants():
     rows, cols = up_matrix(LROWS), up_matrix(LCOLS)
+    tall = np.pad(rows, ((1, 1), (0, 0)))
+    wide = np.stack(
+        [
+            np.concatenate(
+                [np.kron(tall[core * ROWS : core * ROWS + EXT], moved(cols, b)) for b in range(3)]
+            )
+            for core in range(2)
+        ]
+    )
     up = np.kron(rows, cols).reshape(2, PIX, LOW)
     conv = np.concatenate(
         [np.kron(moved(rows, a), moved(cols, b)) for a in range(3) for b in range(3)], axis=1
     ).reshape(2, PIX, LT)
     as_bf = lambda m: jnp.asarray(m, BF)
-    return as_bf(up), as_bf(conv), as_bf(up.transpose(0, 2, 1)), as_bf(conv.transpose(0, 2, 1))
+    return as_bf(wide), as_bf(up.transpose(0, 2, 1)), as_bf(conv.transpose(0, 2, 1))
 
 
 def dot(a, b, dims=((1,), (0,))):
@@ -59,9 +71,9 @@
 
 
 def prepare_kernel(
-    base, cot_h, conv_h, conv_t_h, up_h, up_t_h, ws_h, wt_h,
-    ws, cot, conv, conv_t, time, time_t, big, direct, act, slope1,
-    up, up_t, wt, z, sems,
+    base, cot_h, wide_h, conv_t_h, up_t_h, ws_h, wt_h,
+    ws, cot, wide, conv_t, deep, time, time_t, big, direct, act, slope1,
+    up_t, wt, u3, lhs, sems,
 ):
     core = lax.axis_index("tm")
     copies = [
@@ -69,8 +81,7 @@
         for i, (src, dst) in enumerate(
             (
                 (ws_h, ws),
-                (conv_h.at[core], conv),
-                (up_h.at[core], up),
+                (wide_h.at[core], wide),
                 (cot_h, cot),
                 (up_t_h.at[core], up_t),
                 (wt_h, wt),
@@ -80,26 +91,29 @@
     ]
     for copy in copies:
         copy.start()
-    for copy in copies[:3]:
+    for copy in copies[:2]:
         copy.wait()
-    low_res(base[...], ws, z)
-    for p in range(FRAMES // 2):
-        pre = dot(conv[...], lanes([z[2 * p], z[2 * p + 1]]).astype(BF))
-        sig = jax.nn.sigmoid(pre)
-        one = (pre * sig).astype(BF)
-        slope = sig * (1.0 + pre * (1.0 - sig))
-        for k in range(2):
-            lo = p * GROUP + k * PIX
-            act[lo : lo + PIX, :] = one[:, k * C : (k + 1) * C]
-            slope1[lo : lo + PIX, :] = slope[:, k * C : (k + 1) * C]
+    zero = jnp.zeros((C, C), BF)
+    for b in range(3):
+        for d in range(4):
+            here = slice((b * 4 + d) * C, (b * 4 + d + 1) * C)
+            deep[here, :C] = ws[3 * d + b] if d < 3 else zero
+            deep[here, C:] = ws[3 * (d - 1) + b] if d > 0 else zero
+    frames = [base[f * LOW : (f + 1) * LOW, :] for f in range(FRAMES)]
+    pre = conv_space(frames, wide, deep, u3, lhs)[0]
+    sig = jax.nn.sigmoid(pre)
+    one = (pre * sig).astype(BF)
+    slope = sig * (1.0 + pre * (1.0 - sig))
     for f in range(FRAMES):
-        big[f * PIX : (f + 1) * PIX, :] = dot(up[...], base[f * LOW : (f + 1) * LOW, :]).astype(BF)
-    for copy in copies[3:]:
+        here = slice(f * PIX, (f + 1) * PIX)
+        act[here, :] = image_order(one, f)
+        slope1[here, :] = image_order(slope, f)
+        big[here, :] = u3[f, (EXT + 1) * COLS : (EXT + 1) * COLS + PIX, :]
+    for copy in copies[2:]:
         copy.wait()
     both = dot(up_t[...], lanes([cot[f * PIX : (f + 1) * PIX, :] for f in range(FRAMES)]))
     for f in range(FRAMES):
         direct[f * LOW : (f + 1) * LOW, :] = both[:, f * C : (f + 1) * C]
-    zero = jnp.zeros((C, C), BF)
     for k in range(6):
         here = slice(k * C, (k + 1) * C)
         time[here, :C] = wt[k] if k < 5 else zero
@@ -108,20 +122,37 @@
         time_t[C:, here] = wt[5 - k] if k > 0 else zero
 
 
-def low_res(block, ws, z):
-    frames = block.shape[0] // LOW
-    for first in range(0, TAPS, 2):
-        taps = range(first, min(first + 2, TAPS))
-        prod = dot(block, lanes([ws[tap] for tap in taps]))
-        for k, tap in enumerate(taps):
-            z[:, tap * LOW : (tap + 1) * LOW, :] = prod[:, k * C : (k + 1) * C].reshape(
-                frames, LOW, C
-            )
+def conv_space(base_rows, wide, weights, u3, lhs):
+    count = len(base_rows)
+    for f in range(0, count, 2):
+        both = dot(wide[...], lanes(base_rows[f : f + 2])).astype(BF)
+        u3[f] = both[:, :C]
+        u3[f + 1] = both[:, C:]
+    for f in range(count):
+        for q in range(2):
+            to = (2 * f + q) * COLS
+            for b in range(3):
+                for d in range(4):
+                    frm = (b * EXT + 2 * q + d) * COLS
+                    block = b * 4 + d
+                    lhs[to : to + COLS, block * C : (block + 1) * C] = u3[f, frm : frm + COLS, :]
+    rows = count * PIX // 2
+    return [
+        dot(lhs[first : first + 2 * PIX, :], weights[...]) for first in range(0, rows, 2 * PIX)
+    ]
+
+
+def image_order(pairs, f):
+    out = []
+    for q in range(2):
+        here = slice((2 * f + q) * COLS, (2 * f + q + 1) * COLS)
+        out += [pairs[here, :C], pairs[here, C:]]
+    return jnp.concatenate(out, axis=0)
 
 
 def main_kernel(
-    near, far, even, odd, ws, conv, conv_t, act_own, slope1, time, time_t, cot, base,
-    send, keep, every, act_near, d2_own, extra, z, act,
+    near, far, even, odd, wide, deep, conv_t, act_own, slope1, time, time_t, cot, base,
+    send, keep, every, act_near, d2_own, extra, z, act, u3, lhs,
 ):
     core = lax.axis_index("tm")
     at = lax.axis_index("space")
@@ -130,28 +161,20 @@
     before = jnp.where(core == 0, near[...], far[...])
     after = jnp.where(core == 0, far[...], near[...])
     none = jnp.zeros((size, C), BF)
-    low_res(
-        jnp.concatenate(
-            [
-                jnp.where(at >= 2, before[size:], none),
-                jnp.where(at >= 1, before[:size], none),
-                jnp.where(at + 1 < count, after[:size], none),
-                jnp.where(at + 2 < count, after[size:], none),
-            ],
-            axis=0,
-        ),
-        ws,
-        z,
-    )
-    for p in range(2 * FRAMES):
-        group = p if p < FRAMES else p + FRAMES // 2
-        pre = dot(conv[...], lanes([z[2 * p], z[2 * p + 1]]).astype(BF))
+    blocks = (
+        jnp.where(at >= 2, before[size:], none),
+        jnp.where(at >= 1, before[:size], none),
+        jnp.where(at + 1 < count, after[:size], none),
+        jnp.where(at + 2 < count, after[size:], none),
+    )
+    frames = [block[f * LOW : (f + 1) * LOW] for block in blocks for f in range(FRAMES)]
+    for k, pre in enumerate(conv_space(frames, wide, deep, u3, lhs)):
         one = (pre * jax.nn.sigmoid(pre)).astype(BF)
-        for k in range(2):
-            part = one[:, k * C : (k + 1) * C]
-            lo = group * GROUP + k * PIX
+        for f in range(FRAMES):
+            part = image_order(one, f)
+            lo = (FRAMES * (k if k < 2 else k + 1) + f) * PIX
             act[lo : lo + PIX, :] = part
-            if 2 <= group < 8:
+            if 2 * GROUP <= lo < 8 * GROUP:
                 act_near[lo - 2 * GROUP : lo - 2 * GROUP + PIX, :] = part
     act_near[2 * GROUP : 4 * GROUP, :] = act_own[...]
 
@@ -277,7 +300,8 @@
     bits = count.bit_length() - 1
     if count != 1 << bits:
         return lax.psum(value, "space").astype(BF)
-    orders = [list(range(bits)), [(b + 2) % bits for b in range(bits)]] if bits > 2 else [list(range(bits))] * 2
+    plain = list(range(bits))
+    orders = [plain, plain[1::-1] + plain[2:] if levels else plain[-1:] + plain[:-1]]
 
     def pairs_of(step):
         pairs = []
@@ -314,7 +338,7 @@
     core = lax.axis_index("tm")
     at = lax.axis_index("space")
     count = lax.axis_size("space")
-    up, conv, up_t, conv_t = constants()
+    wide, up_t, conv_t = constants()
     ws = w_spatial.reshape(TAPS, C, C)
     cot = cotangent.reshape(FRAMES * PIX, C)
     own = base_latent.reshape(FRAMES, LCOLS, C)
@@ -333,14 +357,15 @@
     vmem = pl.BlockSpec(memory_space=pltpu.VMEM)
     hbm = pl.BlockSpec(memory_space=pltpu.HBM)
     cost = lambda flops: pl.CostEstimate(flops=flops, bytes_accessed=2 << 20, transcendentals=0)
-    ws_v, cot_v, conv_v, conv_t_v, time, time_t, big, direct, act, slope1 = pl.pallas_call(
+    ws_v, cot_v, wide_v, conv_t_v, deep, time, time_t, big, direct, act, slope1 = pl.pallas_call(
         prepare_kernel,
-        in_specs=[vmem] + [hbm] * 7,
+        in_specs=[vmem] + [hbm] * 6,
         out_shape=(
             shape((TAPS, C, C), BF),
             shape((n_own, C), BF),
-            shape((PIX, LT), BF),
+            shape((WIDE, LOW), BF),
             shape((LT, PIX), BF),
+            shape((DEEP, 2 * C), BF),
             shape((6 * C, 2 * C), BF),
             shape((2 * C, 6 * C), BF),
             shape((n_own, C), BF),
@@ -349,16 +374,16 @@
             shape((n_own, C), F32),
         ),
         scratch_shapes=[
-            pltpu.VMEM((PIX, LOW), BF),
             pltpu.VMEM((LOW, PIX), BF),
             pltpu.VMEM((5, C, C), BF),
-            pltpu.VMEM((FRAMES, LT, C), F32),
-            pltpu.SemaphoreType.DMA((7,)),
+            pltpu.VMEM((FRAMES, WIDE, C), BF),
+            pltpu.VMEM((FRAMES * PIX // 2, DEEP), BF),
+            pltpu.SemaphoreType.DMA((6,)),
         ],
         compiler_params=params,
         cost_estimate=cost(1 << 29),
         name="prepare",
-    )(base, *(pltpu.with_memory_space_constraint(x, pltpu.HBM) for x in (cot, conv, conv_t, up, up_t, ws, w_temporal)))
+    )(base, *(pltpu.with_memory_space_constraint(x, pltpu.HBM) for x in (cot, wide, conv_t, up_t, ws, w_temporal)))
     near, even, cot_v = lax.optimization_barrier((near, even, cot_v))
     far = swap_cores(near)
     half_space = TAPS * C // 2
@@ -374,13 +399,15 @@
             shape((n_own, C), F32),
         ),
         scratch_shapes=[
-            pltpu.VMEM((4 * FRAMES, LT, C), F32),
+            pltpu.VMEM((FRAMES, LT, C), F32),
             pltpu.VMEM((5 * n_own, C), BF),
+            pltpu.VMEM((4 * FRAMES, WIDE, C), BF),
+            pltpu.VMEM((4 * FRAMES * PIX // 2, DEEP), BF),
         ],
         compiler_params=params,
         cost_estimate=cost(1 << 30),
         name="main",
-    )(near, far, even, odd, ws_v, conv_v, conv_t_v, act, slope1, time, time_t, cot_v, base)
+    )(near, far, even, odd, wide_v, deep, conv_t_v, act, slope1, time, time_t, cot_v, base)
     res, gt_send, gt_keep, low_send, low_keep = pl.pallas_call(
         late_kernel,
         out_shape=(

time: 41.2 us -> 42.8 us (1.039)
  Pallas kernels: 5.83 us -> 8.43 us
  waiting for transfers between devices: 7.67 us -> 7.03 us
    pallas_call x1, Pallas kernels: 1.95 us -> 3.77 us  [local(): pl.pallas_call(main_kernel, out_shape=(shape((half_space, C), BF), shape(...]
    pallas_call x1, Pallas kernels: 1.73 us -> 2.5 us  [local(): pl.pallas_call(prepare_kernel, in_specs=[vmem] + [hbm] * 6, out_shape=(sh...]
    ppermute x7, starting transfers between devices: 2.21 us -> 1.47 us  [swap_cores(): return lax.ppermute(value, 'tm', [(0, 1), (1, 0)])]
    ppermute x5, starting transfers between devices: 9.18 us -> 9.77 us  [reduce_chips(): lax.ppermute(out, BOTH, pairs_of(step)).astype(F32)]
    ppermute x2, waiting for transfers between devices: 0.56 us -> 0.01 us  [local(): lax.ppermute(base, BOTH, hop_pairs(count, hop))]
    ppermute x5, waiting for transfers between devices: 2.37 us -> 1.87 us  [reduce_chips(): lax.ppermute(out, BOTH, pairs_of(step)).astype(F32)]
  transfers between devices with their start and end apart: 18 -> 18, of which waited for: 9 -> 8; matrix products, arithmetic and copies ran while one was open for 4% -> 4% of each run, Pallas kernels for 7% -> 9%
where the time goes in v3:
time: 42.8 us; the launch traced here: 42.5 us
  starting transfers between devices  24.5 us (57%)
  Pallas kernels  8.43 us (20%)
  waiting for transfers between devices  7.03 us (16%)
  other arithmetic  1.05 us (2%)
  between operations  0.79 us (2%)
  local copies, waits for them, and re-layouts  0.66 us (2%)
    ppermute x5, starting transfers between devices, reduce_chips(): lax.ppermute(out, BOTH, pairs_of(step)).astype(F32)  9.77 us
    ppermute x2, starting transfers between devices, local(): lax.ppermute(base, BOTH, hop_pairs(count, hop))  5.02 us
    ppermute x2, starting transfers between devices, local(): lax.ppermute(cot, 'space', swap_pairs(count, first))  4.14 us
    pallas_call x1, Pallas kernels, local(): pl.pallas_call(main_kernel, out_shape=(shape((half_space, C), BF), shape(...  3.77 us
    pallas_call x1, Pallas kernels, local(): pl.pallas_call(prepare_kernel, in_specs=[vmem] + [hbm] * 6, out_shape=(sh...  2.5 us
    ppermute x1, starting transfers between devices, reduce_chips(): value = mine + lax.ppermute(out, BOTH, pairs_of(step)).astype(F32)  2.31 us
    ppermute x7, waiting for transfers between devices, swap_cores(): return lax.ppermute(value, 'tm', [(0, 1), (1, 0)])  1.91 us
    ppermute x5, waiting for transfers between devices, reduce_chips(): lax.ppermute(out, BOTH, pairs_of(step)).astype(F32)  1.87 us
  transfers between devices with their start and end apart: 18, of which 8 were waited for; matrix products, arithmetic and copies ran while one was open for 4% of the time, Pallas kernels for 9%

profile of v3, /device:TPU:0, one launch (start us, length us, event | category | flops | bytes accessed | tf_op | source)
XLA Modules:
  0.0 42.5 jit_solution(3212923789522783346)
XLA Ops:
  0.6 0.5 %collective-permute-start = (bf16[4,12,128]{2,0,1:T(4,128)(2,1)}, bf16[4,12,128]{2,0,1:T(4,128)(2,1)S(1)}, u32[]{:S(2)}, u32[]{:S(2)}) collective-permute-start(bf16[4,12,128]{2,0,1:T(4,128)(2,1)} %bitcast.22), channel_id=1, source_target_pairs={{0,1},{1,0},{2,3},{3,2},{4,5},{5,4},{6,7},{7,6},{8,9},{9,8},{10,11... | collective-permute-start | bytes 36872 | tf_op jit(solution)/shard_map/ppermute | solution.py:296
  1.1 2.6 %collective-permute-start.3 = (bf16[768,128]{1,0:T(8,128)(2,1)}, bf16[768,128]{1,0:T(8,128)(2,1)S(1)}, u32[]{:S(2)}, u32[]{:S(2)}) collective-permute-start(bf16[768,128]{1,0:T(8,128)(2,1)} %bitcast.27), channel_id=1, source_target_pairs={{0,2},{2,0},{4,6},{6,4},{8,10},{10,8},{12,14},{14,12},{1,3},{3,1},... | collective-permute-start | bytes 589832 | tf_op jit(solution)/shard_map/ppermute | solution.py:349
  3.7 1.6 %collective-permute-start.5 = (bf16[768,128]{1,0:T(8,128)(2,1)}, bf16[768,128]{1,0:T(8,128)(2,1)S(1)}, u32[]{:S(2)}, u32[]{:S(2)}) collective-permute-start(bf16[768,128]{1,0:T(8,128)(2,1)} %bitcast.28), channel_id=1, source_target_pairs={{2,4},{4,2},{6,8},{8,6},{10,12},{12,10},{0,0},{14,14},{3,5},{5,3},... | collective-permute-start | bytes 589832 | tf_op jit(solution)/shard_map/ppermute | solution.py:349
  5.3 0.0 collective-permute-done
  5.3 0.8 %maximum_select_fusion.1 = bf16[4,24,128]{2,0,1:T(4,128)(2,1)S(1)} fusion(bf16[4,12,128]{2,0,1:T(4,128)(2,1)S(1)} %collective-permute-done, bf16[4,12,128]{2,0,1:T(4,128)(2,1)} %bitcast.23, pred[]{:T(512)S(6)} %eq.8), kind=kLoop, calls=%fused_computation.14 | loop fusion | flops 36864 | bytes 49153 | tf_op jit(solution)/shard_map/jit(_where)/select_n | solution.py:346
  6.1 3.4 %collective-permute-start.1 = (bf16[96,128]{1,0:T(8,128)(2,1)S(1)}, bf16[96,128]{1,0:T(8,128)(2,1)S(1)}, u32[]{:S(2)}, u32[]{:S(2)}) collective-permute-start(bf16[96,128]{1,0:T(8,128)(2,1)S(1)} %bitcast.16), channel_id=1, source_target_pairs={{0,2},{1,0},{2,4},{3,1},{4,6},{5,3},{6,8},{7,5},{8,10},{9,7},{10,1... | collective-permute-start | bytes 73736 | tf_op jit(solution)/shard_map/ppermute | solution.py:351
  9.6 1.6 %collective-permute-start.2 = (bf16[96,128]{1,0:T(8,128)(2,1)S(1)}, bf16[96,128]{1,0:T(8,128)(2,1)S(1)}, u32[]{:S(2)}, u32[]{:S(2)}) collective-permute-start(bf16[96,128]{1,0:T(8,128)(2,1)S(1)} %bitcast.17), channel_id=1, source_target_pairs={{0,4},{1,0},{2,6},{3,2},{4,8},{5,1},{6,10},{7,3},{8,12},{9,5},{10,... | collective-permute-start | bytes 73736 | tf_op jit(solution)/shard_map/ppermute | solution.py:351
  11.1 2.5 %prepare.1 = (bf16[9,128,128]{2,1,0:T(8,128)(2,1)S(1)}, bf16[768,128]{1,0:T(8,128)(2,1)S(1)}, bf16[864,24]{1,0:T(8,128)(2,1)S(1)}, bf16[216,192]{1,0:T(8,128)(2,...) custom-call(bf16[96,128]{1,0:T(8,128)(2,1)S(1)} %bitcast.18, ...), custom_call_target="tpu_custom_call" | custom-call | flops 536870912 | bytes 2097152 | tf_op jit(solution)/shard_map/prepare/pallas_call | solution.py:360
  13.6 0.0 collective-permute-done.1
  13.7 0.0 collective-permute-done.2
  13.7 0.0 collective-permute-done.3.even
  13.7 0.1 collective-permute-start.4
  13.8 0.0 collective-permute-done.5.odd
  13.8 1.2 %collective-permute-done.4.far = bf16[192,128]{1,0:T(8,128)(2,1)S(1)} collective-permute-done((bf16[192,128]{1,0:T(8,128)(2,1)S(1)}, bf16[192,128]{1,0:T(8,128)(2,1)S(1)}, u32[]{:S(2)}, u32[]{:S(2)}) %collective-permute-start.4) | collective-permute-done | bytes 49184 | tf_op jit(solution)/shard_map/ppermute | solution.py:296
  15.0 3.8 %main.1 = (bf16[576,128]{1,0:T(8,128)(2,1)S(1)}, f32[576,128]{1,0:T(8,128)S(1)}, bf16[96,1152]{1,0:T(8,128)(2,1)S(1)}, bf16[2304,128]{1,0:T(8,128)(2,1)S(1)}, bf...) custom-call(bf16[192,128]{1,0:T(8,128)(2,1)S(1)} %pad_maximum_fusion.near, ...), custom_call_target="tpu_custom_call" | custom-call | flops 1073741824 | bytes 2097152 | tf_op jit(solution)/shard_map/main/pallas_call | solution.py:391
  18.8 0.2 collective-permute-start.7
  19.0 1.2 %late.1 = (bf16[768,128]{1,0:T(8,128)(2,1)}, bf16[320,128]{1,0:T(8,128)(2,1)S(1)}, f32[320,128]{1,0:T(8,128)S(1)}, f32[4,12,128]{2,1,0:T(8,128)S(1)}, f32[4,12,128]{2,1,0:T(8,128)S(1)}) custom-call(bf16[2304,128]{1,0:T(8,128)(2,1)S(1)} %get-tuple-element.42.act, bf16[768,128]{1,0:T(8,128)(2,1)S(1)} %get-tuple-element.43.d2, ...), custom_call_target="tpu_custom_call" | custom-call | flops 536870912 | bytes 2097152 | tf_op jit(solution)/shard_map/late/pallas_call | solution.py:411
  20.2 0.3 collective-permute-start.13
  20.5 0.2 collective-permute-start.6
  20.7 0.0 collective-permute-done.7
  20.7 2.3 %collective-permute-start.8 = (bf16[288,128]{1,0:T(8,128)(2,1)S(1)}, bf16[288,128]{1,0:T(8,128)(2,1)S(1)}, u32[]{:S(2)}, u32[]{:S(2)}) collective-permute-start(bf16[288,128]{1,0:T(8,128)(2,1)S(1)} %fusion.1), channel_id=1, source_target_pairs={{0,2},{1,5},{2,0},{3,7},{4,6},{5,1},{6,4},{7,3},{8,10},{9,13},{10,... | collective-permute-start | bytes 221192 | tf_op jit(solution)/shard_map/ppermute | solution.py:322
  23.0 0.0 collective-permute-done.13
  23.1 0.7 %collective-permute-start.14 = (bf16[320,128]{1,0:T(8,128)(2,1)S(1)}, bf16[320,128]{1,0:T(8,128)(2,1)S(1)}, u32[]{:S(2)}, u32[]{:S(2)}) collective-permute-start(bf16[320,128]{1,0:T(8,128)(2,1)S(1)} %add_convert_fusion.3), channel_id=1, source_target_pairs={{0,2},{1,9},{2,0},{3,11},{4,6},{5,13},{6,4},{7,15},{8,10},{9,1},{1... | collective-permute-start | bytes 245768 | tf_op jit(solution)/shard_map/ppermute | solution.py:325
  23.8 1.6 %collective-permute-done.8 = bf16[288,128]{1,0:T(8,128)(2,1)S(1)} collective-permute-done((bf16[288,128]{1,0:T(8,128)(2,1)S(1)}, bf16[288,128]{1,0:T(8,128)(2,1)S(1)}, u32[]{:S(2)}, u32[]{:S(2)}) %collective-permute-start.8) | collective-permute-done | bytes 73760 | tf_op jit(solution)/shard_map/ppermute | solution.py:322
  25.4 1.9 %collective-permute-start.9 = (bf16[288,128]{1,0:T(8,128)(2,1)S(1)}, bf16[288,128]{1,0:T(8,128)(2,1)S(1)}, u32[]{:S(2)}, u32[]{:S(2)}) collective-permute-start(bf16[288,128]{1,0:T(8,128)(2,1)S(1)} %fusion), channel_id=1, source_target_pairs={{0,4},{1,3},{2,6},{3,1},{4,0},{5,7},{6,2},{7,5},{8,12},{9,11},{10,... | collective-permute-start | bytes 221192 | tf_op jit(solution)/shard_map/ppermute | solution.py:325
  27.3 0.3 collective-permute-done.14
  27.6 1.6 %collective-permute-start.15 = (bf16[320,128]{1,0:T(8,128)(2,1)S(1)}, bf16[320,128]{1,0:T(8,128)(2,1)S(1)}, u32[]{:S(2)}, u32[]{:S(2)}) collective-permute-start(bf16[320,128]{1,0:T(8,128)(2,1)S(1)} %add_convert_fusion.2), channel_id=1, source_target_pairs={{0,4},{1,3},{2,6},{3,1},{4,0},{5,7},{6,2},{7,5},{8,12},{9,11},{10,... | collective-permute-start | bytes 245768 | tf_op jit(solution)/shard_map/ppermute | solution.py:325
  29.2 0.6 %collective-permute-done.9 = bf16[288,128]{1,0:T(8,128)(2,1)S(1)} collective-permute-done((bf16[288,128]{1,0:T(8,128)(2,1)S(1)}, bf16[288,128]{1,0:T(8,128)(2,1)S(1)}, u32[]{:S(2)}, u32[]{:S(2)}) %collective-permute-start.9) | collective-permute-done | bytes 73760 | tf_op jit(solution)/shard_map/ppermute | solution.py:325
  29.8 2.9 %collective-permute-start.10 = (bf16[288,128]{1,0:T(8,128)(2,1)S(1)}, bf16[288,128]{1,0:T(8,128)(2,1)S(1)}, u32[]{:S(2)}, u32[]{:S(2)}) collective-permute-start(bf16[288,128]{1,0:T(8,128)(2,1)S(1)} %add_convert_fusion.5), channel_id=1, source_target_pairs={{0,8},{1,9},{2,10},{3,11},{4,12},{5,13},{6,14},{7,15},{8,0},{9,1},... | collective-permute-start | bytes 221192 | tf_op jit(solution)/shard_map/ppermute | solution.py:325
  32.8 0.0 collective-permute-done.15
  32.8 2.6 %collective-permute-start.16 = (bf16[320,128]{1,0:T(8,128)(2,1)S(1)}, bf16[320,128]{1,0:T(8,128)(2,1)S(1)}, u32[]{:S(2)}, u32[]{:S(2)}) collective-permute-start(bf16[320,128]{1,0:T(8,128)(2,1)S(1)} %add_convert_fusion.1), channel_id=1, source_target_pairs={{0,8},{1,5},{2,10},{3,7},{4,12},{5,1},{6,14},{7,3},{8,0},{9,13},{1... | collective-permute-start | bytes 245768 | tf_op jit(solution)/shard_map/ppermute | solution.py:325
  35.4 0.1 collective-permute-done.10
  35.6 1.8 %collective-permute-start.11 = (bf16[288,128]{1,0:T(8,128)(2,1)S(1)}, bf16[288,128]{1,0:T(8,128)(2,1)S(1)}, u32[]{:S(2)}, u32[]{:S(2)}) collective-permute-start(bf16[288,128]{1,0:T(8,128)(2,1)S(1)} %add_convert_fusion.4), channel_id=1, source_target_pairs={{0,2},{1,5},{2,0},{3,7},{4,6},{5,1},{6,4},{7,3},{8,10},{9,13},{10,... | collective-permute-start | bytes 221192 | tf_op jit(solution)/shard_map/ppermute | solution.py:328
  37.4 0.9 %collective-permute-done.16 = bf16[320,128]{1,0:T(8,128)(2,1)S(1)} collective-permute-done((bf16[320,128]{1,0:T(8,128)(2,1)S(1)}, bf16[320,128]{1,0:T(8,128)(2,1)S(1)}, u32[]{:S(2)}, u32[]{:S(2)}) %collective-permute-start.16) | collective-permute-done | bytes 81952 | tf_op jit(solution)/shard_map/ppermute | solution.py:325
  38.3 0.1 collective-permute-start.17
  38.4 1.6 %collective-permute-done.11 = bf16[288,128]{1,0:T(8,128)(2,1)S(1)} collective-permute-done((bf16[288,128]{1,0:T(8,128)(2,1)S(1)}, bf16[288,128]{1,0:T(8,128)(2,1)S(1)}, u32[]{:S(2)}, u32[]{:S(2)}) %collective-permute-start.11) | collective-permute-done | bytes 73760 | tf_op jit(solution)/shard_map/ppermute | solution.py:328
  40.0 0.1 collective-permute-start.12
  40.1 0.0 collective-permute-done.6
  40.1 0.6 %copy.12 = f32[4,1,12,128]{3,1,2,0:T(1,128)} copy(f32[4,1,12,128]{3,2,0,1:T(8,128)S(1)} %add_bitcast_fusion) | data formatting | bytes 49152
  40.8 0.0 collective-permute-done.17.time_rest
  40.8 0.7 %collective-permute-done.12.space_rest = bf16[576,128]{1,0:T(8,128)(2,1)S(1)} collective-permute-done((bf16[576,128]{1,0:T(8,128)(2,1)S(1)}, bf16[576,128]{1,0:T(8,128)(2,1)S(1)}, u32[]{:S(2)}, u32[]{:S(2)}) %collective-permute-start.12) | collective-permute-done | bytes 147488 | tf_op jit(solution)/shard_map/ppermute | solution.py:296
  41.5 1.0 %output.1 = (f32[1152,128]{1,0:T(8,128)}, f32[640,128]{1,0:T(8,128)}) custom-call(bf16[576,128]{1,0:T(8,128)(2,1)S(1)} %maximum_select_fusion.space_half, bf16[576,128]{1,0:T(8,128)(2,1)S(1)} %collective-permute-done.12.space_rest, bf16[320,128]{1,0:T(8,128)(2,1)S(1)} %add_convert_fusion.time_half, bf16[320,128]{1,0:T(8,128)(2,1)S(1)} %collective-permute-done.17.time_rest), custom_call_target="tpu_custom_call" | custom-call | tf_op jit(solution)/shard_map/output/pallas_call | solution.py:430
  (13 shorter events, 0.3 us)
Async XLA Ops:
  0.6 4.7 %collective-permute-start = (bf16[4,12,128]{2,0,1:T(4,128)(2,1)}, bf16[4,12,128]{2,0,1:T(4,128)(2,1)S(1)}, u32[]{:S(2)}, u32[]{:S(2)}) collective-permute-start(bf16[4,12,128]{2,0,1:T(4,128)(2,1)} %bitcast.22), channel_id=1, source_target_pairs={{0,1},{1,0},{2,3},{3,2},{4,5},{5,4},{6,7},{7,6},{8,9},{9,8},{10,11... | collective-permute-start | bytes 36872 | tf_op jit(solution)/shard_map/ppermute | solution.py:296
  1.1 12.5 %collective-permute-start.3 = (bf16[768,128]{1,0:T(8,128)(2,1)}, bf16[768,128]{1,0:T(8,128)(2,1)S(1)}, u32[]{:S(2)}, u32[]{:S(2)}) collective-permute-start(bf16[768,128]{1,0:T(8,128)(2,1)} %bitcast.27), channel_id=1, source_target_pairs={{0,2},{2,0},{4,6},{6,4},{8,10},{10,8},{12,14},{14,12},{1,3},{3,1},... | collective-permute-start | bytes 589832 | tf_op jit(solution)/shard_map/ppermute | solution.py:349
  3.7 10.1 %collective-permute-start.5 = (bf16[768,128]{1,0:T(8,128)(2,1)}, bf16[768,128]{1,0:T(8,128)(2,1)S(1)}, u32[]{:S(2)}, u32[]{:S(2)}) collective-permute-start(bf16[768,128]{1,0:T(8,128)(2,1)} %bitcast.28), channel_id=1, source_target_pairs={{2,4},{4,2},{6,8},{8,6},{10,12},{12,10},{0,0},{14,14},{3,5},{5,3},... | collective-permute-start | bytes 589832 | tf_op jit(solution)/shard_map/ppermute | solution.py:349
  6.1 7.5 %collective-permute-start.1 = (bf16[96,128]{1,0:T(8,128)(2,1)S(1)}, bf16[96,128]{1,0:T(8,128)(2,1)S(1)}, u32[]{:S(2)}, u32[]{:S(2)}) collective-permute-start(bf16[96,128]{1,0:T(8,128)(2,1)S(1)} %bitcast.16), channel_id=1, source_target_pairs={{0,2},{1,0},{2,4},{3,1},{4,6},{5,3},{6,8},{7,5},{8,10},{9,7},{10,1... | collective-permute-start | bytes 73736 | tf_op jit(solution)/shard_map/ppermute | solution.py:351
  9.6 4.1 %collective-permute-start.2 = (bf16[96,128]{1,0:T(8,128)(2,1)S(1)}, bf16[96,128]{1,0:T(8,128)(2,1)S(1)}, u32[]{:S(2)}, u32[]{:S(2)}) collective-permute-start(bf16[96,128]{1,0:T(8,128)(2,1)S(1)} %bitcast.17), channel_id=1, source_target_pairs={{0,4},{1,0},{2,6},{3,2},{4,8},{5,1},{6,10},{7,3},{8,12},{9,5},{10,... | collective-permute-start | bytes 73736 | tf_op jit(solution)/shard_map/ppermute | solution.py:351
  13.7 1.3 %collective-permute-start.4 = (bf16[192,128]{1,0:T(8,128)(2,1)S(1)}, bf16[192,128]{1,0:T(8,128)(2,1)S(1)}, u32[]{:S(2)}, u32[]{:S(2)}) collective-permute-start(bf16[192,128]{1,0:T(8,128)(2,1)S(1)} %pad_maximum_fusion.near), channel_id=1, source_target_pairs={{0,1},{1,0},{2,3},{3,2},{4,5},{5,4},{6,7},{7,6},{8,9},{9,8},{10,11... | collective-permute-start | bytes 147464 | tf_op jit(solution)/shard_map/ppermute | solution.py:296
  18.8 1.9 %collective-permute-start.7 = (bf16[576,128]{1,0:T(8,128)(2,1)S(1)}, bf16[576,128]{1,0:T(8,128)(2,1)S(1)}, u32[]{:S(2)}, u32[]{:S(2)}) collective-permute-start(bf16[576,128]{1,0:T(8,128)(2,1)S(1)} %get-tuple-element.53), channel_id=1, source_target_pairs={{0,1},{1,0},{2,3},{3,2},{4,5},{5,4},{6,7},{7,6},{8,9},{9,8},{10,11... | collective-permute-start | bytes 442376 | tf_op jit(solution)/shard_map/ppermute | solution.py:296
  20.2 2.9 %collective-permute-start.13 = (bf16[320,128]{1,0:T(8,128)(2,1)S(1)}, bf16[320,128]{1,0:T(8,128)(2,1)S(1)}, u32[]{:S(2)}, u32[]{:S(2)}) collective-permute-start(bf16[320,128]{1,0:T(8,128)(2,1)S(1)} %get-tuple-element.55), channel_id=1, source_target_pairs={{0,1},{1,0},{2,3},{3,2},{4,5},{5,4},{6,7},{7,6},{8,9},{9,8},{10,11... | collective-permute-start | bytes 245768 | tf_op jit(solution)/shard_map/ppermute | solution.py:296
  20.5 19.6 %collective-permute-start.6 = (f32[4,12,128]{2,1,0:T(8,128)S(1)}, f32[4,12,128]{2,1,0:T(8,128)S(1)}, u32[]{:S(2)}, u32[]{:S(2)}) collective-permute-start(f32[4,12,128]{2,1,0:T(8,128)S(1)} %get-tuple-element.51), channel_id=1, source_target_pairs={{0,1},{1,0},{2,3},{3,2},{4,5},{5,4},{6,7},{7,6},{8,9},{9,8},{10,11... | collective-permute-start | bytes 73736 | tf_op jit(solution)/shard_map/ppermute | solution.py:296
  20.7 4.6 %collective-permute-start.8 = (bf16[288,128]{1,0:T(8,128)(2,1)S(1)}, bf16[288,128]{1,0:T(8,128)(2,1)S(1)}, u32[]{:S(2)}, u32[]{:S(2)}) collective-permute-start(bf16[288,128]{1,0:T(8,128)(2,1)S(1)} %fusion.1), channel_id=1, source_target_pairs={{0,2},{1,5},{2,0},{3,7},{4,6},{5,1},{6,4},{7,3},{8,10},{9,13},{10,... | collective-permute-start | bytes 221192 | tf_op jit(solution)/shard_map/ppermute | solution.py:322
  23.1 4.5 %collective-permute-start.14 = (bf16[320,128]{1,0:T(8,128)(2,1)S(1)}, bf16[320,128]{1,0:T(8,128)(2,1)S(1)}, u32[]{:S(2)}, u32[]{:S(2)}) collective-permute-start(bf16[320,128]{1,0:T(8,128)(2,1)S(1)} %add_convert_fusion.3), channel_id=1, source_target_pairs={{0,2},{1,9},{2,0},{3,11},{4,6},{5,13},{6,4},{7,15},{8,10},{9,1},{1... | collective-permute-start | bytes 245768 | tf_op jit(solution)/shard_map/ppermute | solution.py:325
  25.4 4.4 %collective-permute-start.9 = (bf16[288,128]{1,0:T(8,128)(2,1)S(1)}, bf16[288,128]{1,0:T(8,128)(2,1)S(1)}, u32[]{:S(2)}, u32[]{:S(2)}) collective-permute-start(bf16[288,128]{1,0:T(8,128)(2,1)S(1)} %fusion), channel_id=1, source_target_pairs={{0,4},{1,3},{2,6},{3,1},{4,0},{5,7},{6,2},{7,5},{8,12},{9,11},{10,... | collective-permute-start | bytes 221192 | tf_op jit(solution)/shard_map/ppermute | solution.py:325
  27.6 5.2 %collective-permute-start.15 = (bf16[320,128]{1,0:T(8,128)(2,1)S(1)}, bf16[320,128]{1,0:T(8,128)(2,1)S(1)}, u32[]{:S(2)}, u32[]{:S(2)}) collective-permute-start(bf16[320,128]{1,0:T(8,128)(2,1)S(1)} %add_convert_fusion.2), channel_id=1, source_target_pairs={{0,4},{1,3},{2,6},{3,1},{4,0},{5,7},{6,2},{7,5},{8,12},{9,11},{10,... | collective-permute-start | bytes 245768 | tf_op jit(solution)/shard_map/ppermute | solution.py:325
  29.8 5.7 %collective-permute-start.10 = (bf16[288,128]{1,0:T(8,128)(2,1)S(1)}, bf16[288,128]{1,0:T(8,128)(2,1)S(1)}, u32[]{:S(2)}, u32[]{:S(2)}) collective-permute-start(bf16[288,128]{1,0:T(8,128)(2,1)S(1)} %add_convert_fusion.5), channel_id=1, source_target_pairs={{0,8},{1,9},{2,10},{3,11},{4,12},{5,13},{6,14},{7,15},{8,0},{9,1},... | collective-permute-start | bytes 221192 | tf_op jit(solution)/shard_map/ppermute | solution.py:325
  32.8 5.5 %collective-permute-start.16 = (bf16[320,128]{1,0:T(8,128)(2,1)S(1)}, bf16[320,128]{1,0:T(8,128)(2,1)S(1)}, u32[]{:S(2)}, u32[]{:S(2)}) collective-permute-start(bf16[320,128]{1,0:T(8,128)(2,1)S(1)} %add_convert_fusion.1), channel_id=1, source_target_pairs={{0,8},{1,5},{2,10},{3,7},{4,12},{5,1},{6,14},{7,3},{8,0},{9,13},{1... | collective-permute-start | bytes 245768 | tf_op jit(solution)/shard_map/ppermute | solution.py:325
  35.6 4.4 %collective-permute-start.11 = (bf16[288,128]{1,0:T(8,128)(2,1)S(1)}, bf16[288,128]{1,0:T(8,128)(2,1)S(1)}, u32[]{:S(2)}, u32[]{:S(2)}) collective-permute-start(bf16[288,128]{1,0:T(8,128)(2,1)S(1)} %add_convert_fusion.4), channel_id=1, source_target_pairs={{0,2},{1,5},{2,0},{3,7},{4,6},{5,1},{6,4},{7,3},{8,10},{9,13},{10,... | collective-permute-start | bytes 221192 | tf_op jit(solution)/shard_map/ppermute | solution.py:328
  38.3 2.5 %collective-permute-start.17 = (bf16[320,128]{1,0:T(8,128)(2,1)S(1)}, bf16[320,128]{1,0:T(8,128)(2,1)S(1)}, u32[]{:S(2)}, u32[]{:S(2)}) collective-permute-start(bf16[320,128]{1,0:T(8,128)(2,1)S(1)} %add_convert_fusion.time_half), channel_id=1, source_target_pairs={{0,1},{1,0},{2,3},{3,2},{4,5},{5,4},{6,7},{7,6},{8,9},{9,8},{10,11... | collective-permute-start | bytes 245768 | tf_op jit(solution)/shard_map/ppermute | solution.py:296
  40.0 1.4 %collective-permute-start.12 = (bf16[576,128]{1,0:T(8,128)(2,1)S(1)}, bf16[576,128]{1,0:T(8,128)(2,1)S(1)}, u32[]{:S(2)}, u32[]{:S(2)}) collective-permute-start(bf16[576,128]{1,0:T(8,128)(2,1)S(1)} %maximum_select_fusion.space_half), channel_id=1, source_target_pairs={{0,1},{1,0},{2,3},{3,2},{4,5},{5,4},{6,7},{7,6},{8,9},{9,8},{10,11... | collective-permute-start | bytes 442376 | tf_op jit(solution)/shard_map/ppermute | solution.py:296

commit v4 on v3

--- a/solution.py
+++ b/solution.py
@@ -70,10 +70,8 @@
     return jnp.concatenate(parts, axis=1)
 
 
-def prepare_kernel(
-    base, cot_h, wide_h, conv_t_h, up_t_h, ws_h, wt_h,
-    ws, cot, wide, conv_t, deep, time, time_t, big, direct, act, slope1,
-    up_t, wt, u3, lhs, sems,
+def weights_kernel(
+    cot_h, wide_h, conv_t_h, up_t_h, ws_h, wt_h, ws, cot, wide, conv_t, up_t, deep, time, time_t, wt, sems
 ):
     core = lax.axis_index("tm")
     copies = [
@@ -81,17 +79,17 @@
         for i, (src, dst) in enumerate(
             (
                 (ws_h, ws),
+                (wt_h, wt),
+                (cot_h, cot),
                 (wide_h.at[core], wide),
-                (cot_h, cot),
                 (up_t_h.at[core], up_t),
-                (wt_h, wt),
                 (conv_t_h.at[core], conv_t),
             )
         )
     ]
     for copy in copies:
         copy.start()
-    for copy in copies[:2]:
+    for copy in copies:
         copy.wait()
     zero = jnp.zeros((C, C), BF)
     for b in range(3):
@@ -99,6 +97,15 @@
             here = slice((b * 4 + d) * C, (b * 4 + d + 1) * C)
             deep[here, :C] = ws[3 * d + b] if d < 3 else zero
             deep[here, C:] = ws[3 * (d - 1) + b] if d > 0 else zero
+    for k in range(6):
+        here = slice(k * C, (k + 1) * C)
+        time[here, :C] = wt[k] if k < 5 else zero
+        time[here, C:] = wt[k - 1] if k > 0 else zero
+        time_t[:C, here] = wt[4 - k] if k < 5 else zero
+        time_t[C:, here] = wt[5 - k] if k > 0 else zero
+
+
+def prepare_kernel(base, wide, deep, up_t, cot, big, direct, act, slope1, u3, lhs):
     frames = [base[f * LOW : (f + 1) * LOW, :] for f in range(FRAMES)]
     pre = conv_space(frames, wide, deep, u3, lhs)[0]
     sig = jax.nn.sigmoid(pre)
@@ -109,17 +116,9 @@
         act[here, :] = image_order(one, f)
         slope1[here, :] = image_order(slope, f)
         big[here, :] = u3[f, (EXT + 1) * COLS : (EXT + 1) * COLS + PIX, :]
-    for copy in copies[2:]:
-        copy.wait()
     both = dot(up_t[...], lanes([cot[f * PIX : (f + 1) * PIX, :] for f in range(FRAMES)]))
     for f in range(FRAMES):
         direct[f * LOW : (f + 1) * LOW, :] = both[:, f * C : (f + 1) * C]
-    for k in range(6):
-        here = slice(k * C, (k + 1) * C)
-        time[here, :C] = wt[k] if k < 5 else zero
-        time[here, C:] = wt[k - 1] if k > 0 else zero
-        time_t[:C, here] = wt[4 - k] if k < 5 else zero
-        time_t[C:, here] = wt[5 - k] if k > 0 else zero
 
 
 def conv_space(base_rows, wide, weights, u3, lhs):
@@ -150,9 +149,8 @@
     return jnp.concatenate(out, axis=0)
 
 
-def main_kernel(
-    near, far, even, odd, wide, deep, conv_t, act_own, slope1, time, time_t, cot, base,
-    send, keep, every, act_near, d2_own, extra, z, act, u3, lhs,
+def forward_kernel(
+    near, far, wide, deep, act_own, time, cot, big, res, gt_send, gt_keep, d2, slope2, act, u3, lhs
 ):
     core = lax.axis_index("tm")
     at = lax.axis_index("space")
@@ -171,55 +169,78 @@
     for k, pre in enumerate(conv_space(frames, wide, deep, u3, lhs)):
         one = (pre * jax.nn.sigmoid(pre)).astype(BF)
         for f in range(FRAMES):
-            part = image_order(one, f)
             lo = (FRAMES * (k if k < 2 else k + 1) + f) * PIX
-            act[lo : lo + PIX, :] = part
-            if 2 * GROUP <= lo < 8 * GROUP:
-                act_near[lo - 2 * GROUP : lo - 2 * GROUP + PIX, :] = part
-    act_near[2 * GROUP : 4 * GROUP, :] = act_own[...]
+            act[lo : lo + PIX, :] = image_order(one, f)
 
     def group_of(p):
         if p in (4, 5):
             return act_own[(p - 4) * GROUP : (p - 3) * GROUP, :]
         return act[p * GROUP : (p + 1) * GROUP, :]
 
+    def window(first):
+        return lanes([group_of(first + k) for k in range(6)])
+
     def time_conv(first):
-        pre = dot(lanes([group_of(first + k) for k in range(6)]), time[...])
+        pre = dot(window(first), time[...])
         sig = jax.nn.sigmoid(pre)
         return pre, sig, sig * (1.0 + pre * (1.0 - sig))
 
+    pre, sig, slope = time_conv(2)
+    extra = pre * sig
+    for p in range(2):
+        here = slice(p * GROUP, (p + 1) * GROUP)
+        part = slice(p * C, (p + 1) * C)
+        res[here, :] = (big[here, :].astype(F32) + extra[:, part]).astype(BF)
+        d2[here, :] = (cot[here, :].astype(F32) * slope[:, part]).astype(BF)
+    for side, first in ((0, 0), (1, 4)):
+        slope = time_conv(first)[2]
+        for p in range(2):
+            slope2[side, p * GROUP : (p + 1) * GROUP, :] = slope[:, p * C : (p + 1) * C]
+
+    outer = dot(window(2), lanes([d2[:GROUP, :], d2[GROUP:, :]]), ((0,), (0,)))
+    grads = jnp.concatenate(
+        [
+            outer[t * C : (t + 1) * C, :C] + outer[(t + 1) * C : (t + 2) * C, C:]
+            for t in range(5)
+        ],
+        axis=0,
+    )
+    halve(grads, core, gt_send, gt_keep)
+
+
+def halve(grads, core, send, keep):
+    rows = grads.shape[0] // 2
+    send[...] = jnp.where(core == 0, grads[rows:], grads[:rows]).astype(send.dtype)
+    keep[...] = jnp.where(core == 0, grads[:rows], grads[rows:])
+
+
+def backward_kernel(
+    even, odd, d2, slope1, slope2, base, conv_t, time_t, send, keep, every, dsc,
+):
+    core = lax.axis_index("tm")
+    at = lax.axis_index("space")
+    count = lax.axis_size("space")
     is_even = at % 2 == 0
-    blank = jnp.zeros((GROUP, C), BF)
-    d2 = []
-    for first, inside in ((0, at > 0), (2, None), (4, at < count - 1)):
-        pre, sig, slope = time_conv(first)
-        for p in range(2):
-            here = slice(p * GROUP, (p + 1) * GROUP)
-            part = slice(p * C, (p + 1) * C)
-            if inside is None:
-                got = cot[here, :]
-                extra[here, :] = pre[:, part] * sig[:, part]
-            else:
-                first_choice, other = (odd, even) if first == 0 else (even, odd)
-                got = jnp.where(is_even, first_choice[here, :], other[here, :])
-                got = jnp.where(inside, got, blank)
-            value = (got.astype(F32) * slope[:, part]).astype(BF)
-            if inside is None:
-                d2_own[here, :] = value
-            d2.append(value)
-
-    back = dot(lanes(d2), time_t[...], ((1,), (1,)))
+    zeros = jnp.zeros((FRAMES * PIX, C), F32)
+
+    def outside(first, second, inside, side):
+        got = jnp.where(is_even, first[...], second[...]).astype(F32)
+        return jnp.where(inside, got * slope2[side], zeros).astype(BF)
+
+    before = outside(odd, even, at > 0, 0)
+    after = outside(even, odd, at < count - 1, 1)
+    window = lanes(
+        [before[:GROUP], before[GROUP:], d2[:GROUP, :], d2[GROUP:, :], after[:GROUP], after[GROUP:]]
+    )
+    back = dot(window, time_t[...], ((1,), (1,)))
     for p in range(2):
         lo = p * GROUP
         d1 = (back[:, p * C : (p + 1) * C] * slope1[lo : lo + GROUP, :]).astype(BF)
         small = dot(conv_t[...], lanes([d1[:PIX], d1[PIX:]]))
-        z[2 * p] = small[:, :C]
-        z[2 * p + 1] = small[:, C:]
+        dsc[2 * p] = small[:, :C]
+        dsc[2 * p + 1] = small[:, C:]
     every[...] = lanes(
-        [
-            z[:FRAMES, k * LOW : (k + 1) * LOW, :].reshape(FRAMES * LOW, C).astype(BF)
-            for k in range(TAPS)
-        ]
+        [dsc[:, k * LOW : (k + 1) * LOW, :].reshape(FRAMES * LOW, C).astype(BF) for k in range(TAPS)]
     )
     space = dot(base[...], every[...], ((0,), (0,)))
     halve(
@@ -230,33 +251,14 @@
     )
 
 
-def late_kernel(
-    act, d2, extra, big, every, ws, direct, res, gt_send, gt_keep, low_send, low_keep
-):
-    core = lax.axis_index("tm")
-    window = lanes([act[k * GROUP : (k + 1) * GROUP, :] for k in range(6)])
-    outer = dot(window, lanes([d2[:GROUP, :], d2[GROUP:, :]]), ((0,), (0,)))
-    grads = jnp.concatenate(
-        [
-            outer[t * C : (t + 1) * C, :C] + outer[(t + 1) * C : (t + 2) * C, C:]
-            for t in range(5)
-        ],
-        axis=0,
-    )
-    halve(grads, core, gt_send, gt_keep)
+def late_kernel(every, ws, direct, low_send, low_keep):
+    core = lax.axis_index("tm")
     total = dot(every[...], lanes([ws[k] for k in range(TAPS)]), ((1,), (1,))) + direct[...]
     for f in range(FRAMES):
         upper = total[f * LOW : f * LOW + LCOLS, :]
         lower = total[f * LOW + LCOLS : (f + 1) * LOW, :]
         low_send[f] = jnp.where(core == 0, lower, upper)
         low_keep[f] = jnp.where(core == 0, upper, lower)
-    res[...] = (big[...].astype(F32) + extra[...]).astype(BF)
-
-
-def halve(grads, core, send, keep):
-    rows = grads.shape[0] // 2
-    send[...] = jnp.where(core == 0, grads[rows:], grads[:rows]).astype(send.dtype)
-    keep[...] = jnp.where(core == 0, grads[:rows], grads[rows:])
 
 
 def output_kernel(space_half, space_rest, time_half, time_rest, space, time):
@@ -342,90 +344,107 @@
     ws = w_spatial.reshape(TAPS, C, C)
     cot = cotangent.reshape(FRAMES * PIX, C)
     own = base_latent.reshape(FRAMES, LCOLS, C)
-    other = swap_cores(own)
-    base = jnp.where(
-        core == 0, jnp.concatenate([own, other], axis=1), jnp.concatenate([other, own], axis=1)
-    ).reshape(FRAMES * LOW, C)
-    even, odd = (lax.ppermute(cot, "space", swap_pairs(count, first)) for first in (0, 1))
-    near = jnp.concatenate(
-        [lax.ppermute(base, BOTH, hop_pairs(count, hop)) for hop in (1, 2)], axis=0
-    )
-
     shape = jax.ShapeDtypeStruct
     n_own = FRAMES * PIX
     params = pltpu.CompilerParams(vmem_limit_bytes=32 << 20)
     vmem = pl.BlockSpec(memory_space=pltpu.VMEM)
     hbm = pl.BlockSpec(memory_space=pltpu.HBM)
     cost = lambda flops: pl.CostEstimate(flops=flops, bytes_accessed=2 << 20, transcendentals=0)
-    ws_v, cot_v, wide_v, conv_t_v, deep, time, time_t, big, direct, act, slope1 = pl.pallas_call(
-        prepare_kernel,
-        in_specs=[vmem] + [hbm] * 6,
+    ws_v, cot_v, wide_v, conv_t_v, up_t_v, deep, time, time_t = pl.pallas_call(
+        weights_kernel,
+        in_specs=[pl.BlockSpec(memory_space=pltpu.HBM)] * 6,
         out_shape=(
             shape((TAPS, C, C), BF),
             shape((n_own, C), BF),
             shape((WIDE, LOW), BF),
             shape((LT, PIX), BF),
+            shape((LOW, PIX), BF),
             shape((DEEP, 2 * C), BF),
             shape((6 * C, 2 * C), BF),
             shape((2 * C, 6 * C), BF),
+        ),
+        scratch_shapes=[pltpu.VMEM((5, C, C), BF), pltpu.SemaphoreType.DMA((6,))],
+        compiler_params=params,
+        cost_estimate=cost(1 << 29),
+        name="weights",
+    )(
+        *(
+            pltpu.with_memory_space_constraint(x, pltpu.HBM)
+            for x in (cot, wide, conv_t, up_t, ws, w_temporal)
+        )
+    )
+    other = swap_cores(own)
+    other, wide_v = lax.optimization_barrier((other, wide_v))
+    base = jnp.where(
+        core == 0, jnp.concatenate([own, other], axis=1), jnp.concatenate([other, own], axis=1)
+    ).reshape(FRAMES * LOW, C)
+    tied, base = lax.optimization_barrier((cot, base))
+    even, odd = (lax.ppermute(tied, "space", swap_pairs(count, first)) for first in (0, 1))
+    near = jnp.concatenate(
+        [lax.ppermute(base, BOTH, hop_pairs(count, hop)) for hop in (1, 2)], axis=0
+    )
+    far = swap_cores(near)
+
+    big, direct, act, slope1 = pl.pallas_call(
+        prepare_kernel,
+        out_shape=(
             shape((n_own, C), BF),
             shape((FRAMES * LOW, C), F32),
             shape((n_own, C), BF),
             shape((n_own, C), F32),
         ),
         scratch_shapes=[
-            pltpu.VMEM((LOW, PIX), BF),
-            pltpu.VMEM((5, C, C), BF),
             pltpu.VMEM((FRAMES, WIDE, C), BF),
             pltpu.VMEM((FRAMES * PIX // 2, DEEP), BF),
-            pltpu.SemaphoreType.DMA((6,)),
         ],
         compiler_params=params,
         cost_estimate=cost(1 << 29),
         name="prepare",
-    )(base, *(pltpu.with_memory_space_constraint(x, pltpu.HBM) for x in (cot, wide, conv_t, up_t, ws, w_temporal)))
-    near, even, cot_v = lax.optimization_barrier((near, even, cot_v))
-    far = swap_cores(near)
-    half_space = TAPS * C // 2
-    half_time = 5 * C // 2
-    send, keep, every, act_near, d2, extra = pl.pallas_call(
-        main_kernel,
+    )(base, wide_v, deep, up_t_v, cot_v)
+    res, gt_send, gt_keep, d2, slope2 = pl.pallas_call(
+        forward_kernel,
         out_shape=(
-            shape((half_space, C), BF),
-            shape((half_space, C), F32),
-            shape((FRAMES * LOW, TAPS * C), BF),
-            shape((6 * GROUP, C), BF),
             shape((n_own, C), BF),
-            shape((n_own, C), F32),
+            shape((5 * C // 2, C), BF),
+            shape((5 * C // 2, C), F32),
+            shape((n_own, C), BF),
+            shape((2, n_own, C), F32),
         ),
         scratch_shapes=[
-            pltpu.VMEM((FRAMES, LT, C), F32),
             pltpu.VMEM((5 * n_own, C), BF),
             pltpu.VMEM((4 * FRAMES, WIDE, C), BF),
             pltpu.VMEM((4 * FRAMES * PIX // 2, DEEP), BF),
         ],
         compiler_params=params,
         cost_estimate=cost(1 << 30),
-        name="main",
-    )(near, far, even, odd, wide_v, deep, conv_t_v, act, slope1, time, time_t, cot_v, base)
-    res, gt_send, gt_keep, low_send, low_keep = pl.pallas_call(
+        name="forward",
+    )(near, far, wide_v, deep, act, time, cot_v, big)
+    send, keep, every = pl.pallas_call(
+        backward_kernel,
+        out_shape=(
+            shape((TAPS * C // 2, C), BF),
+            shape((TAPS * C // 2, C), F32),
+            shape((FRAMES * LOW, TAPS * C), BF),
+        ),
+        scratch_shapes=[pltpu.VMEM((FRAMES, LT, C), F32)],
+        compiler_params=params,
+        cost_estimate=cost(1 << 29),
+        name="backward",
+    )(even, odd, d2, slope1, slope2, base, conv_t_v, time_t)
+    sum_space = keep + swap_cores(send).astype(F32)
+    low_send, low_keep = pl.pallas_call(
         late_kernel,
-        out_shape=(
-            shape((n_own, C), BF),
-            shape((half_time, C), BF),
-            shape((half_time, C), F32),
-            shape((FRAMES, LCOLS, C), F32),
-            shape((FRAMES, LCOLS, C), F32),
-        ),
-        compiler_params=params,
-        cost_estimate=cost(1 << 29),
+        out_shape=(shape((FRAMES, LCOLS, C), F32),) * 2,
+        compiler_params=params,
+        cost_estimate=cost(1 << 27),
         name="late",
-    )(act_near, d2, extra, big, every, ws_v, direct)
+    )(every, ws_v, direct)
 
     grad_base = low_keep + swap_cores(low_send)
     halves = []
-    for out, mine, levels in ((gt_send, gt_keep, 0), (send, keep, 1)):
-        halves.append(reduce_chips(mine + swap_cores(out).astype(F32), count, core, at, levels))
+    sum_time = gt_keep + swap_cores(gt_send).astype(F32)
+    for value, levels in ((sum_time, 0), (sum_space, 1)):
+        halves.append(reduce_chips(value, count, core, at, levels))
     time_half, space_half = halves
     grad_spatial, grad_temporal = pl.pallas_call(
         output_kernel,

time: 42.8 us -> 41.4 us (0.967)
  starting transfers between devices: 24.5 us -> 23.4 us
  other arithmetic: 1.05 us -> 0.26 us
    ppermute x2, starting transfers between devices: 4.14 us -> 2.21 us  [local(): lax.ppermute(tied, 'space', swap_pairs(count, first))]
    ppermute x7, starting transfers between devices: 1.47 us -> 3.11 us  [swap_cores(): return lax.ppermute(value, 'tm', [(0, 1), (1, 0)])]
    ppermute x2, waiting for transfers between devices: 0.01 us -> 1.61 us  [local(): lax.ppermute(tied, 'space', swap_pairs(count, first))]
    ppermute x1, waiting for transfers between devices: 1.6 us -> 0.02 us  [reduce_chips(): value = mine + lax.ppermute(out, BOTH, pairs_of(step)).astype(F32)]
    ppermute x5, starting transfers between devices: 9.77 us -> 8.25 us  [reduce_chips(): lax.ppermute(out, BOTH, pairs_of(step)).astype(F32)]
    ppermute x1, starting transfers between devices: 1.8 us -> 2.87 us  [reduce_chips(): got = lax.ppermute(value, BOTH, pairs_of(step))]
    ppermute x2, starting transfers between devices: 5.02 us -> 4.15 us  [local(): lax.ppermute(base, BOTH, hop_pairs(count, hop))]
    select_n x1, other arithmetic: 0.81 us -> 0.02 us  [local(): jnp.where(core == 0, jnp.concatenate([own, other], axis=1), jnp.concatena...]
  transfers between devices with their start and end apart: 18 -> 18, of which waited for: 8 -> 8; matrix products, arithmetic and copies ran while one was open for 4% -> 2% of each run, Pallas kernels for 9% -> 16%
where the time goes in v4:
time: 41.4 us; the launch traced here: 41.2 us
  starting transfers between devices  23.4 us (57%)
  Pallas kernels  8.76 us (21%)
  waiting for transfers between devices  7.2 us (17%)
  between operations  0.86 us (2%)
  local copies, waits for them, and re-layouts  0.68 us (2%)
    ppermute x5, starting transfers between devices, reduce_chips(): lax.ppermute(out, BOTH, pairs_of(step)).astype(F32)  8.25 us
    ppermute x2, starting transfers between devices, local(): lax.ppermute(base, BOTH, hop_pairs(count, hop))  4.15 us
    pallas_call x1, Pallas kernels, local(): pl.pallas_call(forward_kernel, out_shape=(shape((n_own, C), BF), shape((5...  3.85 us
    ppermute x7, starting transfers between devices, swap_cores(): return lax.ppermute(value, 'tm', [(0, 1), (1, 0)])  3.11 us
    ppermute x1, starting transfers between devices, reduce_chips(): got = lax.ppermute(value, BOTH, pairs_of(step))  2.87 us
    ppermute x1, starting transfers between devices, reduce_chips(): value = mine + lax.ppermute(out, BOTH, pairs_of(step)).astype(F32)  2.85 us
    ppermute x2, starting transfers between devices, local(): lax.ppermute(tied, 'space', swap_pairs(count, first))  2.21 us
    ppermute x1, waiting for transfers between devices, reduce_chips(): got = lax.ppermute(value, BOTH, pairs_of(step))  2.17 us
  transfers between devices with their start and end apart: 18, of which 8 were waited for; matrix products, arithmetic and copies ran while one was open for 2% of the time, Pallas kernels for 16%

profile of v4, /device:TPU:0, one launch (start us, length us, event | category | flops | bytes accessed | tf_op | source)
XLA Modules:
  0.0 41.2 jit_solution(7967140046345374609)
XLA Ops:
  0.6 0.5 %collective-permute-start = (bf16[4,12,128]{2,0,1:T(4,128)(2,1)}, bf16[4,12,128]{2,0,1:T(4,128)(2,1)S(1)}, u32[]{:S(2)}, u32[]{:S(2)}) collective-permute-start(bf16[4,12,128]{2,0,1:T(4,128)(2,1)} %bitcast.22), channel_id=1, source_target_pairs={{0,1},{1,0},{2,3},{3,2},{4,5},{5,4},{6,7},{7,6},{8,9},{9,8},{10,11... | collective-permute-start | bytes 36872 | tf_op jit(solution)/shard_map/ppermute | solution.py:298
  1.1 0.0 copy-start
  1.2 0.0 copy-start.1
  1.2 1.5 %weights.1 = (bf16[9,128,128]{2,1,0:T(8,128)(2,1)S(1)}, bf16[768,128]{1,0:T(8,128)(2,1)S(1)}, bf16[864,24]{1,0:T(8,128)(2,1)S(1)}, bf16[216,192]{1,0:T(8,128)(2,...) custom-call(bf16[768,128]{1,0:T(8,128)(2,1)} %bitcast.27, ...), custom_call_target="tpu_custom_call" | custom-call | flops 536870912 | bytes 2097152 | tf_op jit(solution)/shard_map/weights/pallas_call | solution.py:353
  2.7 0.0 collective-permute-done
  2.7 0.0 copy-done
  2.8 2.6 %collective-permute-start.1 = (bf16[96,128]{1,0:T(8,128)(2,1)S(1)}, bf16[96,128]{1,0:T(8,128)(2,1)S(1)}, u32[]{:S(2)}, u32[]{:S(2)}) collective-permute-start(bf16[96,128]{1,0:T(8,128)(2,1)S(1)} %bitcast.16), channel_id=1, source_target_pairs={{0,2},{1,0},{2,4},{3,1},{4,6},{5,3},{6,8},{7,5},{8,10},{9,7},{10,1... | collective-permute-start | bytes 73736 | tf_op jit(solution)/shard_map/ppermute | solution.py:384
  5.3 1.6 %collective-permute-start.2 = (bf16[96,128]{1,0:T(8,128)(2,1)S(1)}, bf16[96,128]{1,0:T(8,128)(2,1)S(1)}, u32[]{:S(2)}, u32[]{:S(2)}) collective-permute-start(bf16[96,128]{1,0:T(8,128)(2,1)S(1)} %bitcast.17), channel_id=1, source_target_pairs={{0,4},{1,0},{2,6},{3,2},{4,8},{5,1},{6,10},{7,3},{8,12},{9,5},{10,... | collective-permute-start | bytes 73736 | tf_op jit(solution)/shard_map/ppermute | solution.py:384
  6.9 0.0 copy-done.1
  6.9 1.5 %collective-permute-start.4 = (bf16[768,128]{1,0:T(8,128)(2,1)S(1)}, bf16[768,128]{1,0:T(8,128)(2,1)S(1)}, u32[]{:S(2)}, u32[]{:S(2)}) collective-permute-start(bf16[768,128]{1,0:T(8,128)(2,1)S(1)} %bitcast.28), channel_id=1, source_target_pairs={{0,2},{2,0},{4,6},{6,4},{8,10},{10,8},{12,14},{14,12},{1,3},{3,1},... | collective-permute-start | bytes 589832 | tf_op jit(solution)/shard_map/ppermute | solution.py:382
  8.5 0.7 %collective-permute-start.5 = (bf16[768,128]{1,0:T(8,128)(2,1)S(1)}, bf16[768,128]{1,0:T(8,128)(2,1)S(1)}, u32[]{:S(2)}, u32[]{:S(2)}) collective-permute-start(bf16[768,128]{1,0:T(8,128)(2,1)S(1)} %bitcast.29), channel_id=1, source_target_pairs={{2,4},{4,2},{6,8},{8,6},{10,12},{12,10},{0,0},{14,14},{3,5},{5,3},... | collective-permute-start | bytes 589832 | tf_op jit(solution)/shard_map/ppermute | solution.py:382
  9.1 0.0 collective-permute-done.1
  9.2 0.0 collective-permute-done.2
  9.2 0.1 collective-permute-start.3
  9.3 1.2 %prepare.1 = (bf16[768,128]{1,0:T(8,128)(2,1)S(1)}, f32[96,128]{1,0:T(8,128)S(1)}, bf16[768,128]{1,0:T(8,128)(2,1)S(1)}, f32[768,128]{1,0:T(8,128)S(1)}) custom-call(bf16[96,128]{1,0:T(8,128)(2,1)S(1)} %bitcast.18, bf16[864,24]{1,0:T(8,128)(2,1)S(1)} %get-tuple-element.35.wide, bf16[1536,256]{1,0:T(8,128)(2,1)S(1)} %get-tuple-element.36.deep, ...), custom_call_target="tpu_custom_call" | custom-call | flops 536870912 | bytes 2097152 | tf_op jit(solution)/shard_map/prepare/pallas_call | solution.py:388
  10.4 0.0 collective-permute-done.3.far
  10.5 3.9 %forward.1 = (bf16[768,128]{1,0:T(8,128)(2,1)}, bf16[320,128]{1,0:T(8,128)(2,1)S(1)}, f32[320,128]{1,0:T(8,128)S(1)}, bf16[768,128]{1,0:T(8,128)(2,1)S(1)}, f32[2,768,128]{2,1,0:T(8,128)S(1)}) custom-call(bf16[192,128]{1,0:T(8,128)(2,1)S(1)} %constant_dynamic-update-slice_fusion.near, bf16[192,128]{1,0:T(8,128)(2,1)S(1)} %collective-permute-done.3.far, ...), custom_call_target="tpu_custom_call" | custom-call | flops 1073741824 | bytes 2097152 | tf_op jit(solution)/shard_map/forward/pallas_call | solution.py:404
  14.3 1.6 %collective-permute-done.4.even = bf16[768,128]{1,0:T(8,128)(2,1)S(1)} collective-permute-done((bf16[768,128]{1,0:T(8,128)(2,1)S(1)}, bf16[768,128]{1,0:T(8,128)(2,1)S(1)}, u32[]{:S(2)}, u32[]{:S(2)}) %collective-permute-start.4) | collective-permute-done | bytes 196640 | tf_op jit(solution)/shard_map/ppermute | solution.py:382
  15.9 0.0 collective-permute-done.5.odd
  15.9 1.0 %backward.1 = (bf16[576,128]{1,0:T(8,128)(2,1)S(1)}, f32[576,128]{1,0:T(8,128)S(1)}, bf16[96,1152]{1,0:T(8,128)(2,1)S(1)}) custom-call(bf16[768,128]{1,0:T(8,128)(2,1)S(1)} %collective-permute-done.4.even, bf16[768,128]{1,0:T(8,128)(2,1)S(1)} %collective-permute-done.5.odd, bf16[768,128]{1,0:T(8,128)(2,1)S(1)} %get-tuple-element.44.d2, ...), custom_call_target="tpu_custom_call" | custom-call | flops 536870912 | bytes 2097152 | tf_op jit(solution)/shard_map/backward/pallas_call | solution.py:422
  16.9 0.1 collective-permute-start.7
  17.0 0.5 %collective-permute-start.13 = (bf16[320,128]{1,0:T(8,128)(2,1)S(1)}, bf16[320,128]{1,0:T(8,128)(2,1)S(1)}, u32[]{:S(2)}, u32[]{:S(2)}) collective-permute-start(bf16[320,128]{1,0:T(8,128)(2,1)S(1)} %get-tuple-element.57), channel_id=1, source_target_pairs={{0,1},{1,0},{2,3},{3,2},{4,5},{5,4},{6,7},{7,6},{8,9},{9,8},{10,11... | collective-permute-start | bytes 245768 | tf_op jit(solution)/shard_map/ppermute | solution.py:298
  17.5 0.9 %collective-permute-done.7 = bf16[576,128]{1,0:T(8,128)(2,1)S(1)} collective-permute-done((bf16[576,128]{1,0:T(8,128)(2,1)S(1)}, bf16[576,128]{1,0:T(8,128)(2,1)S(1)}, u32[]{:S(2)}, u32[]{:S(2)}) %collective-permute-start.7) | collective-permute-done | bytes 147488 | tf_op jit(solution)/shard_map/ppermute | solution.py:298
  18.4 2.8 %collective-permute-start.8 = (bf16[288,128]{1,0:T(8,128)(2,1)S(1)}, bf16[288,128]{1,0:T(8,128)(2,1)S(1)}, u32[]{:S(2)}, u32[]{:S(2)}) collective-permute-start(bf16[288,128]{1,0:T(8,128)(2,1)S(1)} %fusion.1), channel_id=1, source_target_pairs={{0,2},{1,5},{2,0},{3,7},{4,6},{5,1},{6,4},{7,3},{8,10},{9,13},{10,... | collective-permute-start | bytes 221192 | tf_op jit(solution)/shard_map/ppermute | solution.py:324
  21.3 0.0 collective-permute-done.13
  21.3 0.2 collective-permute-start.14
  21.5 0.2 late.1
  21.8 1.8 %collective-permute-start.6 = (f32[4,12,128]{2,1,0:T(8,128)S(1)}, f32[4,12,128]{2,1,0:T(8,128)S(1)}, u32[]{:S(2)}, u32[]{:S(2)}) collective-permute-start(f32[4,12,128]{2,1,0:T(8,128)S(1)} %get-tuple-element.53), channel_id=1, source_target_pairs={{0,1},{1,0},{2,3},{3,2},{4,5},{5,4},{6,7},{7,6},{8,9},{9,8},{10,11... | collective-permute-start | bytes 73736 | tf_op jit(solution)/shard_map/ppermute | solution.py:298
  23.6 0.0 collective-permute-done.8
  23.6 1.9 %collective-permute-start.9 = (bf16[288,128]{1,0:T(8,128)(2,1)S(1)}, bf16[288,128]{1,0:T(8,128)(2,1)S(1)}, u32[]{:S(2)}, u32[]{:S(2)}) collective-permute-start(bf16[288,128]{1,0:T(8,128)(2,1)S(1)} %fusion), channel_id=1, source_target_pairs={{0,4},{1,3},{2,6},{3,1},{4,0},{5,7},{6,2},{7,5},{8,12},{9,11},{10,... | collective-permute-start | bytes 221192 | tf_op jit(solution)/shard_map/ppermute | solution.py:327
  25.5 0.3 collective-permute-done.14
  25.8 1.3 %collective-permute-start.15 = (bf16[320,128]{1,0:T(8,128)(2,1)S(1)}, bf16[320,128]{1,0:T(8,128)(2,1)S(1)}, u32[]{:S(2)}, u32[]{:S(2)}) collective-permute-start(bf16[320,128]{1,0:T(8,128)(2,1)S(1)} %add_convert_fusion.2), channel_id=1, source_target_pairs={{0,4},{1,3},{2,6},{3,1},{4,0},{5,7},{6,2},{7,5},{8,12},{9,11},{10,... | collective-permute-start | bytes 245768 | tf_op jit(solution)/shard_map/ppermute | solution.py:327
  27.1 0.9 %collective-permute-done.9 = bf16[288,128]{1,0:T(8,128)(2,1)S(1)} collective-permute-done((bf16[288,128]{1,0:T(8,128)(2,1)S(1)}, bf16[288,128]{1,0:T(8,128)(2,1)S(1)}, u32[]{:S(2)}, u32[]{:S(2)}) %collective-permute-start.9) | collective-permute-done | bytes 73760 | tf_op jit(solution)/shard_map/ppermute | solution.py:327
  28.1 2.8 %collective-permute-start.10 = (bf16[288,128]{1,0:T(8,128)(2,1)S(1)}, bf16[288,128]{1,0:T(8,128)(2,1)S(1)}, u32[]{:S(2)}, u32[]{:S(2)}) collective-permute-start(bf16[288,128]{1,0:T(8,128)(2,1)S(1)} %add_convert_fusion.5), channel_id=1, source_target_pairs={{0,8},{1,9},{2,10},{3,11},{4,12},{5,13},{6,14},{7,15},{8,0},{9,1},... | collective-permute-start | bytes 221192 | tf_op jit(solution)/shard_map/ppermute | solution.py:327
  30.9 0.0 collective-permute-done.15
  30.9 2.1 %collective-permute-start.16 = (bf16[320,128]{1,0:T(8,128)(2,1)S(1)}, bf16[320,128]{1,0:T(8,128)(2,1)S(1)}, u32[]{:S(2)}, u32[]{:S(2)}) collective-permute-start(bf16[320,128]{1,0:T(8,128)(2,1)S(1)} %add_convert_fusion.1), channel_id=1, source_target_pairs={{0,8},{1,5},{2,10},{3,7},{4,12},{5,1},{6,14},{7,3},{8,0},{9,13},{1... | collective-permute-start | bytes 245768 | tf_op jit(solution)/shard_map/ppermute | solution.py:327
  33.0 0.5 %collective-permute-done.10 = bf16[288,128]{1,0:T(8,128)(2,1)S(1)} collective-permute-done((bf16[288,128]{1,0:T(8,128)(2,1)S(1)}, bf16[288,128]{1,0:T(8,128)(2,1)S(1)}, u32[]{:S(2)}, u32[]{:S(2)}) %collective-permute-start.10) | collective-permute-done | bytes 73760 | tf_op jit(solution)/shard_map/ppermute | solution.py:327
  33.5 2.9 %collective-permute-start.11 = (bf16[288,128]{1,0:T(8,128)(2,1)S(1)}, bf16[288,128]{1,0:T(8,128)(2,1)S(1)}, u32[]{:S(2)}, u32[]{:S(2)}) collective-permute-start(bf16[288,128]{1,0:T(8,128)(2,1)S(1)} %add_convert_fusion.4), channel_id=1, source_target_pairs={{0,2},{1,5},{2,0},{3,7},{4,6},{5,1},{6,4},{7,3},{8,10},{9,13},{10,... | collective-permute-start | bytes 221192 | tf_op jit(solution)/shard_map/ppermute | solution.py:330
  36.4 0.1 collective-permute-done.16
  36.5 0.1 collective-permute-start.17
  36.6 2.2 %collective-permute-done.11 = bf16[288,128]{1,0:T(8,128)(2,1)S(1)} collective-permute-done((bf16[288,128]{1,0:T(8,128)(2,1)S(1)}, bf16[288,128]{1,0:T(8,128)(2,1)S(1)}, u32[]{:S(2)}, u32[]{:S(2)}) %collective-permute-start.11) | collective-permute-done | bytes 73760 | tf_op jit(solution)/shard_map/ppermute | solution.py:330
  38.8 0.1 collective-permute-start.12
  38.8 0.0 collective-permute-done.6
  38.9 0.6 %copy.12 = f32[4,1,12,128]{3,1,2,0:T(1,128)} copy(f32[4,1,12,128]{3,2,0,1:T(8,128)S(1)} %add_bitcast_fusion) | data formatting | bytes 49152
  39.5 0.0 collective-permute-done.17.time_rest
  39.5 0.7 %collective-permute-done.12.space_rest = bf16[576,128]{1,0:T(8,128)(2,1)S(1)} collective-permute-done((bf16[576,128]{1,0:T(8,128)(2,1)S(1)}, bf16[576,128]{1,0:T(8,128)(2,1)S(1)}, u32[]{:S(2)}, u32[]{:S(2)}) %collective-permute-start.12) | collective-permute-done | bytes 147488 | tf_op jit(solution)/shard_map/ppermute | solution.py:298
  40.2 1.0 %output.1 = (f32[1152,128]{1,0:T(8,128)}, f32[640,128]{1,0:T(8,128)}) custom-call(bf16[576,128]{1,0:T(8,128)(2,1)S(1)} %maximum_select_fusion.space_half, bf16[576,128]{1,0:T(8,128)(2,1)S(1)} %collective-permute-done.12.space_rest, bf16[320,128]{1,0:T(8,128)(2,1)S(1)} %add_convert_fusion.time_half, bf16[320,128]{1,0:T(8,128)(2,1)S(1)} %collective-permute-done.17.time_rest), custom_call_target="tpu_custom_call" | custom-call | tf_op jit(solution)/shard_map/output/pallas_call | solution.py:449
  (15 shorter events, 0.3 us)
Async XLA Ops:
  0.6 2.1 %collective-permute-start = (bf16[4,12,128]{2,0,1:T(4,128)(2,1)}, bf16[4,12,128]{2,0,1:T(4,128)(2,1)S(1)}, u32[]{:S(2)}, u32[]{:S(2)}) collective-permute-start(bf16[4,12,128]{2,0,1:T(4,128)(2,1)} %bitcast.22), channel_id=1, source_target_pairs={{0,1},{1,0},{2,3},{3,2},{4,5},{5,4},{6,7},{7,6},{8,9},{9,8},{10,11... | collective-permute-start | bytes 36872 | tf_op jit(solution)/shard_map/ppermute | solution.py:298
  1.1 1.6 %copy-start = (bf16[4,1,12,128]{3,0,2,1:T(4,128)(2,1)S(1)}, bf16[4,1,12,128]{3,0,2,1:T(4,128)(2,1)}, u32[]{:S(2)}) copy-start(bf16[4,1,12,128]{3,0,2,1:T(4,128)(2,1)} %param.7) | copy-start | bytes 36868
  1.2 5.8 %copy-start.1 = (bf16[4,4,48,128]{3,2,1,0:T(8,128)(2,1)S(1)}, bf16[4,4,48,128]{3,2,1,0:T(8,128)(2,1)}, u32[]{:S(2)}) copy-start(bf16[4,4,48,128]{3,2,1,0:T(8,128)(2,1)} %param.8) | copy-start | bytes 589828
  2.8 6.4 %collective-permute-start.1 = (bf16[96,128]{1,0:T(8,128)(2,1)S(1)}, bf16[96,128]{1,0:T(8,128)(2,1)S(1)}, u32[]{:S(2)}, u32[]{:S(2)}) collective-permute-start(bf16[96,128]{1,0:T(8,128)(2,1)S(1)} %bitcast.16), channel_id=1, source_target_pairs={{0,2},{1,0},{2,4},{3,1},{4,6},{5,3},{6,8},{7,5},{8,10},{9,7},{10,1... | collective-permute-start | bytes 73736 | tf_op jit(solution)/shard_map/ppermute | solution.py:384
  5.3 3.8 %collective-permute-start.2 = (bf16[96,128]{1,0:T(8,128)(2,1)S(1)}, bf16[96,128]{1,0:T(8,128)(2,1)S(1)}, u32[]{:S(2)}, u32[]{:S(2)}) collective-permute-start(bf16[96,128]{1,0:T(8,128)(2,1)S(1)} %bitcast.17), channel_id=1, source_target_pairs={{0,4},{1,0},{2,6},{3,2},{4,8},{5,1},{6,10},{7,3},{8,12},{9,5},{10,... | collective-permute-start | bytes 73736 | tf_op jit(solution)/shard_map/ppermute | solution.py:384
  6.9 9.0 %collective-permute-start.4 = (bf16[768,128]{1,0:T(8,128)(2,1)S(1)}, bf16[768,128]{1,0:T(8,128)(2,1)S(1)}, u32[]{:S(2)}, u32[]{:S(2)}) collective-permute-start(bf16[768,128]{1,0:T(8,128)(2,1)S(1)} %bitcast.28), channel_id=1, source_target_pairs={{0,2},{2,0},{4,6},{6,4},{8,10},{10,8},{12,14},{14,12},{1,3},{3,1},... | collective-permute-start | bytes 589832 | tf_op jit(solution)/shard_map/ppermute | solution.py:382
  8.5 7.5 %collective-permute-start.5 = (bf16[768,128]{1,0:T(8,128)(2,1)S(1)}, bf16[768,128]{1,0:T(8,128)(2,1)S(1)}, u32[]{:S(2)}, u32[]{:S(2)}) collective-permute-start(bf16[768,128]{1,0:T(8,128)(2,1)S(1)} %bitcast.29), channel_id=1, source_target_pairs={{2,4},{4,2},{6,8},{8,6},{10,12},{12,10},{0,0},{14,14},{3,5},{5,3},... | collective-permute-start | bytes 589832 | tf_op jit(solution)/shard_map/ppermute | solution.py:382
  9.2 1.3 %collective-permute-start.3 = (bf16[192,128]{1,0:T(8,128)(2,1)S(1)}, bf16[192,128]{1,0:T(8,128)(2,1)S(1)}, u32[]{:S(2)}, u32[]{:S(2)}) collective-permute-start(bf16[192,128]{1,0:T(8,128)(2,1)S(1)} %constant_dynamic-update-slice_fusion.near), channel_id=1, source_target_pairs={{0,1},{1,0},{2,3},{3,2},{4,5},{5,4},{6,7},{7,6},{8,9},{9,8},{10,11... | collective-permute-start | bytes 147464 | tf_op jit(solution)/shard_map/ppermute | solution.py:298
  16.9 1.4 %collective-permute-start.7 = (bf16[576,128]{1,0:T(8,128)(2,1)S(1)}, bf16[576,128]{1,0:T(8,128)(2,1)S(1)}, u32[]{:S(2)}, u32[]{:S(2)}) collective-permute-start(bf16[576,128]{1,0:T(8,128)(2,1)S(1)} %get-tuple-element.55), channel_id=1, source_target_pairs={{0,1},{1,0},{2,3},{3,2},{4,5},{5,4},{6,7},{7,6},{8,9},{9,8},{10,11... | collective-permute-start | bytes 442376 | tf_op jit(solution)/shard_map/ppermute | solution.py:298
  17.0 4.3 %collective-permute-start.13 = (bf16[320,128]{1,0:T(8,128)(2,1)S(1)}, bf16[320,128]{1,0:T(8,128)(2,1)S(1)}, u32[]{:S(2)}, u32[]{:S(2)}) collective-permute-start(bf16[320,128]{1,0:T(8,128)(2,1)S(1)} %get-tuple-element.57), channel_id=1, source_target_pairs={{0,1},{1,0},{2,3},{3,2},{4,5},{5,4},{6,7},{7,6},{8,9},{9,8},{10,11... | collective-permute-start | bytes 245768 | tf_op jit(solution)/shard_map/ppermute | solution.py:298
  18.4 5.2 %collective-permute-start.8 = (bf16[288,128]{1,0:T(8,128)(2,1)S(1)}, bf16[288,128]{1,0:T(8,128)(2,1)S(1)}, u32[]{:S(2)}, u32[]{:S(2)}) collective-permute-start(bf16[288,128]{1,0:T(8,128)(2,1)S(1)} %fusion.1), channel_id=1, source_target_pairs={{0,2},{1,5},{2,0},{3,7},{4,6},{5,1},{6,4},{7,3},{8,10},{9,13},{10,... | collective-permute-start | bytes 221192 | tf_op jit(solution)/shard_map/ppermute | solution.py:324
  21.3 4.5 %collective-permute-start.14 = (bf16[320,128]{1,0:T(8,128)(2,1)S(1)}, bf16[320,128]{1,0:T(8,128)(2,1)S(1)}, u32[]{:S(2)}, u32[]{:S(2)}) collective-permute-start(bf16[320,128]{1,0:T(8,128)(2,1)S(1)} %add_convert_fusion.3), channel_id=1, source_target_pairs={{0,2},{1,9},{2,0},{3,11},{4,6},{5,13},{6,4},{7,15},{8,10},{9,1},{1... | collective-permute-start | bytes 245768 | tf_op jit(solution)/shard_map/ppermute | solution.py:327
  21.8 17.1 %collective-permute-start.6 = (f32[4,12,128]{2,1,0:T(8,128)S(1)}, f32[4,12,128]{2,1,0:T(8,128)S(1)}, u32[]{:S(2)}, u32[]{:S(2)}) collective-permute-start(f32[4,12,128]{2,1,0:T(8,128)S(1)} %get-tuple-element.53), channel_id=1, source_target_pairs={{0,1},{1,0},{2,3},{3,2},{4,5},{5,4},{6,7},{7,6},{8,9},{9,8},{10,11... | collective-permute-start | bytes 73736 | tf_op jit(solution)/shard_map/ppermute | solution.py:298
  23.6 4.4 %collective-permute-start.9 = (bf16[288,128]{1,0:T(8,128)(2,1)S(1)}, bf16[288,128]{1,0:T(8,128)(2,1)S(1)}, u32[]{:S(2)}, u32[]{:S(2)}) collective-permute-start(bf16[288,128]{1,0:T(8,128)(2,1)S(1)} %fusion), channel_id=1, source_target_pairs={{0,4},{1,3},{2,6},{3,1},{4,0},{5,7},{6,2},{7,5},{8,12},{9,11},{10,... | collective-permute-start | bytes 221192 | tf_op jit(solution)/shard_map/ppermute | solution.py:327
  25.8 5.1 %collective-permute-start.15 = (bf16[320,128]{1,0:T(8,128)(2,1)S(1)}, bf16[320,128]{1,0:T(8,128)(2,1)S(1)}, u32[]{:S(2)}, u32[]{:S(2)}) collective-permute-start(bf16[320,128]{1,0:T(8,128)(2,1)S(1)} %add_convert_fusion.2), channel_id=1, source_target_pairs={{0,4},{1,3},{2,6},{3,1},{4,0},{5,7},{6,2},{7,5},{8,12},{9,11},{10,... | collective-permute-start | bytes 245768 | tf_op jit(solution)/shard_map/ppermute | solution.py:327
  28.1 5.4 %collective-permute-start.10 = (bf16[288,128]{1,0:T(8,128)(2,1)S(1)}, bf16[288,128]{1,0:T(8,128)(2,1)S(1)}, u32[]{:S(2)}, u32[]{:S(2)}) collective-permute-start(bf16[288,128]{1,0:T(8,128)(2,1)S(1)} %add_convert_fusion.5), channel_id=1, source_target_pairs={{0,8},{1,9},{2,10},{3,11},{4,12},{5,13},{6,14},{7,15},{8,0},{9,1},... | collective-permute-start | bytes 221192 | tf_op jit(solution)/shard_map/ppermute | solution.py:327
  30.9 5.5 %collective-permute-start.16 = (bf16[320,128]{1,0:T(8,128)(2,1)S(1)}, bf16[320,128]{1,0:T(8,128)(2,1)S(1)}, u32[]{:S(2)}, u32[]{:S(2)}) collective-permute-start(bf16[320,128]{1,0:T(8,128)(2,1)S(1)} %add_convert_fusion.1), channel_id=1, source_target_pairs={{0,8},{1,5},{2,10},{3,7},{4,12},{5,1},{6,14},{7,3},{8,0},{9,13},{1... | collective-permute-start | bytes 245768 | tf_op jit(solution)/shard_map/ppermute | solution.py:327
  33.5 5.2 %collective-permute-start.11 = (bf16[288,128]{1,0:T(8,128)(2,1)S(1)}, bf16[288,128]{1,0:T(8,128)(2,1)S(1)}, u32[]{:S(2)}, u32[]{:S(2)}) collective-permute-start(bf16[288,128]{1,0:T(8,128)(2,1)S(1)} %add_convert_fusion.4), channel_id=1, source_target_pairs={{0,2},{1,5},{2,0},{3,7},{4,6},{5,1},{6,4},{7,3},{8,10},{9,13},{10,... | collective-permute-start | bytes 221192 | tf_op jit(solution)/shard_map/ppermute | solution.py:330
  36.5 3.0 %collective-permute-start.17 = (bf16[320,128]{1,0:T(8,128)(2,1)S(1)}, bf16[320,128]{1,0:T(8,128)(2,1)S(1)}, u32[]{:S(2)}, u32[]{:S(2)}) collective-permute-start(bf16[320,128]{1,0:T(8,128)(2,1)S(1)} %add_convert_fusion.time_half), channel_id=1, source_target_pairs={{0,1},{1,0},{2,3},{3,2},{4,5},{5,4},{6,7},{7,6},{8,9},{9,8},{10,11... | collective-permute-start | bytes 245768 | tf_op jit(solution)/shard_map/ppermute | solution.py:298
  38.8 1.4 %collective-permute-start.12 = (bf16[576,128]{1,0:T(8,128)(2,1)S(1)}, bf16[576,128]{1,0:T(8,128)(2,1)S(1)}, u32[]{:S(2)}, u32[]{:S(2)}) collective-permute-start(bf16[576,128]{1,0:T(8,128)(2,1)S(1)} %maximum_select_fusion.space_half), channel_id=1, source_target_pairs={{0,1},{1,0},{2,3},{3,2},{4,5},{5,4},{6,7},{7,6},{8,9},{9,8},{10,11... | collective-permute-start | bytes 442376 | tf_op jit(solution)/shard_map/ppermute | solution.py:298

commit v5 on v4

--- a/solution.py
+++ b/solution.py
@@ -303,7 +303,7 @@
     if count != 1 << bits:
         return lax.psum(value, "space").astype(BF)
     plain = list(range(bits))
-    orders = [plain, plain[1::-1] + plain[2:] if levels else plain[-1:] + plain[:-1]]
+    orders = [plain, plain[-1:] + plain[:-1]]
 
     def pairs_of(step):
         pairs = []
@@ -432,6 +432,7 @@
         name="backward",
     )(even, odd, d2, slope1, slope2, base, conv_t_v, time_t)
     sum_space = keep + swap_cores(send).astype(F32)
+    sum_space, every = lax.optimization_barrier((sum_space, every))
     low_send, low_keep = pl.pallas_call(
         late_kernel,
         out_shape=(shape((FRAMES, LCOLS, C), F32),) * 2,

time: 41.4 us -> 41 us (level)
  starting transfers between devices: 23.4 us -> 21.4 us
  waiting for transfers between devices: 7.2 us -> 8.87 us
    ppermute x1, waiting for transfers between devices: 0.02 us -> 2.09 us  [reduce_chips(): value = mine + lax.ppermute(out, BOTH, pairs_of(step)).astype(F32)]
    ppermute x7, starting transfers between devices: 3.11 us -> 2.12 us  [swap_cores(): return lax.ppermute(value, 'tm', [(0, 1), (1, 0)])]
    ppermute x1, starting transfers between devices: 2.87 us -> 2.23 us  [reduce_chips(): got = lax.ppermute(value, BOTH, pairs_of(step))]
    ppermute x1, waiting for transfers between devices: 2.17 us -> 1.54 us  [reduce_chips(): got = lax.ppermute(value, BOTH, pairs_of(step))]
    ppermute x5, waiting for transfers between devices: 1.8 us -> 2.36 us  [reduce_chips(): lax.ppermute(out, BOTH, pairs_of(step)).astype(F32)]
  transfers between devices with their start and end apart: 18 -> 18, of which waited for: 8 -> 9; matrix products, arithmetic and copies ran while one was open for 2% -> 2% of each run, Pallas kernels for 16% -> 17%
where the time goes in v5:
time: 41 us; the launch traced here: 40.9 us
  starting transfers between devices  21.4 us (52%)
  waiting for transfers between devices  8.87 us (22%)
  Pallas kernels  8.76 us (21%)
  between operations  0.84 us (2%)
  local copies, waits for them, and re-layouts  0.68 us (2%)
    ppermute x5, starting transfers between devices, reduce_chips(): lax.ppermute(out, BOTH, pairs_of(step)).astype(F32)  7.89 us
    ppermute x2, starting transfers between devices, local(): lax.ppermute(base, BOTH, hop_pairs(count, hop))  4.15 us
    pallas_call x1, Pallas kernels, local(): pl.pallas_call(forward_kernel, out_shape=(shape((n_own, C), BF), shape((5...  3.85 us
    ppermute x1, starting transfers between devices, reduce_chips(): value = mine + lax.ppermute(out, BOTH, pairs_of(step)).astype(F32)  2.85 us
    ppermute x5, waiting for transfers between devices, reduce_chips(): lax.ppermute(out, BOTH, pairs_of(step)).astype(F32)  2.36 us
    ppermute x1, starting transfers between devices, reduce_chips(): got = lax.ppermute(value, BOTH, pairs_of(step))  2.23 us
    ppermute x2, starting transfers between devices, local(): lax.ppermute(tied, 'space', swap_pairs(count, first))  2.21 us
    ppermute x7, starting transfers between devices, swap_cores(): return lax.ppermute(value, 'tm', [(0, 1), (1, 0)])  2.12 us
  transfers between devices with their start and end apart: 18, of which 9 were waited for; matrix products, arithmetic and copies ran while one was open for 2% of the time, Pallas kernels for 17%

profile of v5, /device:TPU:0, one launch (start us, length us, event | category | flops | bytes accessed | tf_op | source)
XLA Modules:
  0.0 40.9 jit_solution(1933726444511480035)
XLA Ops:
  0.6 0.5 %collective-permute-start = (bf16[4,12,128]{2,0,1:T(4,128)(2,1)}, bf16[4,12,128]{2,0,1:T(4,128)(2,1)S(1)}, u32[]{:S(2)}, u32[]{:S(2)}) collective-permute-start(bf16[4,12,128]{2,0,1:T(4,128)(2,1)} %bitcast.22), channel_id=1, source_target_pairs={{0,1},{1,0},{2,3},{3,2},{4,5},{5,4},{6,7},{7,6},{8,9},{9,8},{10,11... | collective-permute-start | bytes 36872 | tf_op jit(solution)/shard_map/ppermute | solution.py:298
  1.1 0.0 copy-start
  1.2 0.0 copy-start.1
  1.2 1.5 %weights.1 = (bf16[9,128,128]{2,1,0:T(8,128)(2,1)S(1)}, bf16[768,128]{1,0:T(8,128)(2,1)S(1)}, bf16[864,24]{1,0:T(8,128)(2,1)S(1)}, bf16[216,192]{1,0:T(8,128)(2,...) custom-call(bf16[768,128]{1,0:T(8,128)(2,1)} %bitcast.27, ...), custom_call_target="tpu_custom_call" | custom-call | flops 536870912 | bytes 2097152 | tf_op jit(solution)/shard_map/weights/pallas_call | solution.py:353
  2.7 0.0 collective-permute-done
  2.7 0.0 copy-done
  2.8 2.6 %collective-permute-start.1 = (bf16[96,128]{1,0:T(8,128)(2,1)S(1)}, bf16[96,128]{1,0:T(8,128)(2,1)S(1)}, u32[]{:S(2)}, u32[]{:S(2)}) collective-permute-start(bf16[96,128]{1,0:T(8,128)(2,1)S(1)} %bitcast.16), channel_id=1, source_target_pairs={{0,2},{1,0},{2,4},{3,1},{4,6},{5,3},{6,8},{7,5},{8,10},{9,7},{10,1... | collective-permute-start | bytes 73736 | tf_op jit(solution)/shard_map/ppermute | solution.py:384
  5.3 1.6 %collective-permute-start.2 = (bf16[96,128]{1,0:T(8,128)(2,1)S(1)}, bf16[96,128]{1,0:T(8,128)(2,1)S(1)}, u32[]{:S(2)}, u32[]{:S(2)}) collective-permute-start(bf16[96,128]{1,0:T(8,128)(2,1)S(1)} %bitcast.17), channel_id=1, source_target_pairs={{0,4},{1,0},{2,6},{3,2},{4,8},{5,1},{6,10},{7,3},{8,12},{9,5},{10,... | collective-permute-start | bytes 73736 | tf_op jit(solution)/shard_map/ppermute | solution.py:384
  6.9 0.0 copy-done.1
  6.9 1.5 %collective-permute-start.4 = (bf16[768,128]{1,0:T(8,128)(2,1)S(1)}, bf16[768,128]{1,0:T(8,128)(2,1)S(1)}, u32[]{:S(2)}, u32[]{:S(2)}) collective-permute-start(bf16[768,128]{1,0:T(8,128)(2,1)S(1)} %bitcast.28), channel_id=1, source_target_pairs={{0,2},{2,0},{4,6},{6,4},{8,10},{10,8},{12,14},{14,12},{1,3},{3,1},... | collective-permute-start | bytes 589832 | tf_op jit(solution)/shard_map/ppermute | solution.py:382
  8.5 0.7 %collective-permute-start.5 = (bf16[768,128]{1,0:T(8,128)(2,1)S(1)}, bf16[768,128]{1,0:T(8,128)(2,1)S(1)}, u32[]{:S(2)}, u32[]{:S(2)}) collective-permute-start(bf16[768,128]{1,0:T(8,128)(2,1)S(1)} %bitcast.29), channel_id=1, source_target_pairs={{2,4},{4,2},{6,8},{8,6},{10,12},{12,10},{0,0},{14,14},{3,5},{5,3},... | collective-permute-start | bytes 589832 | tf_op jit(solution)/shard_map/ppermute | solution.py:382
  9.1 0.0 collective-permute-done.1
  9.2 0.0 collective-permute-done.2
  9.2 0.1 collective-permute-start.3
  9.3 1.2 %prepare.1 = (bf16[768,128]{1,0:T(8,128)(2,1)S(1)}, f32[96,128]{1,0:T(8,128)S(1)}, bf16[768,128]{1,0:T(8,128)(2,1)S(1)}, f32[768,128]{1,0:T(8,128)S(1)}) custom-call(bf16[96,128]{1,0:T(8,128)(2,1)S(1)} %bitcast.18, bf16[864,24]{1,0:T(8,128)(2,1)S(1)} %get-tuple-element.37.wide, bf16[1536,256]{1,0:T(8,128)(2,1)S(1)} %get-tuple-element.38.deep, ...), custom_call_target="tpu_custom_call" | custom-call | flops 536870912 | bytes 2097152 | tf_op jit(solution)/shard_map/prepare/pallas_call | solution.py:388
  10.4 0.0 collective-permute-done.3.far
  10.5 3.9 %forward.1 = (bf16[768,128]{1,0:T(8,128)(2,1)}, bf16[320,128]{1,0:T(8,128)(2,1)S(1)}, f32[320,128]{1,0:T(8,128)S(1)}, bf16[768,128]{1,0:T(8,128)(2,1)S(1)}, f32[2,768,128]{2,1,0:T(8,128)S(1)}) custom-call(bf16[192,128]{1,0:T(8,128)(2,1)S(1)} %constant_dynamic-update-slice_fusion.near, bf16[192,128]{1,0:T(8,128)(2,1)S(1)} %collective-permute-done.3.far, ...), custom_call_target="tpu_custom_call" | custom-call | flops 1073741824 | bytes 2097152 | tf_op jit(solution)/shard_map/forward/pallas_call | solution.py:404
  14.3 1.6 %collective-permute-done.4.even = bf16[768,128]{1,0:T(8,128)(2,1)S(1)} collective-permute-done((bf16[768,128]{1,0:T(8,128)(2,1)S(1)}, bf16[768,128]{1,0:T(8,128)(2,1)S(1)}, u32[]{:S(2)}, u32[]{:S(2)}) %collective-permute-start.4) | collective-permute-done | bytes 196640 | tf_op jit(solution)/shard_map/ppermute | solution.py:382
  15.9 0.0 collective-permute-done.5.odd
  15.9 1.0 %backward.1 = (bf16[576,128]{1,0:T(8,128)(2,1)S(1)}, f32[576,128]{1,0:T(8,128)S(1)}, bf16[96,1152]{1,0:T(8,128)(2,1)S(1)}) custom-call(bf16[768,128]{1,0:T(8,128)(2,1)S(1)} %collective-permute-done.4.even, bf16[768,128]{1,0:T(8,128)(2,1)S(1)} %collective-permute-done.5.odd, bf16[768,128]{1,0:T(8,128)(2,1)S(1)} %get-tuple-element.46.d2, ...), custom_call_target="tpu_custom_call" | custom-call | flops 536870912 | bytes 2097152 | tf_op jit(solution)/shard_map/backward/pallas_call | solution.py:422
  16.9 0.1 collective-permute-start.6
  17.0 0.5 %collective-permute-start.13 = (bf16[320,128]{1,0:T(8,128)(2,1)S(1)}, bf16[320,128]{1,0:T(8,128)(2,1)S(1)}, u32[]{:S(2)}, u32[]{:S(2)}) collective-permute-start(bf16[320,128]{1,0:T(8,128)(2,1)S(1)} %get-tuple-element.61), channel_id=1, source_target_pairs={{0,1},{1,0},{2,3},{3,2},{4,5},{5,4},{6,7},{7,6},{8,9},{9,8},{10,11... | collective-permute-start | bytes 245768 | tf_op jit(solution)/shard_map/ppermute | solution.py:298
  17.5 0.9 %collective-permute-done.6 = bf16[576,128]{1,0:T(8,128)(2,1)S(1)} collective-permute-done((bf16[576,128]{1,0:T(8,128)(2,1)S(1)}, bf16[576,128]{1,0:T(8,128)(2,1)S(1)}, u32[]{:S(2)}, u32[]{:S(2)}) %collective-permute-start.6) | collective-permute-done | bytes 147488 | tf_op jit(solution)/shard_map/ppermute | solution.py:298
  18.4 2.8 %collective-permute-start.8 = (bf16[288,128]{1,0:T(8,128)(2,1)S(1)}, bf16[288,128]{1,0:T(8,128)(2,1)S(1)}, u32[]{:S(2)}, u32[]{:S(2)}) collective-permute-start(bf16[288,128]{1,0:T(8,128)(2,1)S(1)} %fusion.1), channel_id=1, source_target_pairs={{0,2},{1,9},{2,0},{3,11},{4,6},{5,13},{6,4},{7,15},{8,10},{9,1},{1... | collective-permute-start | bytes 221192 | tf_op jit(solution)/shard_map/ppermute | solution.py:324
  21.3 0.0 collective-permute-done.13
  21.3 0.2 collective-permute-start.14
  21.5 2.1 %collective-permute-done.8 = bf16[288,128]{1,0:T(8,128)(2,1)S(1)} collective-permute-done((bf16[288,128]{1,0:T(8,128)(2,1)S(1)}, bf16[288,128]{1,0:T(8,128)(2,1)S(1)}, u32[]{:S(2)}, u32[]{:S(2)}) %collective-permute-start.8) | collective-permute-done | bytes 73760 | tf_op jit(solution)/shard_map/ppermute | solution.py:324
  23.6 1.9 %collective-permute-start.9 = (bf16[288,128]{1,0:T(8,128)(2,1)S(1)}, bf16[288,128]{1,0:T(8,128)(2,1)S(1)}, u32[]{:S(2)}, u32[]{:S(2)}) collective-permute-start(bf16[288,128]{1,0:T(8,128)(2,1)S(1)} %fusion), channel_id=1, source_target_pairs={{0,4},{1,3},{2,6},{3,1},{4,0},{5,7},{6,2},{7,5},{8,12},{9,11},{10,... | collective-permute-start | bytes 221192 | tf_op jit(solution)/shard_map/ppermute | solution.py:327
  25.5 0.3 collective-permute-done.14
  25.8 1.3 %collective-permute-start.15 = (bf16[320,128]{1,0:T(8,128)(2,1)S(1)}, bf16[320,128]{1,0:T(8,128)(2,1)S(1)}, u32[]{:S(2)}, u32[]{:S(2)}) collective-permute-start(bf16[320,128]{1,0:T(8,128)(2,1)S(1)} %add_convert_fusion.2), channel_id=1, source_target_pairs={{0,4},{1,3},{2,6},{3,1},{4,0},{5,7},{6,2},{7,5},{8,12},{9,11},{10,... | collective-permute-start | bytes 245768 | tf_op jit(solution)/shard_map/ppermute | solution.py:327
  27.1 0.9 %collective-permute-done.9 = bf16[288,128]{1,0:T(8,128)(2,1)S(1)} collective-permute-done((bf16[288,128]{1,0:T(8,128)(2,1)S(1)}, bf16[288,128]{1,0:T(8,128)(2,1)S(1)}, u32[]{:S(2)}, u32[]{:S(2)}) %collective-permute-start.9) | collective-permute-done | bytes 73760 | tf_op jit(solution)/shard_map/ppermute | solution.py:327
  28.1 2.8 %collective-permute-start.10 = (bf16[288,128]{1,0:T(8,128)(2,1)S(1)}, bf16[288,128]{1,0:T(8,128)(2,1)S(1)}, u32[]{:S(2)}, u32[]{:S(2)}) collective-permute-start(bf16[288,128]{1,0:T(8,128)(2,1)S(1)} %add_convert_fusion.5), channel_id=1, source_target_pairs={{0,8},{1,5},{2,10},{3,7},{4,12},{5,1},{6,14},{7,3},{8,0},{9,13},{1... | collective-permute-start | bytes 221192 | tf_op jit(solution)/shard_map/ppermute | solution.py:327
  30.9 0.0 collective-permute-done.15
  30.9 1.7 %collective-permute-start.16 = (bf16[320,128]{1,0:T(8,128)(2,1)S(1)}, bf16[320,128]{1,0:T(8,128)(2,1)S(1)}, u32[]{:S(2)}, u32[]{:S(2)}) collective-permute-start(bf16[320,128]{1,0:T(8,128)(2,1)S(1)} %add_convert_fusion.1), channel_id=1, source_target_pairs={{0,8},{1,5},{2,10},{3,7},{4,12},{5,1},{6,14},{7,3},{8,0},{9,13},{1... | collective-permute-start | bytes 245768 | tf_op jit(solution)/shard_map/ppermute | solution.py:327
  32.7 0.2 late.1
  32.9 0.1 collective-permute-start.7
  33.0 0.4 collective-permute-done.10
  33.4 2.2 %collective-permute-start.11 = (bf16[288,128]{1,0:T(8,128)(2,1)S(1)}, bf16[288,128]{1,0:T(8,128)(2,1)S(1)}, u32[]{:S(2)}, u32[]{:S(2)}) collective-permute-start(bf16[288,128]{1,0:T(8,128)(2,1)S(1)} %add_convert_fusion.4), channel_id=1, source_target_pairs={{0,2},{1,9},{2,0},{3,11},{4,6},{5,13},{6,4},{7,15},{8,10},{9,1},{1... | collective-permute-start | bytes 221192 | tf_op jit(solution)/shard_map/ppermute | solution.py:330
  35.6 0.7 %collective-permute-done.16 = bf16[320,128]{1,0:T(8,128)(2,1)S(1)} collective-permute-done((bf16[320,128]{1,0:T(8,128)(2,1)S(1)}, bf16[320,128]{1,0:T(8,128)(2,1)S(1)}, u32[]{:S(2)}, u32[]{:S(2)}) %collective-permute-start.16) | collective-permute-done | bytes 81952 | tf_op jit(solution)/shard_map/ppermute | solution.py:327
  36.4 0.1 collective-permute-start.17
  36.4 1.5 %collective-permute-done.11 = bf16[288,128]{1,0:T(8,128)(2,1)S(1)} collective-permute-done((bf16[288,128]{1,0:T(8,128)(2,1)S(1)}, bf16[288,128]{1,0:T(8,128)(2,1)S(1)}, u32[]{:S(2)}, u32[]{:S(2)}) %collective-permute-start.11) | collective-permute-done | bytes 73760 | tf_op jit(solution)/shard_map/ppermute | solution.py:330
  38.0 0.8 %collective-permute-start.12 = (bf16[576,128]{1,0:T(8,128)(2,1)S(1)}, bf16[576,128]{1,0:T(8,128)(2,1)S(1)}, u32[]{:S(2)}, u32[]{:S(2)}) collective-permute-start(bf16[576,128]{1,0:T(8,128)(2,1)S(1)} %maximum_select_fusion.space_half), channel_id=1, source_target_pairs={{0,1},{1,0},{2,3},{3,2},{4,5},{5,4},{6,7},{7,6},{8,9},{9,8},{10,11... | collective-permute-start | bytes 442376 | tf_op jit(solution)/shard_map/ppermute | solution.py:298
  38.9 0.0 collective-permute-done.7
  38.9 0.6 %copy.12 = f32[4,1,12,128]{3,1,2,0:T(1,128)} copy(f32[4,1,12,128]{3,2,0,1:T(8,128)S(1)} %add_bitcast_fusion) | data formatting | bytes 49152
  39.5 0.0 collective-permute-done.17.time_rest
  39.5 0.4 collective-permute-done.12.space_rest
  39.9 1.0 %output.1 = (f32[1152,128]{1,0:T(8,128)}, f32[640,128]{1,0:T(8,128)}) custom-call(bf16[576,128]{1,0:T(8,128)(2,1)S(1)} %maximum_select_fusion.space_half, bf16[576,128]{1,0:T(8,128)(2,1)S(1)} %collective-permute-done.12.space_rest, bf16[320,128]{1,0:T(8,128)(2,1)S(1)} %add_convert_fusion.time_half, bf16[320,128]{1,0:T(8,128)(2,1)S(1)} %collective-permute-done.17.time_rest), custom_call_target="tpu_custom_call" | custom-call | tf_op jit(solution)/shard_map/output/pallas_call | solution.py:450
  (15 shorter events, 0.3 us)
Async XLA Ops:
  0.6 2.1 %collective-permute-start = (bf16[4,12,128]{2,0,1:T(4,128)(2,1)}, bf16[4,12,128]{2,0,1:T(4,128)(2,1)S(1)}, u32[]{:S(2)}, u32[]{:S(2)}) collective-permute-start(bf16[4,12,128]{2,0,1:T(4,128)(2,1)} %bitcast.22), channel_id=1, source_target_pairs={{0,1},{1,0},{2,3},{3,2},{4,5},{5,4},{6,7},{7,6},{8,9},{9,8},{10,11... | collective-permute-start | bytes 36872 | tf_op jit(solution)/shard_map/ppermute | solution.py:298
  1.1 1.6 %copy-start = (bf16[4,1,12,128]{3,0,2,1:T(4,128)(2,1)S(1)}, bf16[4,1,12,128]{3,0,2,1:T(4,128)(2,1)}, u32[]{:S(2)}) copy-start(bf16[4,1,12,128]{3,0,2,1:T(4,128)(2,1)} %param.7) | copy-start | bytes 36868
  1.2 5.8 %copy-start.1 = (bf16[4,4,48,128]{3,2,1,0:T(8,128)(2,1)S(1)}, bf16[4,4,48,128]{3,2,1,0:T(8,128)(2,1)}, u32[]{:S(2)}) copy-start(bf16[4,4,48,128]{3,2,1,0:T(8,128)(2,1)} %param.8) | copy-start | bytes 589828
  2.8 6.4 %collective-permute-start.1 = (bf16[96,128]{1,0:T(8,128)(2,1)S(1)}, bf16[96,128]{1,0:T(8,128)(2,1)S(1)}, u32[]{:S(2)}, u32[]{:S(2)}) collective-permute-start(bf16[96,128]{1,0:T(8,128)(2,1)S(1)} %bitcast.16), channel_id=1, source_target_pairs={{0,2},{1,0},{2,4},{3,1},{4,6},{5,3},{6,8},{7,5},{8,10},{9,7},{10,1... | collective-permute-start | bytes 73736 | tf_op jit(solution)/shard_map/ppermute | solution.py:384
  5.3 3.8 %collective-permute-start.2 = (bf16[96,128]{1,0:T(8,128)(2,1)S(1)}, bf16[96,128]{1,0:T(8,128)(2,1)S(1)}, u32[]{:S(2)}, u32[]{:S(2)}) collective-permute-start(bf16[96,128]{1,0:T(8,128)(2,1)S(1)} %bitcast.17), channel_id=1, source_target_pairs={{0,4},{1,0},{2,6},{3,2},{4,8},{5,1},{6,10},{7,3},{8,12},{9,5},{10,... | collective-permute-start | bytes 73736 | tf_op jit(solution)/shard_map/ppermute | solution.py:384
  6.9 9.0 %collective-permute-start.4 = (bf16[768,128]{1,0:T(8,128)(2,1)S(1)}, bf16[768,128]{1,0:T(8,128)(2,1)S(1)}, u32[]{:S(2)}, u32[]{:S(2)}) collective-permute-start(bf16[768,128]{1,0:T(8,128)(2,1)S(1)} %bitcast.28), channel_id=1, source_target_pairs={{0,2},{2,0},{4,6},{6,4},{8,10},{10,8},{12,14},{14,12},{1,3},{3,1},... | collective-permute-start | bytes 589832 | tf_op jit(solution)/shard_map/ppermute | solution.py:382
  8.5 7.5 %collective-permute-start.5 = (bf16[768,128]{1,0:T(8,128)(2,1)S(1)}, bf16[768,128]{1,0:T(8,128)(2,1)S(1)}, u32[]{:S(2)}, u32[]{:S(2)}) collective-permute-start(bf16[768,128]{1,0:T(8,128)(2,1)S(1)} %bitcast.29), channel_id=1, source_target_pairs={{2,4},{4,2},{6,8},{8,6},{10,12},{12,10},{0,0},{14,14},{3,5},{5,3},... | collective-permute-start | bytes 589832 | tf_op jit(solution)/shard_map/ppermute | solution.py:382
  9.2 1.3 %collective-permute-start.3 = (bf16[192,128]{1,0:T(8,128)(2,1)S(1)}, bf16[192,128]{1,0:T(8,128)(2,1)S(1)}, u32[]{:S(2)}, u32[]{:S(2)}) collective-permute-start(bf16[192,128]{1,0:T(8,128)(2,1)S(1)} %constant_dynamic-update-slice_fusion.near), channel_id=1, source_target_pairs={{0,1},{1,0},{2,3},{3,2},{4,5},{5,4},{6,7},{7,6},{8,9},{9,8},{10,11... | collective-permute-start | bytes 147464 | tf_op jit(solution)/shard_map/ppermute | solution.py:298
  16.9 1.4 %collective-permute-start.6 = (bf16[576,128]{1,0:T(8,128)(2,1)S(1)}, bf16[576,128]{1,0:T(8,128)(2,1)S(1)}, u32[]{:S(2)}, u32[]{:S(2)}) collective-permute-start(bf16[576,128]{1,0:T(8,128)(2,1)S(1)} %get-tuple-element.52), channel_id=1, source_target_pairs={{0,1},{1,0},{2,3},{3,2},{4,5},{5,4},{6,7},{7,6},{8,9},{9,8},{10,11... | collective-permute-start | bytes 442376 | tf_op jit(solution)/shard_map/ppermute | solution.py:298
  17.0 4.3 %collective-permute-start.13 = (bf16[320,128]{1,0:T(8,128)(2,1)S(1)}, bf16[320,128]{1,0:T(8,128)(2,1)S(1)}, u32[]{:S(2)}, u32[]{:S(2)}) collective-permute-start(bf16[320,128]{1,0:T(8,128)(2,1)S(1)} %get-tuple-element.61), channel_id=1, source_target_pairs={{0,1},{1,0},{2,3},{3,2},{4,5},{5,4},{6,7},{7,6},{8,9},{9,8},{10,11... | collective-permute-start | bytes 245768 | tf_op jit(solution)/shard_map/ppermute | solution.py:298
  18.4 5.2 %collective-permute-start.8 = (bf16[288,128]{1,0:T(8,128)(2,1)S(1)}, bf16[288,128]{1,0:T(8,128)(2,1)S(1)}, u32[]{:S(2)}, u32[]{:S(2)}) collective-permute-start(bf16[288,128]{1,0:T(8,128)(2,1)S(1)} %fusion.1), channel_id=1, source_target_pairs={{0,2},{1,9},{2,0},{3,11},{4,6},{5,13},{6,4},{7,15},{8,10},{9,1},{1... | collective-permute-start | bytes 221192 | tf_op jit(solution)/shard_map/ppermute | solution.py:324
  21.3 4.5 %collective-permute-start.14 = (bf16[320,128]{1,0:T(8,128)(2,1)S(1)}, bf16[320,128]{1,0:T(8,128)(2,1)S(1)}, u32[]{:S(2)}, u32[]{:S(2)}) collective-permute-start(bf16[320,128]{1,0:T(8,128)(2,1)S(1)} %add_convert_fusion.3), channel_id=1, source_target_pairs={{0,2},{1,9},{2,0},{3,11},{4,6},{5,13},{6,4},{7,15},{8,10},{9,1},{1... | collective-permute-start | bytes 245768 | tf_op jit(solution)/shard_map/ppermute | solution.py:327
  23.6 4.4 %collective-permute-start.9 = (bf16[288,128]{1,0:T(8,128)(2,1)S(1)}, bf16[288,128]{1,0:T(8,128)(2,1)S(1)}, u32[]{:S(2)}, u32[]{:S(2)}) collective-permute-start(bf16[288,128]{1,0:T(8,128)(2,1)S(1)} %fusion), channel_id=1, source_target_pairs={{0,4},{1,3},{2,6},{3,1},{4,0},{5,7},{6,2},{7,5},{8,12},{9,11},{10,... | collective-permute-start | bytes 221192 | tf_op jit(solution)/shard_map/ppermute | solution.py:327
  25.8 5.1 %collective-permute-start.15 = (bf16[320,128]{1,0:T(8,128)(2,1)S(1)}, bf16[320,128]{1,0:T(8,128)(2,1)S(1)}, u32[]{:S(2)}, u32[]{:S(2)}) collective-permute-start(bf16[320,128]{1,0:T(8,128)(2,1)S(1)} %add_convert_fusion.2), channel_id=1, source_target_pairs={{0,4},{1,3},{2,6},{3,1},{4,0},{5,7},{6,2},{7,5},{8,12},{9,11},{10,... | collective-permute-start | bytes 245768 | tf_op jit(solution)/shard_map/ppermute | solution.py:327
  28.1 5.3 %collective-permute-start.10 = (bf16[288,128]{1,0:T(8,128)(2,1)S(1)}, bf16[288,128]{1,0:T(8,128)(2,1)S(1)}, u32[]{:S(2)}, u32[]{:S(2)}) collective-permute-start(bf16[288,128]{1,0:T(8,128)(2,1)S(1)} %add_convert_fusion.5), channel_id=1, source_target_pairs={{0,8},{1,5},{2,10},{3,7},{4,12},{5,1},{6,14},{7,3},{8,0},{9,13},{1... | collective-permute-start | bytes 221192 | tf_op jit(solution)/shard_map/ppermute | solution.py:327
  30.9 5.4 %collective-permute-start.16 = (bf16[320,128]{1,0:T(8,128)(2,1)S(1)}, bf16[320,128]{1,0:T(8,128)(2,1)S(1)}, u32[]{:S(2)}, u32[]{:S(2)}) collective-permute-start(bf16[320,128]{1,0:T(8,128)(2,1)S(1)} %add_convert_fusion.1), channel_id=1, source_target_pairs={{0,8},{1,5},{2,10},{3,7},{4,12},{5,1},{6,14},{7,3},{8,0},{9,13},{1... | collective-permute-start | bytes 245768 | tf_op jit(solution)/shard_map/ppermute | solution.py:327
  32.9 6.0 %collective-permute-start.7 = (f32[4,12,128]{2,1,0:T(8,128)S(1)}, f32[4,12,128]{2,1,0:T(8,128)S(1)}, u32[]{:S(2)}, u32[]{:S(2)}) collective-permute-start(f32[4,12,128]{2,1,0:T(8,128)S(1)} %get-tuple-element.58), channel_id=1, source_target_pairs={{0,1},{1,0},{2,3},{3,2},{4,5},{5,4},{6,7},{7,6},{8,9},{9,8},{10,11... | collective-permute-start | bytes 73736 | tf_op jit(solution)/shard_map/ppermute | solution.py:298
  33.4 4.6 %collective-permute-start.11 = (bf16[288,128]{1,0:T(8,128)(2,1)S(1)}, bf16[288,128]{1,0:T(8,128)(2,1)S(1)}, u32[]{:S(2)}, u32[]{:S(2)}) collective-permute-start(bf16[288,128]{1,0:T(8,128)(2,1)S(1)} %add_convert_fusion.4), channel_id=1, source_target_pairs={{0,2},{1,9},{2,0},{3,11},{4,6},{5,13},{6,4},{7,15},{8,10},{9,1},{1... | collective-permute-start | bytes 221192 | tf_op jit(solution)/shard_map/ppermute | solution.py:330
  36.4 3.1 %collective-permute-start.17 = (bf16[320,128]{1,0:T(8,128)(2,1)S(1)}, bf16[320,128]{1,0:T(8,128)(2,1)S(1)}, u32[]{:S(2)}, u32[]{:S(2)}) collective-permute-start(bf16[320,128]{1,0:T(8,128)(2,1)S(1)} %add_convert_fusion.time_half), channel_id=1, source_target_pairs={{0,1},{1,0},{2,3},{3,2},{4,5},{5,4},{6,7},{7,6},{8,9},{9,8},{10,11... | collective-permute-start | bytes 245768 | tf_op jit(solution)/shard_map/ppermute | solution.py:298
  38.0 1.8 %collective-permute-start.12 = (bf16[576,128]{1,0:T(8,128)(2,1)S(1)}, bf16[576,128]{1,0:T(8,128)(2,1)S(1)}, u32[]{:S(2)}, u32[]{:S(2)}) collective-permute-start(bf16[576,128]{1,0:T(8,128)(2,1)S(1)} %maximum_select_fusion.space_half), channel_id=1, source_target_pairs={{0,1},{1,0},{2,3},{3,2},{4,5},{5,4},{6,7},{7,6},{8,9},{9,8},{10,11... | collective-permute-start | bytes 442376 | tf_op jit(solution)/shard_map/ppermute | solution.py:298
